TPU v7x, 32 devices: a whole 2x2x4 slice. The times are simulated.
32 devices in a mesh: dp: 8 (over y, x, core), seq: 4 (over z).
Axes of the slice: x: 2, y: 2, z: 4, core: 2. Of those that a mesh axis runs over, the one named last changes fastest.
Arguments:
- tokens: bfloat16 [8, 1024, 1536], P('dp', 'seq'), may hold values from -6 to 6
- cotangent: bfloat16 [8, 1024, 1536], P('dp', 'seq'), may hold values from -6 to 6
- w_query: bfloat16 [1, 1536, 1536], P(None, 'dp'), may hold values from -1 to 1
- w_key: bfloat16 [1, 1536, 768], P(None, 'dp'), may hold values from -1 to 1
- w_value: bfloat16 [1, 1536, 768], P(None, 'dp'), may hold values from -0.15625 to 0.15625
- w_out: bfloat16 [1, 1536, 1536], P(None, 'dp'), may hold values from -1.25 to 1.25
- w_gate: bfloat16 [1, 1536, 4096], P(None, 'dp'), may hold values from -0.15625 to 0.15625
- w_up: bfloat16 [1, 1536, 4096], P(None, 'dp'), may hold values from -0.15625 to 0.15625
- w_down: bfloat16 [1, 4096, 1536], P(None, 'dp'), may hold values from -0.09375 to 0.09375
- gain_attn: bfloat16 [1, 1536], P(None, 'dp'), may hold values from 0.5 to 1.5
- gain_mlp: bfloat16 [1, 1536], P(None, 'dp'), may hold values from 0.5 to 1.5
Outputs:
- activations: float32 [8, 1024, 1536], P('dp', 'seq')
- input_grad: float32 [8, 1024, 1536], P('dp', 'seq')
- grad_w_query: float32 [1, 1536, 1536], P(None, 'dp')
- grad_w_key: float32 [1, 1536, 768], P(None, 'dp')
- grad_w_value: float32 [1, 1536, 768], P(None, 'dp')
- grad_w_out: float32 [1, 1536, 1536], P(None, 'dp')
- grad_w_gate: float32 [1, 1536, 4096], P(None, 'dp')
- grad_w_up: float32 [1, 1536, 4096], P(None, 'dp')
- grad_w_down: float32 [1, 4096, 1536], P(None, 'dp')
- grad_gain_attn: float32 [1, 1536], P(None, 'dp')
- grad_gain_mlp: float32 [1, 1536], P(None, 'dp')
All inputs are finite; a program needn't handle non-finite values.
Results may differ from a plain program's by a relative error of at most 0.02.
Values may be sent and summed in bfloat16 or wider, within the bound.
A program may use at most 256 MiB of HBM per device.

v0:
```python
import jax
import jax.numpy as jnp
from jax import lax
from jax.sharding import PartitionSpec as P

HEADS = 16
KV_HEADS = 8
HEAD_DIM = 96
LAYERS = 1


EPS = 1e-05
ROPE_BASE = 100000.0


def rope_tables(positions, half_dim):
    frequency = ROPE_BASE ** (-jnp.arange(half_dim).astype(jnp.float32) / half_dim)
    angles = positions[:, None] * frequency[None, :]
    return (jnp.cos(angles), jnp.sin(angles))


def rotate(field, cosine_table, sine_table):
    half_dim = field.shape[-1] // 2
    first_half = field[..., :half_dim]
    second = field[..., half_dim:]
    cosine_b = cosine_table[:, None, :]
    sine_b = sine_table[:, None, :]
    return jnp.concatenate(
        [first_half * cosine_b - second * sine_b, second * cosine_b + first_half * sine_b], axis=-1
    )


def norm_apply(values, gain):
    return values * lax.rsqrt(jnp.mean(values * values, axis=-1, keepdims=True) + EPS) * gain


def causal_mask(block_start, block_rows, full_span):
    key_pos = jnp.arange(full_span, dtype=jnp.int32)
    query_pos = block_start + jnp.arange(block_rows, dtype=jnp.int32)
    return key_pos[None, :] <= query_pos[:, None]


def attend(query_all, key_all, value_all):
    full_span = query_all.shape[1]
    block_rows = min(512, full_span)
    scale = HEAD_DIM ** (-0.5)
    starts = jnp.arange(full_span // block_rows, dtype=jnp.int32) * block_rows

    def one_sequence(triple):
        query_seq, key_seq, value_seq = triple

        def one_block(block_start):
            query_rows = lax.dynamic_slice_in_dim(query_seq, block_start, block_rows, 0)
            scores = (
                jnp.einsum(
                    "qgrd,kgd->grqk", query_rows, key_seq, preferred_element_type=jnp.float32
                )
                * scale
            )
            scores = jnp.where(causal_mask(block_start, block_rows, full_span), scores, -1e30)
            row_max = jnp.max(scores, axis=-1, keepdims=True)
            weights = jnp.exp(scores - row_max)
            row_total = jnp.sum(weights, axis=-1, keepdims=True)
            probs_low = (weights / row_total).astype(jnp.bfloat16)
            result = jnp.einsum(
                "grqk,kgd->qgrd", probs_low, value_seq, preferred_element_type=jnp.float32
            )
            return (
                result.astype(jnp.bfloat16).reshape(block_rows, -1),
                (row_max + jnp.log(row_total))[..., 0],
            )

        outputs, log_total = lax.map(one_block, starts)
        return (outputs.reshape(full_span, -1), log_total)

    return lax.map(one_sequence, (query_all, key_all, value_all))


def attend_back(query_all, key_all, value_all, log_total, grad_att):
    full_span = query_all.shape[1]
    block_rows = min(512, full_span)
    scale = HEAD_DIM ** (-0.5)
    starts = jnp.arange(full_span // block_rows, dtype=jnp.int32) * block_rows

    def one_sequence(inputs_seq):
        query_seq, key_seq, value_seq, total_seq, grad_seq = inputs_seq

        def one_block(carry, block_in):
            grad_key, grad_value = carry
            block_start, total_blk = block_in
            query_rows = lax.dynamic_slice_in_dim(query_seq, block_start, block_rows, 0)
            grad_rows = lax.dynamic_slice_in_dim(grad_seq, block_start, block_rows, 0)
            scores = (
                jnp.einsum(
                    "qgrd,kgd->grqk", query_rows, key_seq, preferred_element_type=jnp.float32
                )
                * scale
            )
            scores = jnp.where(causal_mask(block_start, block_rows, full_span), scores, -1e30)
            probs = jnp.exp(scores - total_blk[..., None])
            grad_probs = jnp.einsum(
                "qgrd,kgd->grqk", grad_rows, value_seq, preferred_element_type=jnp.float32
            )
            row_inner = jnp.sum(probs * grad_probs, axis=-1, keepdims=True)
            grad_scores = (probs * (grad_probs - row_inner)).astype(jnp.bfloat16)
            grad_value = grad_value + jnp.einsum(
                "grqk,qgrd->kgd",
                probs.astype(jnp.bfloat16),
                grad_rows,
                preferred_element_type=jnp.float32,
            )
            grad_query = (
                jnp.einsum(
                    "grqk,kgd->qgrd", grad_scores, key_seq, preferred_element_type=jnp.float32
                )
                * scale
            )
            grad_key = (
                grad_key
                + jnp.einsum(
                    "grqk,qgrd->kgd", grad_scores, query_rows, preferred_element_type=jnp.float32
                )
                * scale
            )
            return ((grad_key, grad_value), grad_query.astype(jnp.bfloat16).reshape(block_rows, -1))

        zero_acc = jnp.zeros(key_seq.shape, jnp.float32)
        (grad_key, grad_value), grad_query = lax.scan(
            one_block, (zero_acc, zero_acc), (starts, total_seq)
        )
        return (
            grad_query.reshape(full_span, -1),
            grad_key.astype(jnp.bfloat16).reshape(full_span, -1),
            grad_value.astype(jnp.bfloat16).reshape(full_span, -1),
        )

    return lax.map(one_sequence, (query_all, key_all, value_all, log_total, grad_att))


def reduce_terms(terms):
    shards_summed = (
        lax.psum_scatter(
            terms[0].astype(jnp.bfloat16), "dp", scatter_dimension=0, tiled=True
        ).astype(jnp.float32),
        lax.psum_scatter(
            terms[1].astype(jnp.bfloat16), "dp", scatter_dimension=0, tiled=True
        ).astype(jnp.float32),
        lax.psum_scatter(
            terms[2].astype(jnp.bfloat16), "dp", scatter_dimension=0, tiled=True
        ).astype(jnp.float32),
        lax.psum_scatter(
            terms[3].astype(jnp.bfloat16), "dp", scatter_dimension=0, tiled=True
        ).astype(jnp.float32),
        lax.psum_scatter(
            terms[4].astype(jnp.bfloat16), "dp", scatter_dimension=0, tiled=True
        ).astype(jnp.float32),
        lax.psum_scatter(
            terms[5].astype(jnp.bfloat16), "dp", scatter_dimension=0, tiled=True
        ).astype(jnp.float32),
        lax.psum_scatter(
            terms[6].astype(jnp.bfloat16), "dp", scatter_dimension=0, tiled=True
        ).astype(jnp.float32),
        lax.psum_scatter(
            terms[7].astype(jnp.bfloat16), "dp", scatter_dimension=0, tiled=True
        ).astype(jnp.float32),
        lax.psum_scatter(
            terms[8].astype(jnp.bfloat16), "dp", scatter_dimension=0, tiled=True
        ).astype(jnp.float32),
    )
    return (
        lax.psum(shards_summed[0].astype(jnp.bfloat16), "seq").astype(jnp.float32),
        lax.psum(shards_summed[1].astype(jnp.bfloat16), "seq").astype(jnp.float32),
        lax.psum(shards_summed[2].astype(jnp.bfloat16), "seq").astype(jnp.float32),
        lax.psum(shards_summed[3].astype(jnp.bfloat16), "seq").astype(jnp.float32),
        lax.psum(shards_summed[4].astype(jnp.bfloat16), "seq").astype(jnp.float32),
        lax.psum(shards_summed[5].astype(jnp.bfloat16), "seq").astype(jnp.float32),
        lax.psum(shards_summed[6].astype(jnp.bfloat16), "seq").astype(jnp.float32),
        lax.psum(shards_summed[7].astype(jnp.bfloat16), "seq").astype(jnp.float32),
        lax.psum(shards_summed[8].astype(jnp.bfloat16), "seq").astype(jnp.float32),
    )


def local(
    tokens, cotangent, w_query, w_key, w_value, w_out, w_gate, w_up, w_down, gain_attn, gain_mlp
):
    seq_count, tok_local, model_width = tokens.shape
    row_count = seq_count * tok_local
    groups = lax.axis_size("seq")
    full_span = tok_local * groups
    group = HEADS // KV_HEADS
    heads_here = HEADS // groups
    kv_here = KV_HEADS // groups
    positions = (lax.axis_index("seq") * tok_local + jnp.arange(tok_local, dtype=jnp.int32)).astype(
        jnp.float32
    )
    cosine_table, sine_table = rope_tables(positions, HEAD_DIM // 2)

    def backward_layer(gradient, weights, saved):
        w_q, w_k, w_v, w_o, w_g, w_u, w_d, gain_one, gain_two = weights
        (
            flat_rows,
            normed_one,
            query_all,
            key_all,
            value_all,
            log_total,
            mixed,
            middle,
            normed_two,
            gate_proj,
            up_proj,
            hidden,
        ) = saved
        gradient = gradient.reshape(row_count, model_width)
        grad_low = gradient.astype(jnp.bfloat16)
        term_down = jnp.einsum("nf,nd->fd", hidden, grad_low, preferred_element_type=jnp.float32)
        grad_hidden = jnp.einsum("nd,fd->nf", grad_low, w_d, preferred_element_type=jnp.float32)
        _, pullback = jax.vjp(
            lambda gate_in, up_in: gate_in * jax.nn.sigmoid(gate_in) * up_in, gate_proj, up_proj
        )
        grad_gate, grad_up = pullback(grad_hidden)
        grad_gate = grad_gate.astype(jnp.bfloat16)
        grad_up = grad_up.astype(jnp.bfloat16)
        term_gate = jnp.einsum(
            "nd,nf->df", normed_two, grad_gate, preferred_element_type=jnp.float32
        )
        term_up = jnp.einsum("nd,nf->df", normed_two, grad_up, preferred_element_type=jnp.float32)
        grad_norm_two = jnp.einsum(
            "nf,df->nd", grad_gate, w_g, preferred_element_type=jnp.float32
        ) + jnp.einsum("nf,df->nd", grad_up, w_u, preferred_element_type=jnp.float32)
        _, pullback = jax.vjp(norm_apply, middle, gain_two.astype(jnp.float32))
        grad_middle, term_gain_two = pullback(grad_norm_two)
        grad_middle = grad_middle + gradient
        middle_low = grad_middle.astype(jnp.bfloat16)
        term_out = jnp.einsum("nk,nd->kd", mixed, middle_low, preferred_element_type=jnp.float32)
        grad_mixed = jnp.einsum(
            "nd,kd->nk", middle_low, w_o, preferred_element_type=jnp.float32
        ).astype(jnp.bfloat16)
        outgoing = grad_mixed.reshape(seq_count, tok_local, groups, heads_here * HEAD_DIM)
        grad_att = lax.all_to_all(outgoing, "seq", split_axis=2, concat_axis=1, tiled=True).reshape(
            seq_count, full_span, kv_here, group, HEAD_DIM
        )
        grad_query, grad_key, grad_value = attend_back(
            query_all, key_all, value_all, log_total, grad_att
        )
        returned = (
            lax.all_to_all(
                grad_query.reshape(seq_count, groups, tok_local, -1),
                "seq",
                split_axis=1,
                concat_axis=3,
                tiled=True,
            ),
            lax.all_to_all(
                grad_key.reshape(seq_count, groups, tok_local, -1),
                "seq",
                split_axis=1,
                concat_axis=3,
                tiled=True,
            ),
            lax.all_to_all(
                grad_value.reshape(seq_count, groups, tok_local, -1),
                "seq",
                split_axis=1,
                concat_axis=3,
                tiled=True,
            ),
        )
        query_back = returned[0].reshape(seq_count, tok_local, HEADS, HEAD_DIM).astype(jnp.float32)
        key_back = returned[1].reshape(seq_count, tok_local, KV_HEADS, HEAD_DIM).astype(jnp.float32)
        query_grad = (
            rotate(query_back, cosine_table, -sine_table)
            .astype(jnp.bfloat16)
            .reshape(row_count, model_width)
        )
        key_grad = (
            rotate(key_back, cosine_table, -sine_table)
            .astype(jnp.bfloat16)
            .reshape(row_count, KV_HEADS * HEAD_DIM)
        )
        value_grad = returned[2].reshape(row_count, KV_HEADS * HEAD_DIM)
        term_query = jnp.einsum(
            "nd,nk->dk", normed_one, query_grad, preferred_element_type=jnp.float32
        )
        term_key = jnp.einsum("nd,nk->dk", normed_one, key_grad, preferred_element_type=jnp.float32)
        term_value = jnp.einsum(
            "nd,nk->dk", normed_one, value_grad, preferred_element_type=jnp.float32
        )
        grad_norm_one = (
            jnp.einsum("nk,dk->nd", query_grad, w_q, preferred_element_type=jnp.float32)
            + jnp.einsum("nk,dk->nd", key_grad, w_k, preferred_element_type=jnp.float32)
            + jnp.einsum("nk,dk->nd", value_grad, w_v, preferred_element_type=jnp.float32)
        )
        _, pullback = jax.vjp(norm_apply, flat_rows, gain_one.astype(jnp.float32))
        grad_input, term_gain_one = pullback(grad_norm_one)
        grad_input = grad_input + grad_middle
        grad_terms = (
            term_query,
            term_key,
            term_value,
            term_out,
            term_gate,
            term_up,
            term_down,
            term_gain_one,
            term_gain_two,
        )
        return (grad_input.reshape(seq_count, tok_local, model_width), grad_terms)

    state = tokens.astype(jnp.float32)
    fetched = []
    layer_index = 0
    weights = (
        lax.all_gather(w_query[layer_index], "dp", axis=0, tiled=True),
        lax.all_gather(w_key[layer_index], "dp", axis=0, tiled=True),
        lax.all_gather(w_value[layer_index], "dp", axis=0, tiled=True),
        lax.all_gather(w_out[layer_index], "dp", axis=0, tiled=True),
        lax.all_gather(w_gate[layer_index], "dp", axis=0, tiled=True),
        lax.all_gather(w_up[layer_index], "dp", axis=0, tiled=True),
        lax.all_gather(w_down[layer_index], "dp", axis=0, tiled=True),
        lax.all_gather(gain_attn[layer_index], "dp", axis=0, tiled=True),
        lax.all_gather(gain_mlp[layer_index], "dp", axis=0, tiled=True),
    )
    w_q, w_k, w_v, w_o, w_g, w_u, w_d, gain_one, gain_two = weights
    flat_rows = state.reshape(row_count, model_width)
    normed_one = norm_apply(flat_rows, gain_one.astype(jnp.float32)).astype(jnp.bfloat16)
    query_pre = jnp.dot(normed_one, w_q, preferred_element_type=jnp.float32).reshape(
        seq_count, tok_local, HEADS, HEAD_DIM
    )
    key_pre = jnp.dot(normed_one, w_k, preferred_element_type=jnp.float32).reshape(
        seq_count, tok_local, KV_HEADS, HEAD_DIM
    )
    value_low = jnp.dot(normed_one, w_v, preferred_element_type=jnp.float32).astype(jnp.bfloat16)
    query_out = (
        rotate(query_pre, cosine_table, sine_table)
        .astype(jnp.bfloat16)
        .reshape(seq_count, tok_local, groups, heads_here * HEAD_DIM)
    )
    key_out = (
        rotate(key_pre, cosine_table, sine_table)
        .astype(jnp.bfloat16)
        .reshape(seq_count, tok_local, groups, kv_here * HEAD_DIM)
    )
    value_out = value_low.reshape(seq_count, tok_local, groups, kv_here * HEAD_DIM)
    query_all = lax.all_to_all(query_out, "seq", split_axis=2, concat_axis=1, tiled=True)
    key_all = lax.all_to_all(key_out, "seq", split_axis=2, concat_axis=1, tiled=True)
    value_all = lax.all_to_all(value_out, "seq", split_axis=2, concat_axis=1, tiled=True)
    query_all = query_all.reshape(seq_count, full_span, kv_here, group, HEAD_DIM)
    key_all = key_all.reshape(seq_count, full_span, kv_here, HEAD_DIM)
    value_all = value_all.reshape(seq_count, full_span, kv_here, HEAD_DIM)
    attended, log_total = attend(query_all, key_all, value_all)
    returned = lax.all_to_all(
        attended.reshape(seq_count, groups, tok_local, heads_here * HEAD_DIM),
        "seq",
        split_axis=1,
        concat_axis=3,
        tiled=True,
    )
    mixed = returned.reshape(row_count, model_width)
    middle = flat_rows + jnp.dot(mixed, w_o, preferred_element_type=jnp.float32)
    normed_two = norm_apply(middle, gain_two.astype(jnp.float32)).astype(jnp.bfloat16)
    gate_proj = jnp.dot(normed_two, w_g, preferred_element_type=jnp.float32)
    up_proj = jnp.dot(normed_two, w_u, preferred_element_type=jnp.float32)
    hidden = (gate_proj * jax.nn.sigmoid(gate_proj) * up_proj).astype(jnp.bfloat16)
    result = middle + jnp.dot(hidden, w_d, preferred_element_type=jnp.float32)
    saved = (
        flat_rows,
        normed_one,
        query_all,
        key_all,
        value_all,
        log_total,
        mixed,
        middle,
        normed_two,
        gate_proj,
        up_proj,
        hidden,
    )
    state, saved = (result.reshape(seq_count, tok_local, model_width), saved)
    saved_all = [saved]
    fetched.append(weights)
    gradient = cotangent.astype(jnp.float32)
    summed = [None] * LAYERS
    for layer_index in reversed(range(LAYERS)):
        weights = (
            lax.all_gather(w_query[layer_index], "dp", axis=0, tiled=True),
            lax.all_gather(w_key[layer_index], "dp", axis=0, tiled=True),
            lax.all_gather(w_value[layer_index], "dp", axis=0, tiled=True),
            lax.all_gather(w_out[layer_index], "dp", axis=0, tiled=True),
            lax.all_gather(w_gate[layer_index], "dp", axis=0, tiled=True),
            lax.all_gather(w_up[layer_index], "dp", axis=0, tiled=True),
            lax.all_gather(w_down[layer_index], "dp", axis=0, tiled=True),
            lax.all_gather(gain_attn[layer_index], "dp", axis=0, tiled=True),
            lax.all_gather(gain_mlp[layer_index], "dp", axis=0, tiled=True),
        )
        gradient, grad_terms = backward_layer(gradient, weights, saved_all[layer_index])
        summed[layer_index] = reduce_terms(grad_terms)
    stacked = [jnp.stack([summed[0][member]]) for member in range(9)]
    return (
        state,
        gradient,
        stacked[0],
        stacked[1],
        stacked[2],
        stacked[3],
        stacked[4],
        stacked[5],
        stacked[6],
        stacked[7],
        stacked[8],
    )


def solution(mesh):
    in_specs = (
        P("dp", "seq", None),
        P("dp", "seq", None),
        P(None, "dp", None),
        P(None, "dp", None),
        P(None, "dp", None),
        P(None, "dp", None),
        P(None, "dp", None),
        P(None, "dp", None),
        P(None, "dp", None),
        P(None, "dp"),
        P(None, "dp"),
    )
    out_specs = (
        P("dp", "seq", None),
        P("dp", "seq", None),
        P(None, "dp", None),
        P(None, "dp", None),
        P(None, "dp", None),
        P(None, "dp", None),
        P(None, "dp", None),
        P(None, "dp", None),
        P(None, "dp", None),
        P(None, "dp"),
        P(None, "dp"),
    )
    return jax.shard_map(local, mesh=mesh, in_specs=in_specs, out_specs=out_specs, check_vma=False)
```

profile of v0, /device:TPU:0, one launch (start us, length us, event | category | flops | bytes accessed | tf_op | source)
XLA Modules:
  0.0 1257.8 jit_solution(14075761006075737872)
XLA Ops:
  13.8 15.5 %all-reduce.5 = (bf16[1536]{0:T(1024)(128)(2,1)S(1)}, bf16[1536]{0:T(1024)(128)(2,1)S(1)}) all-reduce(bf16[1536]{0:T(1024)(128)(2,1)S(1)} %dynamic-update-slice, bf16[1536]{0:T(1024)(128)(2,1)S(1)} %dynamic-update-slice.1), channel_id=2, replica_groups=mesh['dp'=8,'seq'=4] {'dp'}, use_global_device_ids=true, to_apply=%add | all-reduce | flops 3072 | bytes 12288
  31.0 10.7 all-gather.19.cloned.1.call-done
  51.0 21.6 %all-gather.21.cloned.1.call-done = bf16[1,1536,768]{2,1,0:T(8,128)(2,1)} async-done(((bf16[1,192,768]{2,1,0:T(8,128)(2,1)}), bf16[1,1536,768]{2,1,0:T(8,128)(2,1)}) %all-gather.21.cloned.1.call-update) | async-done | bytes 2359312 | tf_op jit(solution)/shard_map/all_gather | solution.py:316
  76.0 37.3 %all-gather.17.cloned.1.call-done = bf16[1,1536,1536]{2,1,0:T(8,128)(2,1)} async-done(((bf16[1,192,1536]{2,1,0:T(8,128)(2,1)}), bf16[1,1536,1536]{2,1,0:T(8,128)(2,1)}) %all-gather.17.cloned.1.call-update) | async-done | bytes 4718608 | tf_op jit(solution)/shard_map/all_gather | solution.py:314
  141.5 18.5 %all-to-all-done = bf16[1,256,4,384]{1,3,0,2:T(8,128)(2,1)S(1)} async-done(((bf16[1,256,4,384]{1,3,0,2:T(8,128)(2,1)}), bf16[1,256,4,384]{1,3,0,2:T(8,128)(2,1)S(1)}, u32[]{:S(2)}, u32[]{:S(2)}) %all-to-all-start) | async-done | bytes 786464 | tf_op jit(solution)/shard_map/all_to_all | solution.py:345
  162.2 24.2 %while.47 = (s32[]{:T(128)}, bf16[2,512,384]{2,1,0:T(8,128)(2,1)}, f32[2,2,2,512]{3,2,1,0:T(2,128)S(1)}, s32[2]{0:T(128)S(1)}, bf16[1024,2,2,96]{0,3,2,1:T(8,128...) while((s32[]{:T(128)}, bf16[2,512,384]{2,1,0:T(8,128)(2,1)}, ...), condition=%wide.region_4.5_spmd, body=%wide.region_1.4_spmd.sunk | while | flops 831191552 | bytes 30479008 | solution.py:73
  191.0 19.7 %all-to-all-done.3 = bf16[1,4,256,384]{3,2,0,1:T(8,128)(2,1)} async-done(((bf16[1,4,256,384]{3,2,0,1:T(8,128)(2,1)}), bf16[1,4,256,384]{3,2,0,1:T(8,128)(2,1)}, u32[]{:S(2)}, u32[]{:S(2)}) %all-to-all-start.3) | async-done | bytes 786464 | tf_op jit(solution)/shard_map/all_to_all | solution.py:352
  217.7 9.9 all-gather.27.cloned.1.call-done
  227.6 9.5 fusion.50
  237.1 64.3 %all-gather.29.cloned.1.call-done = bf16[1,4096,1536]{2,1,0:T(8,128)(2,1)} async-done(((bf16[1,512,1536]{2,1,0:T(8,128)(2,1)}), bf16[1,4096,1536]{2,1,0:T(8,128)(2,1)}) %all-gather.29.cloned.1.call-update) | async-done | bytes 12582928 | tf_op jit(solution)/shard_map/all_gather | solution.py:320
  301.3 14.1 %fusion.44 = f32[256,4096]{1,0:T(8,128)} fusion(bf16[1,4096,1536]{2,1,0:T(8,128)(2,1)} %all-gather.29.cloned.1.call-done, bf16[1,256,1536]{2,1,0:T(8,128)(2,1)S(1)} %copy-done.22), kind=kOutput, calls=%fused_computation.59 | convolution fusion | flops 3221225472 | bytes 17563648 | tf_op jit(solution)/shard_map/nd,fd->nf/dot_general | solution.py:217
  315.5 59.8 %all-gather.25.cloned.1.call-done = bf16[1,1536,4096]{2,1,0:T(8,128)(2,1)} async-done(((bf16[1,192,4096]{2,1,0:T(8,128)(2,1)}), bf16[1,1536,4096]{2,1,0:T(8,128)(2,1)}) %all-gather.25.cloned.1.call-update) | async-done | bytes 12582928 | tf_op jit(solution)/shard_map/all_gather | solution.py:318
  375.3 13.4 %fusion.64 = (bf16[256,4096]{1,0:T(8,128)(2,1)}, bf16[256,4096]{1,0:T(8,128)(2,1)S(1)}, bf16[256,4096]{1,0:T(8,128)(2,1)}) fusion(f32[256,4096]{1,0:T(8,128)} %fusion.44, f32[256,4096]{1,0:T(8,128)} %fusion.50, bf16[256,1536]{1,0:T(8,128)(2,1)S(1)} %multiply_convert_fusion.2, bf16[1,1536,4096]{2,1,0:T(8,128)(2,1)} %all-gather.25.cloned.1.call-done), kind=kOutput, calls=%fused_computation.82 | convolution fusion | flops 3238002688 | bytes 28049408 | tf_op jit(solution)/shard_map/dot_general | solution.py:362
  388.7 19.9 %fusion.48 = f32[256,1536]{1,0:T(8,128)} fusion(bf16[256,4096]{1,0:T(8,128)(2,1)S(1)} %get-tuple-element.258, bf16[1,1536,4096]{2,1,0:T(8,128)(2,1)} %all-gather.27.cloned.1.call-done), kind=kOutput, calls=%fused_computation.63 | convolution fusion | flops 3221225472 | bytes 16252928 | tf_op jit(solution)/shard_map/nf,df->nd/dot_general | solution.py:230
  408.7 10.6 multiply_reduce_fusion
  429.5 20.5 %all-to-all-done.4 = bf16[1,256,4,384]{3,1,0,2:T(8,128)(2,1)S(1)} async-done(((bf16[1,256,4,384]{3,1,0,2:T(8,128)(2,1)}), bf16[1,256,4,384]{3,1,0,2:T(8,128)(2,1)S(1)}, u32[]{:S(2)}, u32[]{:S(2)}) %all-to-all-start.4) | async-done | bytes 786464 | tf_op jit(solution)/shard_map/all_to_all | solution.py:240
  454.8 46.8 %while.48 = (s32[]{:T(128)}, f32[1024,2,96]{0,2,1:T(8,128)S(1)}, f32[1024,2,96]{0,2,1:T(8,128)}, bf16[2,512,384]{2,1,0:T(8,128)(2,1)}, s32[2]{0:T(128)S(1)}, /*i...) while((s32[]{:T(128)}, f32[1024,2,96]{0,2,1:T(8,128)S(1)}, ...), condition=%wide.region_9.10_spmd.clone, body=%wide.region_7.9_spmd.clone.sunk | while | flops 2046622208 | bytes 132707192 | solution.py:128
  502.0 14.0 %all_to_all.108 = bf16[1,4,256,192]{2,3,0,1:T(8,128)(2,1)S(1)} all-to-all(bf16[1,4,256,192]{2,3,0,1:T(8,128)(2,1)S(1)} %copy.86), channel_id=1, replica_groups=mesh['dp'=8,'seq'=4] {'seq'}, dimensions={1} | all-to-all | bytes 786432 | tf_op jit(solution)/shard_map/all_to_all | solution.py:254
  520.2 13.7 %all_to_all.109 = bf16[1,4,256,192]{2,3,0,1:T(8,128)(2,1)S(1)} all-to-all(bf16[1,4,256,192]{2,3,0,1:T(8,128)(2,1)S(1)} %copy.87), channel_id=1, replica_groups=mesh['dp'=8,'seq'=4] {'seq'}, dimensions={1} | all-to-all | bytes 786432 | tf_op jit(solution)/shard_map/all_to_all | solution.py:261
  541.8 22.3 %all_to_all.110 = bf16[1,4,256,384]{3,2,0,1:T(8,128)(2,1)S(1)} all-to-all(bf16[1,4,256,384]{3,2,0,1:T(8,128)(2,1)S(1)} %bitcast.368), channel_id=1, replica_groups=mesh['dp'=8,'seq'=4] {'seq'}, dimensions={1} | all-to-all | bytes 1572864 | tf_op jit(solution)/shard_map/all_to_all | solution.py:247
  573.2 8.1 convolution_convert_fusion.2
  581.4 8.1 convolution_convert_fusion.1
  591.1 7.5 convolution_convert_fusion
  605.5 57.1 %reduce-scatter.14.cloned.1.call-done = bf16[192,1536]{1,0:T(8,128)(2,1)} async-done(((bf16[1536,1536]{1,0:T(8,128)(2,1)}), bf16[192,1536]{1,0:T(8,128)(2,1)}) %reduce-scatter.14.cloned.1.call-update) | async-done | bytes 589840 | tf_op jit(solution)/shard_map/reduce_scatter | solution.py:151
  662.6 57.3 %reduce-scatter.8.cloned.1.call-done = bf16[192,1536]{1,0:T(8,128)(2,1)} async-done(((bf16[1536,1536]{1,0:T(8,128)(2,1)}), bf16[192,1536]{1,0:T(8,128)(2,1)}) %reduce-scatter.8.cloned.1.call-update) | async-done | bytes 589840 | tf_op jit(solution)/shard_map/reduce_scatter | solution.py:142
  719.9 95.7 %reduce-scatter.16.cloned.1.call-done = bf16[192,4096]{1,0:T(8,128)(2,1)} async-done(((bf16[1536,4096]{1,0:T(8,128)(2,1)}), bf16[192,4096]{1,0:T(8,128)(2,1)}) %reduce-scatter.16.cloned.1.call-update) | async-done | bytes 1572880 | tf_op jit(solution)/shard_map/reduce_scatter | solution.py:154
  815.6 95.8 %reduce-scatter.18.cloned.1.call-done = bf16[192,4096]{1,0:T(8,128)(2,1)} async-done(((bf16[1536,4096]{1,0:T(8,128)(2,1)}), bf16[192,4096]{1,0:T(8,128)(2,1)}) %reduce-scatter.18.cloned.1.call-update) | async-done | bytes 1572880 | tf_op jit(solution)/shard_map/reduce_scatter | solution.py:157
  911.4 95.7 %reduce-scatter.20.cloned.1.call-done = bf16[512,1536]{1,0:T(8,128)(2,1)} async-done(((bf16[4096,1536]{1,0:T(8,128)(2,1)}), bf16[512,1536]{1,0:T(8,128)(2,1)}) %reduce-scatter.20.cloned.1.call-update) | async-done | bytes 1572880 | tf_op jit(solution)/shard_map/reduce_scatter | solution.py:160
  1008.5 9.8 fusion.75
  1026.3 13.6 %all-reduce.4 = (bf16[1536]{0:T(1024)(128)(2,1)S(1)}, bf16[1536]{0:T(1024)(128)(2,1)S(1)}) all-reduce(bf16[1536]{0:T(1024)(128)(2,1)S(1)} %get-tuple-element.204, bf16[1536]{0:T(1024)(128)(2,1)S(1)} %copy-done.44), channel_id=18, replica_groups=mesh['dp'=8,'seq'=4] {'dp'}, use_global_device_ids=true, to_apply=%region_26.27.clone | all-reduce | flops 3072 | bytes 12288
  1040.2 12.3 all-reduce.6
  1056.6 182.9 %all-reduce.10.cloned.1.call-done = (bf16[1,192,1536]{2,1,0:T(8,128)(2,1)}, bf16[1,192,768]{2,1,0:T(8,128)(2,1)}, bf16[1,192,768]{2,1,0:T(8,128)(2,1)}, bf16[1,1...) async-done(((bf16[1,192,1536]{2,1,0:T(8,128)(2,1)}, bf16[1,192,768]{2,1,0:T(8,128)(2,1)}, ...) | async-done | bytes 6488080 | tf_op jit(solution)/shard_map/psum | solution.py:171
  (277 shorter events, 194.4 us)
Async XLA Ops:
  7.2 34.6 %all-gather.19.cloned.1.call-start = ((), (), s32[]{:S(2)}) async-start(), calls=%async_computation.23 | async-start | bytes 2654208 | tf_op jit(solution)/shard_map/all_gather | solution.py:315
  7.9 64.6 %all-gather.21.cloned.1.call-start = ((), (), s32[]{:S(2)}) async-start(), calls=%async_computation.24 | async-start | bytes 2654208 | tf_op jit(solution)/shard_map/all_gather | solution.py:316
  8.7 104.6 %all-gather.17.cloned.1.call-start = ((), (), s32[]{:S(2)}) async-start(), calls=%async_computation.22 | async-start | bytes 5308416 | tf_op jit(solution)/shard_map/all_gather | solution.py:314
  9.4 202.7 %all-gather.23.cloned.1.call-start = ((), (), s32[]{:S(2)}) async-start(), calls=%async_computation.25 | async-start | bytes 5308416 | tf_op jit(solution)/shard_map/all_gather | solution.py:317
  10.0 19.4 %copy-start.2 = (bf16[1,256,1536]{2,1,0:T(8,128)(2,1)S(1)}, bf16[1,256,1536]{2,1,0:T(8,128)(2,1)}, u32[]{:S(2)}) copy-start(bf16[1,256,1536]{2,1,0:T(8,128)(2,1)} %param.15) | copy-start | bytes 2359300
  10.0 217.5 %all-gather.27.cloned.1.call-start = ((), (), s32[]{:S(2)}) async-start(), calls=%async_computation.27 | async-start | bytes 14155776 | tf_op jit(solution)/shard_map/all_gather | solution.py:319
  10.6 290.7 %all-gather.29.cloned.1.call-start = ((), (), s32[]{:S(2)}) async-start(), calls=%async_computation.28 | async-start | bytes 14155776 | tf_op jit(solution)/shard_map/all_gather | solution.py:320
  11.2 364.1 %all-gather.25.cloned.1.call-start = ((), (), s32[]{:S(2)}) async-start(), calls=%async_computation.26 | async-start | bytes 14155776 | tf_op jit(solution)/shard_map/all_gather | solution.py:318
  29.3 95.2 %copy-start.35 = (f32[1536]{0:T(1024)}, f32[1536]{0:T(1024)S(1)}, u32[]{:S(2)}) copy-start(f32[1536]{0:T(1024)S(1)} %convert_element_type.298) | copy-start | bytes 18436
  30.1 94.4 %copy-start.40 = (f32[256]{0:T(256)}, f32[256]{0:T(256)S(1)}, u32[]{:S(2)}) copy-start(f32[256]{0:T(256)S(1)} %fusion.116) | copy-start | bytes 3076
  31.0 97.4 %copy-start.31 = (f32[256,48]{0,1:T(8,128)}, f32[256,48]{0,1:T(8,128)S(1)}, u32[]{:S(2)}) copy-start(f32[256,48]{0,1:T(8,128)S(1)} %get-tuple-element.270) | copy-start | bytes 147460
  46.4 73.5 %all-to-all-start.1 = ((bf16[1,256,4,192]{1,3,0,2:T(8,128)(2,1)}), bf16[1,256,4,192]{1,3,0,2:T(8,128)(2,1)S(1)}, u32[]{:S(2)}, u32[]{:S(2)}) async-start(bf16[1,256,4,192]{1,3,0,2:T(8,128)(2,1)} %bitcast.26), calls=%async_computation.1 | async-start | bytes 786432 | tf_op jit(solution)/shard_map/all_to_all | solution.py:346
  119.9 16.7 %all-to-all-start.2 = ((bf16[1,256,4,192]{1,3,0,2:T(8,128)(2,1)}), bf16[1,256,4,192]{1,3,0,2:T(8,128)(2,1)S(1)}, u32[]{:S(2)}, u32[]{:S(2)}) async-start(bf16[1,256,4,192]{1,3,0,2:T(8,128)(2,1)} %bitcast.31), calls=%async_computation.2 | async-start | bytes 786432 | tf_op jit(solution)/shard_map/all_to_all | solution.py:347
  136.6 23.4 %all-to-all-start = ((bf16[1,256,4,384]{1,3,0,2:T(8,128)(2,1)}), bf16[1,256,4,384]{1,3,0,2:T(8,128)(2,1)S(1)}, u32[]{:S(2)}, u32[]{:S(2)}) async-start(bf16[1,256,4,384]{1,3,0,2:T(8,128)(2,1)} %bitcast.18), calls=%async_computation | async-start | bytes 1572864 | tf_op jit(solution)/shard_map/all_to_all | solution.py:345
  186.4 24.3 %all-to-all-start.3 = ((bf16[1,4,256,384]{3,2,0,1:T(8,128)(2,1)}), bf16[1,4,256,384]{3,2,0,1:T(8,128)(2,1)}, u32[]{:S(2)}, u32[]{:S(2)}) async-start(bf16[1,4,256,384]{3,2,0,1:T(8,128)(2,1)} %bitcast.369), calls=%async_computation.3 | async-start | bytes 1572864 | tf_op jit(solution)/shard_map/all_to_all | solution.py:352
  217.7 157.6 %copy-start.17 = (bf16[256,1536]{1,0:T(8,128)(2,1)}, bf16[256,1536]{1,0:T(8,128)(2,1)S(1)}, u32[]{:S(2)}) copy-start(bf16[256,1536]{1,0:T(8,128)(2,1)S(1)} %multiply_convert_fusion.2) | copy-start | bytes 2359300
  217.7 83.7 %copy-start.22 = (bf16[1,256,1536]{2,1,0:T(8,128)(2,1)S(1)}, bf16[1,256,1536]{2,1,0:T(8,128)(2,1)}, u32[]{:S(2)}) copy-start(bf16[1,256,1536]{2,1,0:T(8,128)(2,1)} %param.16) | copy-start | bytes 2359300
  388.6 20.0 %copy-start.27 = (bf16[256,4096]{1,0:T(8,128)(2,1)}, bf16[256,4096]{1,0:T(8,128)(2,1)S(1)}, u32[]{:S(2)}) copy-start(bf16[256,4096]{1,0:T(8,128)(2,1)S(1)} %get-tuple-element.258) | copy-start | bytes 6291460
  388.6 20.0 %copy-start.7 = (f32[256,1536]{1,0:T(8,128)S(1)}, f32[256,1536]{1,0:T(8,128)}, u32[]{:S(2)}) copy-start(f32[256,1536]{1,0:T(8,128)} %copy-done.6) | copy-start | bytes 4718596
  388.6 20.0 %copy-start.28 = (bf16[256,4096]{1,0:T(8,128)(2,1)S(1)}, bf16[256,4096]{1,0:T(8,128)(2,1)}, u32[]{:S(2)}) copy-start(bf16[256,4096]{1,0:T(8,128)(2,1)} %get-tuple-element.257) | copy-start | bytes 6291460
  388.7 33.6 %slice-start = ((s8[4718592]{0:T(1024)(128)(4,1)}), s8[4194304]{0:T(1024)(128)(4,1)S(1)}, s32[]{:S(2)}) async-start(s8[4718592]{0:T(1024)(128)(4,1)} %bitcast.353), calls=%async_computation.30 | async-start | bytes 8388608
  424.9 25.1 %all-to-all-start.4 = ((bf16[1,256,4,384]{3,1,0,2:T(8,128)(2,1)}), bf16[1,256,4,384]{3,1,0,2:T(8,128)(2,1)S(1)}, u32[]{:S(2)}, u32[]{:S(2)}) async-start(bf16[1,256,4,384]{3,1,0,2:T(8,128)(2,1)} %copy.81), calls=%async_computation.4 | async-start | bytes 1572864 | tf_op jit(solution)/shard_map/all_to_all | solution.py:240
  429.5 169.6 %reduce-scatter.10.cloned.1.call-start = ((), (), s32[]{:S(2)}) async-start(), calls=%async_computation.16 | async-start | bytes 2654208 | tf_op jit(solution)/shard_map/reduce_scatter | solution.py:145
  518.6 87.0 %reduce-scatter.12.cloned.1.call-start = ((), (), s32[]{:S(2)}) async-start(), calls=%async_computation.17 | async-start | bytes 2654208 | tf_op jit(solution)/shard_map/reduce_scatter | solution.py:148
  537.0 125.6 %reduce-scatter.14.cloned.1.call-start = ((), (), s32[]{:S(2)}) async-start(), calls=%async_computation.18 | async-start | bytes 5308416 | tf_op jit(solution)/shard_map/reduce_scatter | solution.py:151
  540.7 179.2 %reduce-scatter.8.cloned.1.call-start = ((), (), s32[]{:S(2)}) async-start(), calls=%async_computation.15 | async-start | bytes 5308416 | tf_op jit(solution)/shard_map/reduce_scatter | solution.py:142
  572.1 243.5 %reduce-scatter.16.cloned.1.call-start = ((), (), s32[]{:S(2)}) async-start(), calls=%async_computation.19 | async-start | bytes 14155776 | tf_op jit(solution)/shard_map/reduce_scatter | solution.py:154
  581.4 330.1 %reduce-scatter.18.cloned.1.call-start = ((), (), s32[]{:S(2)}) async-start(), calls=%async_computation.20 | async-start | bytes 14155776 | tf_op jit(solution)/shard_map/reduce_scatter | solution.py:157
  589.5 417.6 %reduce-scatter.20.cloned.1.call-start = ((), (), s32[]{:S(2)}) async-start(), calls=%async_computation.21 | async-start | bytes 14155776 | tf_op jit(solution)/shard_map/reduce_scatter | solution.py:160
  598.6 640.9 %all-reduce.10.cloned.1.call-start = ((), (), s32[]{:S(2)}) async-start(), calls=%async_computation.29 | async-start | bytes 12976128 | tf_op jit(solution)/shard_map/psum | solution.py:171
  1024.1 29.5 %copy-start.43 = (f32[256]{0:T(256)S(1)}, f32[256]{0:T(256)}, u32[]{:S(2)}) copy-start(f32[256]{0:T(256)} %copy-done.42) | copy-start | bytes 3076
  1024.1 29.5 %copy-start.11 = (f32[256,1536]{1,0:T(8,128)S(1)}, f32[256,1536]{1,0:T(8,128)}, u32[]{:S(2)}) copy-start(f32[256,1536]{1,0:T(8,128)} %copy-done.9) | copy-start | bytes 4718596
  (44 other events, 195.5 us)
Sparse Core Ops, SparseCore 0:
  9.9 31.8 all-gather.18
  43.6 28.8 all-gather.20
  74.4 38.7 all-gather.16
  115.0 38.7 all-gather.22
  155.5 71.9 all-gather.26
  229.3 71.9 all-gather.28
  303.2 71.9 all-gather.24
  518.7 40.4 reduce-scatter.9
  563.2 42.3 reduce-scatter.11
  608.8 53.7 reduce-scatter.13
  666.1 53.7 reduce-scatter.7
  723.2 92.3 reduce-scatter.15
  819.1 92.3 reduce-scatter.17
  914.8 92.2 reduce-scatter.19
  1009.9 229.5 all-reduce.9
where the time goes:
time: 1260 us
  waiting for transfers between devices  865 us (69%)
  matrix products  174 us (14%)
  blocking collectives  91.5 us (7%)
  local copies, waits for them, and re-layouts  41.4 us (3%)
  other arithmetic  38.6 us (3%)
  starting transfers between devices  23.1 us (2%)
  between operations  16.1 us (1%)
    psum x1, waiting for transfers between devices, reduce_terms(): lax.psum(shards_summed[0].astype(jnp.bfloat16), 'seq').astype(jnp.float32)  183 us
    reduce_scatter x1, waiting for transfers between devices, reduce_terms(): lax.psum_scatter(terms[5].astype(jnp.bfloat16), 'dp', scatter_dimension=0...  95.8 us
    reduce_scatter x1, waiting for transfers between devices, reduce_terms(): lax.psum_scatter(terms[4].astype(jnp.bfloat16), 'dp', scatter_dimension=0...  95.7 us
    reduce_scatter x1, waiting for transfers between devices, reduce_terms(): lax.psum_scatter(terms[6].astype(jnp.bfloat16), 'dp', scatter_dimension=0...  95.7 us
    all_gather x1, waiting for transfers between devices, local(): lax.all_gather(w_down[layer_index], 'dp', axis=0, tiled=True)  64.3 us
    all_gather x1, waiting for transfers between devices, local(): lax.all_gather(w_gate[layer_index], 'dp', axis=0, tiled=True)  59.8 us
    reduce_scatter x1, waiting for transfers between devices, reduce_terms(): lax.psum_scatter(terms[0].astype(jnp.bfloat16), 'dp', scatter_dimension=0...  57.3 us
    reduce_scatter x1, waiting for transfers between devices, reduce_terms(): lax.psum_scatter(terms[3].astype(jnp.bfloat16), 'dp', scatter_dimension=0...  57.1 us
  transfers between devices with their start and end apart: 20, of which 17 were waited for; matrix products, arithmetic and copies ran while one was open for 11% of the time, Pallas kernels for 0%

commit v1 on v0

v1 whole, which is shorter than its diff:
```python
import functools

import jax
import jax.numpy as jnp
from jax import lax
from jax.experimental import pallas as pl
from jax.experimental.pallas import tpu as pltpu
from jax.sharding import PartitionSpec as P

HEADS = 16
KV_HEADS = 8
HEAD_DIM = 96
GROUP = HEADS // KV_HEADS
EPS = 1e-05
ROPE_BASE = 100000.0
BF = jnp.bfloat16
F32 = jnp.float32
NEG = -1e30
KV_STEP = 4
SCALE = HEAD_DIM ** (-0.5)


def dot(a, b, dims):
    return lax.dot_general(a, b, (dims, ((), ())), preferred_element_type=F32)


def nn(a, b):
    return dot(a, b, ((1,), (0,)))


def nt(a, b):
    return dot(a, b, ((1,), (1,)))


def tn(a, b):
    return dot(a, b, ((0,), (0,)))


def chunk_mask(tokens):
    row = lax.broadcasted_iota(jnp.int32, (tokens, tokens), 0)
    col = lax.broadcasted_iota(jnp.int32, (tokens, tokens), 1)
    mask = col <= row
    return jnp.concatenate([mask] * GROUP, axis=0)


def head_scores(place, q, keys, mask):
    scores = []
    for r, k in enumerate(keys):
        s = nt(q, k) * SCALE
        if r == 0:
            s = jnp.where(mask, s, NEG)
        else:
            s = jnp.where(place >= r, s, NEG)
        scores.append(s)
    return scores


def lanes(ref, head, width=HEAD_DIM):
    return ref[:, head * HEAD_DIM : head * HEAD_DIM + width]


def two_heads(ref, g):
    return jnp.concatenate([lanes(ref, GROUP * g + i) for i in range(GROUP)], axis=0)


def attend_body(chunks, place_ref, q_ref, *refs):
    k_refs, v_refs = refs[:chunks], refs[chunks : 2 * chunks]
    o_ref, lse_ref = refs[2 * chunks :]
    tokens = q_ref.shape[0]
    place = place_ref[0]
    mask = chunk_mask(tokens)
    lse_ref[...] = jnp.zeros_like(lse_ref)
    for g in range(KV_STEP):
        q = two_heads(q_ref, g)
        scores = head_scores(place, q, [lanes(k, g) for k in k_refs], mask)
        top = functools.reduce(
            jnp.maximum, [jnp.max(s, axis=1, keepdims=True) for s in scores]
        )
        weights = [jnp.exp(s - top) for s in scores]
        total = sum(jnp.sum(w, axis=1, keepdims=True) for w in weights)
        inverse = 1.0 / total
        out = sum(
            nn((w * inverse).astype(BF), lanes(v, g)) for w, v in zip(weights, v_refs)
        )
        lse = top + jnp.log(total)
        for i in range(GROUP):
            h = GROUP * g + i
            o_ref[:, h * HEAD_DIM : (h + 1) * HEAD_DIM] = out[
                i * tokens : (i + 1) * tokens
            ].astype(BF)
            lse_ref[0, :, h : h + 1] = lse[i * tokens : (i + 1) * tokens]


def attend_back_body(chunks, place_ref, q_ref, do_ref, lse_ref, *refs):
    k_refs, v_refs = refs[:chunks], refs[chunks : 2 * chunks]
    dq_ref = refs[2 * chunks]
    dk_refs = refs[2 * chunks + 1 : 3 * chunks + 1]
    dv_refs = refs[3 * chunks + 1 :]
    tokens = q_ref.shape[0]
    place = place_ref[0]
    mask = chunk_mask(tokens)
    for g in range(KV_STEP):
        q = two_heads(q_ref, g)
        do = two_heads(do_ref, g)
        lse = jnp.concatenate(
            [lse_ref[0, :, GROUP * g + i : GROUP * g + i + 1] for i in range(GROUP)],
            axis=0,
        )
        keys = [lanes(k, g) for k in k_refs]
        scores = head_scores(place, q, keys, mask)
        probs = [jnp.exp(s - lse) for s in scores]
        dprobs = [nt(do, lanes(v, g)) for v in v_refs]
        inner = sum(
            jnp.sum(p * d, axis=1, keepdims=True) for p, d in zip(probs, dprobs)
        )
        dq = jnp.zeros((GROUP * tokens, HEAD_DIM), F32)
        span = slice(g * HEAD_DIM, (g + 1) * HEAD_DIM)
        for r in range(chunks):
            ds = (probs[r] * (dprobs[r] - inner)).astype(BF)
            dq += nn(ds, keys[r])
            dk_refs[r][:, span] = (tn(ds, q) * SCALE).astype(BF)
            dv_refs[r][:, span] = tn(probs[r].astype(BF), do).astype(BF)
        dq = (dq * SCALE).astype(BF)
        for i in range(GROUP):
            h = GROUP * g + i
            dq_ref[:, h * HEAD_DIM : (h + 1) * HEAD_DIM] = dq[
                i * tokens : (i + 1) * tokens
            ]


def attention_specs(tokens):
    q_width = KV_STEP * GROUP * HEAD_DIM
    k_width = KV_STEP * HEAD_DIM
    steps = KV_HEADS // KV_STEP
    q_spec = pl.BlockSpec((tokens, q_width), lambda i, s: (0, i))
    k_spec = pl.BlockSpec((tokens, k_width), lambda i, s: (0, i))
    v_spec = pl.BlockSpec((tokens, k_width), lambda i, s: (0, i + steps))
    lse_spec = pl.BlockSpec((1, tokens, 128), lambda i, s: (i, 0, 0))
    return steps, q_spec, k_spec, v_spec, lse_spec


def attend(place, q, kvs):
    chunks, tokens = len(kvs), q.shape[0]
    steps, q_spec, k_spec, v_spec, lse_spec = attention_specs(tokens)
    span = chunks * tokens
    flops = 4 * HEADS * HEAD_DIM * tokens * span
    return pl.pallas_call(
        functools.partial(attend_body, chunks),
        grid_spec=pltpu.PrefetchScalarGridSpec(
            num_scalar_prefetch=1,
            grid=(steps,),
            in_specs=[q_spec] + [k_spec] * chunks + [v_spec] * chunks,
            out_specs=[q_spec, lse_spec],
        ),
        out_shape=[
            jax.ShapeDtypeStruct(q.shape, BF),
            jax.ShapeDtypeStruct((steps, tokens, 128), F32),
        ],
        cost_estimate=pl.CostEstimate(
            flops=flops, bytes_accessed=8 * q.size, transcendentals=HEADS * tokens * span
        ),
        name="attend",
    )(place, q, *kvs, *kvs)


def attend_back(place, q, do, lse, kvs):
    chunks, tokens = len(kvs), q.shape[0]
    steps, q_spec, k_spec, v_spec, lse_spec = attention_specs(tokens)
    span = chunks * tokens
    kvd = KV_HEADS * HEAD_DIM
    flops = 10 * HEADS * HEAD_DIM * tokens * span
    outs = pl.pallas_call(
        functools.partial(attend_back_body, chunks),
        grid_spec=pltpu.PrefetchScalarGridSpec(
            num_scalar_prefetch=1,
            grid=(steps,),
            in_specs=[q_spec, q_spec, lse_spec] + [k_spec] * chunks + [v_spec] * chunks,
            out_specs=[q_spec] + [k_spec] * (2 * chunks),
        ),
        out_shape=[jax.ShapeDtypeStruct(q.shape, BF)]
        + [jax.ShapeDtypeStruct((tokens, kvd), BF)] * (2 * chunks),
        cost_estimate=pl.CostEstimate(
            flops=flops, bytes_accessed=16 * q.size, transcendentals=HEADS * tokens * span
        ),
        name="attend_back",
    )(place, q, do, lse, *kvs, *kvs)
    return outs[0], outs[1 : chunks + 1], outs[chunks + 1 :]


def flip(value, axis, bit):
    size = lax.axis_size(axis)
    return lax.ppermute(value, axis, [(i, i ^ bit) for i in range(size)])


def gather_rows(shard, bits, me, parts):
    pieces = {0: shard}
    for bit in list(bits) + [1]:
        pieces.update({off ^ bit: flip(piece, "dp", bit) for off, piece in list(pieces.items())})
    rows = shard.shape[0]
    whole = jnp.zeros((parts * rows, shard.shape[1]), shard.dtype)
    for off, piece in pieces.items():
        whole = lax.dynamic_update_slice(whole, piece, ((me ^ off) * rows, 0))
    return whole


def xor_order(bits):
    order = [0]
    for bit in list(reversed(bits)) + [1]:
        order = order + [off ^ bit for off in order]
    return order


def scatter_term(left, right, bits):
    half = left.shape[1] // 2
    away = tn(left[:, half:], right).astype(BF)
    came = flip(away, "dp", 1)
    quarter = half // 2
    away = (tn(left[:, quarter:half], right) + came[quarter:]).astype(BF)
    kept = (tn(left[:, :quarter], right) + came[:quarter]).astype(BF)
    came = flip(away, "dp", bits[0])
    for bit in bits[1:]:
        size = kept.shape[0] // 2
        away = (kept[size:].astype(F32) + came[size:]).astype(BF)
        kept = (kept[:size].astype(F32) + came[:size]).astype(BF)
        came = flip(away, "dp", bit)
    return (kept.astype(F32) + came).astype(BF)


def line_sum(value, place):
    size = lax.axis_size("seq")
    rows = value.shape[0] // size

    def chunk(index):
        index = jnp.clip(index, 0, size - 1)
        return lax.dynamic_slice_in_dim(value, index * rows, rows, 0)

    total = chunk(place).astype(F32)
    for way in (1, -1):
        held = None
        for far in range(size - 1, 0, -1):
            mine = chunk(place + way * far)
            if held is not None:
                mine = (mine.astype(F32) + held).astype(BF)
            pairs = [(i, i + way) for i in range(size) if 0 <= i + way * far < size]
            held = lax.ppermute(mine, "seq", pairs)
        total = total + held
    total = total.astype(BF)
    out = jnp.zeros(value.shape, F32)
    out = lax.dynamic_update_slice(out, total.astype(F32), (place * rows, 0))
    for way in (1, -1):
        held = total
        for far in range(1, size):
            pairs = [
                (i, i + way) for i in range(size) if 0 <= i + way < size and 0 <= i - way * (far - 1) < size
            ]
            held = lax.ppermute(held, "seq", pairs)
            source = place - way * far
            index = jnp.clip(source, 0, size - 1) * rows
            old = lax.dynamic_slice(out, (index, 0), held.shape)
            good = (source >= 0) & (source < size)
            out = lax.dynamic_update_slice(
                out, jnp.where(good, held.astype(F32), old), (index, 0)
            )
    return out


def rope_tables(place, tokens, width):
    half = HEAD_DIM // 2
    positions = (place * tokens + jnp.arange(tokens, dtype=jnp.int32)).astype(F32)
    frequency = ROPE_BASE ** (-jnp.arange(half).astype(F32) / half)
    angles = positions[:, None] * frequency[None, :]
    cos, sin = jnp.cos(angles), jnp.sin(angles)
    zero = jnp.zeros_like(sin)
    heads = width // HEAD_DIM
    tile = lambda a, b: jnp.tile(jnp.concatenate([a, b], axis=1), (1, heads))
    return tile(cos, cos), tile(sin, zero), tile(zero, sin)


def rotate(field, tables, sign):
    cos, first, second = tables
    half = HEAD_DIM // 2
    width = field.shape[1]
    cos, first, second = cos[:, :width], first[:, :width], second[:, :width]
    ahead = jnp.concatenate([field[:, half:], field[:, :half]], axis=1)
    behind = jnp.concatenate([field[:, -half:], field[:, :-half]], axis=1)
    return field * cos + sign * (behind * second - ahead * first)


def norm_scale(values):
    return lax.rsqrt(jnp.mean(values * values, axis=-1, keepdims=True) + EPS)


def norm_back(values, scale, gain, grad):
    unit = values * scale
    grad_gain = jnp.sum(grad * unit, axis=0)
    scaled = grad * gain
    inner = jnp.mean(scaled * unit, axis=-1, keepdims=True)
    return scale * (scaled - unit * inner), grad_gain


def local(tokens, cotangent, w_query, w_key, w_value, w_out, w_gate, w_up, w_down, gain_attn, gain_mlp):
    dp, seq = lax.axis_size("dp"), lax.axis_size("seq")
    me, place = lax.axis_index("dp"), lax.axis_index("seq")
    bits = [1 << i for i in range(1, dp.bit_length() - 1)]
    turned = bits[1:] + bits[:1]
    model = tokens.shape[-1]
    rows = tokens.shape[1]
    kvd = w_key.shape[-1]
    place_arr = place.reshape(1).astype(jnp.int32)

    gains = {0: jnp.concatenate([gain_attn, gain_mlp], axis=0)}
    for bit in [1] + bits:
        gains.update({off ^ bit: flip(g, "dp", bit) for off, g in list(gains.items())})
    stacked = jnp.stack([gains[off] for off in range(dp)]).astype(F32)
    owner = (jnp.arange(dp)[:, None] ^ me) == jnp.arange(dp)[None, :]
    natural = jnp.sum(jnp.where(owner[:, :, None, None], stacked[None], 0.0), axis=1)
    natural = natural.transpose(1, 0, 2).reshape(2, 1, model)
    gain_one, gain_two = natural[0], natural[1]

    gather = functools.partial(gather_rows, me=me, parts=dp)
    w_q = gather(w_query[0], bits)
    w_k = gather(w_key[0], turned)
    w_v = gather(w_value[0], turned)
    w_o = gather(w_out[0], bits)
    w_g = gather(w_gate[0], bits)
    w_u = gather(w_up[0], turned)
    half_model = model // 2
    w_d = jnp.concatenate(
        [gather(w_down[0][:, :half_model], bits), gather(w_down[0][:, half_model:], turned)], axis=1
    )

    def xor_columns(value, way):
        width = value.shape[1] // dp
        cut = lambda off: lax.dynamic_slice_in_dim(value, (me ^ off) * width, width, 1)
        return jnp.concatenate([cut(off) for off in xor_order(way)], axis=1)

    tables = rope_tables(place, rows, model)
    x = tokens[0].astype(F32)
    scale_one = norm_scale(x)
    n1 = (x * scale_one * gain_one).astype(BF)
    q = rotate(nn(n1, w_q), tables, 1.0).astype(BF)
    kv = jnp.concatenate(
        [rotate(nn(n1, w_k), tables, 1.0).astype(BF), nn(n1, w_v).astype(BF)], axis=1
    )
    kvs = [kv]
    for far in range(1, seq):
        pairs = [(i, i + 1) for i in range(far - 1, seq - 1)]
        kvs.append(lax.ppermute(kvs[-1], "seq", pairs))
    mixed, lse = attend(place_arr, q, kvs)
    x2 = x + nn(mixed, w_o)
    scale_two = norm_scale(x2)
    n2 = (x2 * scale_two * gain_two).astype(BF)
    gate = nn(n2, w_g)
    up = nn(n2, w_u)
    sig = jax.nn.sigmoid(gate)
    hidden = (gate * sig * up).astype(BF)
    result = x2 + nn(hidden, w_d)

    e = cotangent[0].astype(F32)
    eb = cotangent[0]
    hidden_a = xor_columns(hidden, bits)
    hidden_b = xor_columns(hidden, turned)
    sum_down = jnp.concatenate(
        [
            scatter_term(hidden_a, eb[:, :half_model], bits),
            scatter_term(hidden_b, eb[:, half_model:], turned),
        ],
        axis=1,
    )
    dh = nt(eb, w_d)
    dgate = (dh * up * sig * (1.0 + gate * (1.0 - sig))).astype(BF)
    dup = (dh * gate * sig).astype(BF)
    n2_a, n2_b = xor_columns(n2, bits), xor_columns(n2, turned)
    sum_gate = scatter_term(n2_a, dgate, bits)
    sum_up = scatter_term(n2_b, dup, turned)
    dn2 = nt(dgate, w_g) + nt(dup, w_u)
    dx2, term_gain_two = norm_back(x2, scale_two, gain_two, dn2)
    e2 = e + dx2
    e2b = e2.astype(BF)
    mixed_a, mixed_b = xor_columns(mixed, bits), xor_columns(mixed, turned)
    sum_out = jnp.concatenate(
        [
            scatter_term(mixed_a, e2b[:, :half_model], bits),
            scatter_term(mixed_b, e2b[:, half_model:], turned),
        ],
        axis=1,
    )
    do = nt(e2b, w_o).astype(BF)
    dq, dks, dvs = attend_back(place_arr, q, do, lse, kvs)
    held = None
    for far in range(seq - 1, -1, -1):
        mine = jnp.concatenate([dks[far], dvs[far]], axis=1)
        if held is not None:
            mine = (mine.astype(F32) + held).astype(BF)
        if far:
            held = lax.ppermute(mine, "seq", [(i, i - 1) for i in range(far, seq)])
    dk, dv = mine[:, :kvd], mine[:, kvd:]
    dqp = rotate(dq.astype(F32), tables, -1.0).astype(BF)
    dkp = rotate(dk.astype(F32), tables, -1.0).astype(BF)
    n1_a, n1_b = xor_columns(n1, bits), xor_columns(n1, turned)
    sum_query = scatter_term(n1_a, dqp, bits)
    sum_kv = scatter_term(n1_b, jnp.concatenate([dkp, dv], axis=1), turned)
    dn1 = nt(dqp, w_q) + nt(dkp, w_k) + nt(dv, w_v)
    dx1, term_gain_one = norm_back(x, scale_one, gain_one, dn1)
    input_grad = e2 + dx1

    both = jnp.stack([term_gain_one, term_gain_two])
    for bit in [1] + bits:
        both = both + flip(both, "dp", bit)
    for bit in [1 << i for i in range(seq.bit_length() - 1)]:
        both = both + flip(both, "seq", bit)
    width = model // dp
    both = lax.dynamic_slice_in_dim(both, me * width, width, 1)

    g_down = line_sum(sum_down, place)
    g_gate = line_sum(sum_gate, place)
    g_up = line_sum(sum_up, place)
    g_out = line_sum(sum_out, place)
    g_query = line_sum(sum_query, place)
    g_kv = line_sum(sum_kv, place)
    return (
        result[None],
        input_grad[None],
        g_query[None],
        g_kv[None, :, :kvd],
        g_kv[None, :, kvd:],
        g_out[None],
        g_gate[None],
        g_up[None],
        g_down[None],
        both[0:1],
        both[1:2],
    )


def solution(mesh):
    by_token = P("dp", "seq", None)
    by_row = P(None, "dp", None)
    by_gain = P(None, "dp")
    in_specs = (by_token,) * 2 + (by_row,) * 7 + (by_gain,) * 2
    return jax.shard_map(local, mesh=mesh, in_specs=in_specs, out_specs=in_specs, check_vma=False)
```

time: 1260 us -> 994 us (0.79)
  waiting for transfers between devices: 865 us -> 421 us
  starting transfers between devices: 23.1 us -> 245 us
  blocking collectives: 91.5 us -> 0 us
  local copies, waits for them, and re-layouts: 41.4 us -> 128 us
  matrix products: 174 us -> 111 us
  Pallas kernels: 0 us -> 38.2 us
    ppermute x0 -> x170, waiting for transfers between devices: none -> 421 us  [the longest x92 308 us: flip(): return lax.ppermute(value, axis, [(i, i ^ bit) for i in range(size)])]
    reduce_scatter x7 -> x0, waiting for transfers between devices: 408 us -> none  [the longest x1 95.8 us: reduce_terms(): lax.psum_scatter(terms[5].astype(jnp.bfloat16), 'dp', scatter_dimension=0...]
    ppermute x0 -> x170, starting transfers between devices: none -> 245 us  [the longest x36 106 us: line_sum(): held = lax.ppermute(mine, 'seq', pairs)]
    all_gather x7 -> x0, waiting for transfers between devices: 204 us -> none  [the longest x1 64.3 us: local(): lax.all_gather(w_down[layer_index], 'dp', axis=0, tiled=True)]
    psum x1 -> x0, waiting for transfers between devices: 183 us -> none  [reduce_terms(): lax.psum(shards_summed[0].astype(jnp.bfloat16), 'seq').astype(jnp.float32)]
    all_to_all x5 -> x0, waiting for transfers between devices: 65.7 us -> none  [the longest x1 20.5 us: backward_layer(): lax.all_to_all(outgoing, 'seq', split_axis=2, concat_axis=1, tiled=True)]
    dot_general x35 -> x38, matrix products: 174 us -> 111 us  [dot(): return lax.dot_general(a, b, (dims, ((), ())), preferred_element_type=F32)]
    dynamic_update_slice x8 -> x63, local copies, waits for them, and re-layouts: 4.01 us -> 63 us  [gather_rows(): whole = lax.dynamic_update_slice(whole, piece, ((me ^ off) * rows, 0))]
  transfers between devices with their start and end apart: 20 -> 170, of which waited for: 17 -> 67; matrix products, arithmetic and copies ran while one was open for 11% -> 21% of each run, Pallas kernels for 0% -> 2%
where the time goes in v1:
time: 994 us; the launch traced here: 982 us
  waiting for transfers between devices  421 us (42%)
  starting transfers between devices  245 us (25%)
  local copies, waits for them, and re-layouts  128 us (13%)
  matrix products  111 us (11%)
  Pallas kernels  38.2 us (4%)
  other arithmetic  34.4 us (3%)
    ppermute x92, waiting for transfers between devices, flip(): return lax.ppermute(value, axis, [(i, i ^ bit) for i in range(size)])  308 us
    dot_general x38, matrix products, dot(): return lax.dot_general(a, b, (dims, ((), ())), preferred_element_type=F32)  111 us
    ppermute x36, starting transfers between devices, line_sum(): held = lax.ppermute(mine, 'seq', pairs)  106 us
    ppermute x36, waiting for transfers between devices, line_sum(): held = lax.ppermute(held, 'seq', pairs)  73 us
    ppermute x92, starting transfers between devices, flip(): return lax.ppermute(value, axis, [(i, i ^ bit) for i in range(size)])  66.2 us
    ppermute x36, starting transfers between devices, line_sum(): held = lax.ppermute(held, 'seq', pairs)  64.2 us
    dynamic_update_slice x63, local copies, waits for them, and re-layouts, gather_rows(): whole = lax.dynamic_update_slice(whole, piece, ((me ^ off) * rows, 0))  63 us
    ppermute x36, waiting for transfers between devices, line_sum(): held = lax.ppermute(mine, 'seq', pairs)  34 us
  transfers between devices with their start and end apart: 170, of which 67 were waited for; matrix products, arithmetic and copies ran while one was open for 21% of the time, Pallas kernels for 2%

profile of v1, /device:TPU:0, one launch (start us, length us, event | category | flops | bytes accessed | tf_op | source)
XLA Modules:
  0.0 982.4 jit_solution(16122616669997591050)
XLA Ops:
  70.3 11.3 %collective-permute-done.22 = bf16[192,768]{1,0:T(8,128)(2,1)S(1)} collective-permute-done((bf16[192,768]{1,0:T(8,128)(2,1)}, bf16[192,768]{1,0:T(8,128)(2,1)S(1)}, u32[]{:S(2)}, u32[]{:S(2)}) %collective-permute-start.22) | collective-permute-done | bytes 294944 | tf_op jit(solution)/shard_map/ppermute | solution.py:192
  87.6 9.9 %collective-permute-done.31 = bf16[192,1536]{1,0:T(8,128)(2,1)S(1)} collective-permute-done((bf16[192,1536]{1,0:T(8,128)(2,1)}, bf16[192,1536]{1,0:T(8,128)(2,1)S(1)}, u32[]{:S(2)}, u32[]{:S(2)}) %collective-permute-start.31) | collective-permute-done | bytes 589856 | tf_op jit(solution)/shard_map/ppermute | solution.py:192
  118.7 9.6 collective-permute-done.52
  132.9 14.1 %collective-permute-done.59 = bf16[512,768]{1,0:T(8,128)(2,1)S(1)} collective-permute-done((bf16[512,768]{1,0:T(8,128)(2,1)S(1)}, bf16[512,768]{1,0:T(8,128)(2,1)S(1)}, u32[]{:S(2)}, u32[]{:S(2)}) %collective-permute-start.59) | collective-permute-done | bytes 786464 | tf_op jit(solution)/shard_map/ppermute | solution.py:192
  159.0 35.2 %collective-permute-done.9 = bf16[192,1536]{1,0:T(8,128)(2,1)S(1)} collective-permute-done((bf16[192,1536]{1,0:T(8,128)(2,1)}, bf16[192,1536]{1,0:T(8,128)(2,1)S(1)}, u32[]{:S(2)}, u32[]{:S(2)}) %collective-permute-start.9) | collective-permute-done | bytes 589856 | tf_op jit(solution)/shard_map/ppermute | solution.py:192
  196.5 13.6 %collective-permute-done.33 = bf16[192,1536]{1,0:T(8,128)(2,1)S(1)} collective-permute-done((bf16[192,1536]{1,0:T(8,128)(2,1)S(1)}, bf16[192,1536]{1,0:T(8,128)(2,1)S(1)}, u32[]{:S(2)}, u32[]{:S(2)}) %collective-permute-start.33) | collective-permute-done | bytes 589856 | tf_op jit(solution)/shard_map/ppermute | solution.py:192
  217.1 12.0 %collective-permute-done.54 = bf16[512,768]{1,0:T(8,128)(2,1)S(1)} collective-permute-done((bf16[512,768]{1,0:T(8,128)(2,1)S(1)}, bf16[512,768]{1,0:T(8,128)(2,1)S(1)}, u32[]{:S(2)}, u32[]{:S(2)}) %collective-permute-start.54) | collective-permute-done | bytes 786464 | tf_op jit(solution)/shard_map/ppermute | solution.py:192
  231.9 34.5 %collective-permute-done.61 = bf16[512,768]{1,0:T(8,128)(2,1)S(1)} collective-permute-done((bf16[512,768]{1,0:T(8,128)(2,1)S(1)}, bf16[512,768]{1,0:T(8,128)(2,1)S(1)}, u32[]{:S(2)}, u32[]{:S(2)}) %collective-permute-start.61) | collective-permute-done | bytes 786464 | tf_op jit(solution)/shard_map/ppermute | solution.py:192
  277.1 21.4 %collective-permute-done.38 = bf16[192,4096]{1,0:T(8,128)(2,1)S(1)} collective-permute-done((bf16[192,4096]{1,0:T(8,128)(2,1)S(1)}, bf16[192,4096]{1,0:T(8,128)(2,1)S(1)}, u32[]{:S(2)}, u32[]{:S(2)}) %collective-permute-start.38) | collective-permute-done | bytes 1572896 | tf_op jit(solution)/shard_map/ppermute | solution.py:192
  315.1 7.9 fusion.2
  323.0 16.9 %collective-permute-done.47 = bf16[192,4096]{1,0:T(8,128)(2,1)} collective-permute-done((bf16[192,4096]{1,0:T(8,128)(2,1)S(1)}, bf16[192,4096]{1,0:T(8,128)(2,1)}, u32[]{:S(2)}, u32[]{:S(2)}) %collective-permute-start.47) | collective-permute-done | bytes 1572896 | tf_op jit(solution)/shard_map/ppermute | solution.py:192
  350.7 23.8 %collective-permute-done.40 = bf16[192,4096]{1,0:T(8,128)(2,1)} collective-permute-done((bf16[192,4096]{1,0:T(8,128)(2,1)S(1)}, bf16[192,4096]{1,0:T(8,128)(2,1)}, u32[]{:S(2)}, u32[]{:S(2)}) %collective-permute-start.40) | collective-permute-done | bytes 1572896 | tf_op jit(solution)/shard_map/ppermute | solution.py:192
  382.7 18.4 %attend.1 = (bf16[256,1536]{1,0:T(8,128)(2,1)}, f32[2,256,128]{2,1,0:T(8,128)}) custom-call(s32[1]{0:T(128)} %bitcast.1.place_ref, bf16[256,1536]{1,0:T(8,128)(2,1)} %fusion.20.q_ref, bf16[256,1536]{1,0:T(8,128)(2,1)} %copy-done.45, bf16[256,1536]{1,0:T(8,128)(2,1)} %collective-permute-done.28.refs_1_.refs_5_, bf16[256,1536]{1,0:T(8,128)(2,1)} %copy-done.94, ...), custom_call_target="tpu_custom_call" | custom-call | flops 1610612736 | bytes 3145728 | tf_op jit(solution)/shard_map/attend/pallas_call | solution.py:147
  412.2 6.6 fusion.168
  421.6 9.6 multiply_convert_fusion.1
  431.2 9.1 fusion.169
  440.3 9.5 multiply_reduce_fusion
  455.9 19.8 %attend_back.1 = (bf16[256,1536]{1,0:T(8,128)(2,1)}, bf16[256,768]{1,0:T(8,128)(2,1)}, bf16[256,768]{1,0:T(8,128)(2,1)}, bf16[256,768]{1,0:T(8,128)(2,1)}, bf16[...) custom-call(s32[1]{0:T(128)} %bitcast.1.place_ref, ...), custom_call_target="tpu_custom_call" | custom-call | flops 4026531840 | bytes 6291456 | tf_op jit(solution)/shard_map/attend_back/pallas_call | solution.py:172
  488.3 6.9 fusion.4
  514.1 11.2 %collective-permute-done.103 = bf16[384,768]{1,0:T(8,128)(2,1)S(1)} collective-permute-done((bf16[384,768]{1,0:T(8,128)(2,1)S(1)}, bf16[384,768]{1,0:T(8,128)(2,1)S(1)}, u32[]{:S(2)}, u32[]{:S(2)}) %collective-permute-start.103) | collective-permute-done | bytes 589856 | tf_op jit(solution)/shard_map/ppermute | solution.py:192
  535.4 13.1 %collective-permute-start.105 = (bf16[48,1536]{1,0:T(8,128)(2,1)S(1)}, bf16[48,1536]{1,0:T(8,128)(2,1)S(1)}, u32[]{:S(2)}, u32[]{:S(2)}) collective-permute-start(bf16[48,1536]{1,0:T(8,128)(2,1)S(1)} %get-tuple-element.259), channel_id=1, source_target_pairs={{0,1},{4,5},{8,9},{12,13},{16,17},{20,21},{24,25},{28,29}} | collective-permute-start | bytes 442376 | tf_op jit(solution)/shard_map/ppermute | solution.py:245
  555.6 6.6 collective-permute-done.68
  572.1 10.9 %collective-permute-start.107 = (bf16[48,1536]{1,0:T(8,128)(2,1)S(1)}, bf16[48,1536]{1,0:T(8,128)(2,1)S(1)}, u32[]{:S(2)}, u32[]{:S(2)}) collective-permute-start(bf16[48,1536]{1,0:T(8,128)(2,1)S(1)} %get-tuple-element.255), channel_id=1, source_target_pairs={{0,1},{1,2},{2,3},{4,5},{5,6},{6,7},{8,9},{9,10},{10,11},{12,13},{... | collective-permute-start | bytes 442376 | tf_op jit(solution)/shard_map/ppermute | solution.py:245
  630.6 9.5 collective-permute-done.71
  658.5 7.9 collective-permute-start.74
  709.9 9.8 %collective-permute-done.149 = bf16[512,768]{0,1:T(8,128)(2,1)S(1)} collective-permute-done((bf16[512,768]{0,1:T(8,128)(2,1)S(1)}, bf16[512,768]{0,1:T(8,128)(2,1)S(1)}, u32[]{:S(2)}, u32[]{:S(2)}) %collective-permute-start.149) | collective-permute-done | bytes 786464 | tf_op jit(solution)/shard_map/ppermute | solution.py:192
  723.5 19.1 %collective-permute-done.85 = bf16[384,1536]{1,0:T(8,128)(2,1)S(1)} collective-permute-done((bf16[384,1536]{1,0:T(8,128)(2,1)S(1)}, bf16[384,1536]{1,0:T(8,128)(2,1)S(1)}, u32[]{:S(2)}, u32[]{:S(2)}) %collective-permute-start.85) | collective-permute-done | bytes 1179680 | tf_op jit(solution)/shard_map/ppermute | solution.py:192
  808.3 15.1 %collective-permute-done.97 = bf16[48,1536]{1,0:T(8,128)(2,1)S(1)} collective-permute-done((bf16[48,1536]{1,0:T(8,128)(2,1)S(1)}, bf16[48,1536]{1,0:T(8,128)(2,1)S(1)}, u32[]{:S(2)}, u32[]{:S(2)}) %collective-permute-start.97) | collective-permute-done | bytes 147488 | tf_op jit(solution)/shard_map/ppermute | solution.py:256
  846.8 20.3 %collective-permute-done.134 = bf16[192,4096]{1,0:T(8,128)(2,1)} collective-permute-done((bf16[192,4096]{1,0:T(8,128)(2,1)}, bf16[192,4096]{1,0:T(8,128)(2,1)}, u32[]{:S(2)}, u32[]{:S(2)}) %collective-permute-start.134) | collective-permute-done | bytes 1572896 | tf_op jit(solution)/shard_map/ppermute | solution.py:192
  916.0 7.3 collective-permute-done.140
  923.8 10.6 %collective-permute-start.141 = (bf16[48,4096]{1,0:T(8,128)(2,1)S(1)}, bf16[48,4096]{1,0:T(8,128)(2,1)S(1)}, u32[]{:S(2)}, u32[]{:S(2)}) collective-permute-start(bf16[48,4096]{1,0:T(8,128)(2,1)S(1)} %get-tuple-element.174), channel_id=1, source_target_pairs={{0,1},{1,2},{2,3},{4,5},{5,6},{6,7},{8,9},{9,10},{10,11},{12,13},{... | collective-permute-start | bytes 1179656 | tf_op jit(solution)/shard_map/ppermute | solution.py:256
  936.3 6.6 collective-permute-start.126
  (800 shorter events, 540.1 us)
Async XLA Ops:
  1.4 49.0 %collective-permute-start = (bf16[2,192]{1,0:T(2,128)(2,1)S(1)}, bf16[2,192]{1,0:T(2,128)(2,1)S(1)}, u32[]{:S(2)}, u32[]{:S(2)}) collective-permute-start(bf16[2,192]{1,0:T(2,128)(2,1)S(1)} %pad_maximum_fusion.97), channel_id=1, source_target_pairs={{0,4},{4,0},{8,12},{12,8},{16,20},{20,16},{24,28},{28,24},{1,5},{5... | collective-permute-start | bytes 2312 | tf_op jit(solution)/shard_map/ppermute | solution.py:192
  1.9 50.5 %collective-permute-start.1 = (bf16[2,192]{1,0:T(2,128)(2,1)S(1)}, bf16[2,192]{1,0:T(2,128)(2,1)S(1)}, u32[]{:S(2)}, u32[]{:S(2)}) collective-permute-start(bf16[2,192]{1,0:T(2,128)(2,1)S(1)} %pad_maximum_fusion.97), channel_id=1, source_target_pairs={{0,8},{4,12},{8,0},{12,4},{16,24},{20,28},{24,16},{28,20},{1,9},{5... | collective-permute-start | bytes 2312 | tf_op jit(solution)/shard_map/ppermute | solution.py:192
  4.5 51.0 %collective-permute-start.3 = (bf16[2,192]{1,0:T(2,128)(2,1)S(1)}, bf16[2,192]{1,0:T(2,128)(2,1)S(1)}, u32[]{:S(2)}, u32[]{:S(2)}) collective-permute-start(bf16[2,192]{1,0:T(2,128)(2,1)S(1)} %pad_maximum_fusion.97), channel_id=1, source_target_pairs={{0,16},{4,20},{8,24},{12,28},{16,0},{20,4},{24,8},{28,12},{1,17},{... | collective-permute-start | bytes 2312 | tf_op jit(solution)/shard_map/ppermute | solution.py:192
  6.0 56.3 %collective-permute-start.14 = (bf16[192,768]{1,0:T(8,128)(2,1)}, bf16[192,768]{1,0:T(8,128)(2,1)}, u32[]{:S(2)}, u32[]{:S(2)}) collective-permute-start(bf16[192,768]{1,0:T(8,128)(2,1)} %bitcast.139), channel_id=1, source_target_pairs={{0,16},{4,20},{8,24},{12,28},{16,0},{20,4},{24,8},{28,12},{1,17},{... | collective-permute-start | bytes 884744 | tf_op jit(solution)/shard_map/ppermute | solution.py:192
  56.0 45.4 %collective-permute-start.17 = (bf16[192,768]{1,0:T(8,128)(2,1)S(1)}, bf16[192,768]{1,0:T(8,128)(2,1)}, u32[]{:S(2)}, u32[]{:S(2)}) collective-permute-start(bf16[192,768]{1,0:T(8,128)(2,1)S(1)} %bitcast.141), channel_id=1, source_target_pairs={{0,4},{4,0},{8,12},{12,8},{16,20},{20,16},{24,28},{28,24},{1,5},{5... | collective-permute-start | bytes 884744 | tf_op jit(solution)/shard_map/ppermute | solution.py:192
  68.6 36.8 %collective-permute-start.24 = (bf16[192,768]{1,0:T(8,128)(2,1)}, bf16[192,768]{1,0:T(8,128)(2,1)S(1)}, u32[]{:S(2)}, u32[]{:S(2)}) collective-permute-start(bf16[192,768]{1,0:T(8,128)(2,1)} %bitcast.144), channel_id=1, source_target_pairs={{0,4},{4,0},{8,12},{12,8},{16,20},{20,16},{24,28},{28,24},{1,5},{5... | collective-permute-start | bytes 884744 | tf_op jit(solution)/shard_map/ppermute | solution.py:192
  117.8 76.5 %collective-permute-start.10 = (bf16[192,1536]{1,0:T(8,128)(2,1)S(1)}, bf16[192,1536]{1,0:T(8,128)(2,1)S(1)}, u32[]{:S(2)}, u32[]{:S(2)}) collective-permute-start(bf16[192,1536]{1,0:T(8,128)(2,1)S(1)} %bitcast.135), channel_id=1, source_target_pairs={{0,4},{4,0},{8,12},{12,8},{16,20},{20,16},{24,28},{28,24},{1,5},{5... | collective-permute-start | bytes 1769480 | tf_op jit(solution)/shard_map/ppermute | solution.py:192
  128.3 84.0 %collective-permute-start.34 = (bf16[192,1536]{1,0:T(8,128)(2,1)S(1)}, bf16[192,1536]{1,0:T(8,128)(2,1)S(1)}, u32[]{:S(2)}, u32[]{:S(2)}) collective-permute-start(bf16[192,1536]{1,0:T(8,128)(2,1)S(1)} %bitcast.138), channel_id=1, source_target_pairs={{0,4},{4,0},{8,12},{12,8},{16,20},{20,16},{24,28},{28,24},{1,5},{5... | collective-permute-start | bytes 1769480 | tf_op jit(solution)/shard_map/ppermute | solution.py:192
  147.0 70.0 %collective-permute-start.45 = (bf16[192,4096]{1,0:T(8,128)(2,1)S(1)}, bf16[192,4096]{1,0:T(8,128)(2,1)S(1)}, u32[]{:S(2)}, u32[]{:S(2)}) collective-permute-start(bf16[192,4096]{1,0:T(8,128)(2,1)S(1)} %bitcast.127), channel_id=1, source_target_pairs={{0,16},{4,20},{8,24},{12,28},{16,0},{20,4},{24,8},{28,12},{1,17},{... | collective-permute-start | bytes 4718600 | tf_op jit(solution)/shard_map/ppermute | solution.py:192
  150.2 44.0 %collective-permute-start.9 = (bf16[192,1536]{1,0:T(8,128)(2,1)}, bf16[192,1536]{1,0:T(8,128)(2,1)S(1)}, u32[]{:S(2)}, u32[]{:S(2)}) collective-permute-start(bf16[192,1536]{1,0:T(8,128)(2,1)} %collective-permute-done.7), channel_id=1, source_target_pairs={{0,16},{4,20},{8,24},{12,28},{16,0},{20,4},{24,8},{28,12},{1,17},{... | collective-permute-start | bytes 1769480 | tf_op jit(solution)/shard_map/ppermute | solution.py:192
  154.5 41.2 %collective-permute-start.11 = (bf16[192,1536]{1,0:T(8,128)(2,1)}, bf16[192,1536]{1,0:T(8,128)(2,1)S(1)}, u32[]{:S(2)}, u32[]{:S(2)}) collective-permute-start(bf16[192,1536]{1,0:T(8,128)(2,1)} %collective-permute-done.7), channel_id=1, source_target_pairs={{0,4},{4,0},{8,12},{12,8},{16,20},{20,16},{24,28},{28,24},{1,5},{5... | collective-permute-start | bytes 1769480 | tf_op jit(solution)/shard_map/ppermute | solution.py:192
  212.3 56.4 %collective-permute-start.46 = (bf16[192,4096]{1,0:T(8,128)(2,1)S(1)}, bf16[192,4096]{1,0:T(8,128)(2,1)S(1)}, u32[]{:S(2)}, u32[]{:S(2)}) collective-permute-start(bf16[192,4096]{1,0:T(8,128)(2,1)S(1)} %bitcast.128), channel_id=1, source_target_pairs={{0,8},{4,12},{8,0},{12,4},{16,24},{20,28},{24,16},{28,20},{1,9},{5... | collective-permute-start | bytes 4718600 | tf_op jit(solution)/shard_map/ppermute | solution.py:192
  214.7 52.6 %collective-permute-start.55 = (bf16[512,768]{1,0:T(8,128)(2,1)S(1)}, bf16[512,768]{1,0:T(8,128)(2,1)S(1)}, u32[]{:S(2)}, u32[]{:S(2)}) collective-permute-start(bf16[512,768]{1,0:T(8,128)(2,1)S(1)} %copy-done.47), channel_id=1, source_target_pairs={{0,4},{4,0},{8,12},{12,8},{16,20},{20,16},{24,28},{28,24},{1,5},{5... | collective-permute-start | bytes 2359304 | tf_op jit(solution)/shard_map/ppermute | solution.py:192
  215.6 50.8 %collective-permute-start.61 = (bf16[512,768]{1,0:T(8,128)(2,1)S(1)}, bf16[512,768]{1,0:T(8,128)(2,1)S(1)}, u32[]{:S(2)}, u32[]{:S(2)}) collective-permute-start(bf16[512,768]{1,0:T(8,128)(2,1)S(1)} %collective-permute-done.59), channel_id=1, source_target_pairs={{0,8},{4,12},{8,0},{12,4},{16,24},{20,28},{24,16},{28,20},{1,9},{5... | collective-permute-start | bytes 2359304 | tf_op jit(solution)/shard_map/ppermute | solution.py:192
  216.9 51.0 %collective-permute-start.62 = (bf16[512,768]{1,0:T(8,128)(2,1)S(1)}, bf16[512,768]{1,0:T(8,128)(2,1)S(1)}, u32[]{:S(2)}, u32[]{:S(2)}) collective-permute-start(bf16[512,768]{1,0:T(8,128)(2,1)S(1)} %copy-done.46), channel_id=1, source_target_pairs={{0,4},{4,0},{8,12},{12,8},{16,20},{20,16},{24,28},{28,24},{1,5},{5... | collective-permute-start | bytes 2359304 | tf_op jit(solution)/shard_map/ppermute | solution.py:192
  229.2 69.3 %collective-permute-start.38 = (bf16[192,4096]{1,0:T(8,128)(2,1)S(1)}, bf16[192,4096]{1,0:T(8,128)(2,1)S(1)}, u32[]{:S(2)}, u32[]{:S(2)}) collective-permute-start(bf16[192,4096]{1,0:T(8,128)(2,1)S(1)} %bitcast.130), channel_id=1, source_target_pairs={{0,8},{4,12},{8,0},{12,4},{16,24},{20,28},{24,16},{28,20},{1,9},{5... | collective-permute-start | bytes 4718600 | tf_op jit(solution)/shard_map/ppermute | solution.py:192
  267.9 36.4 %collective-permute-start.39 = (bf16[192,4096]{1,0:T(8,128)(2,1)S(1)}, bf16[192,4096]{1,0:T(8,128)(2,1)S(1)}, u32[]{:S(2)}, u32[]{:S(2)}) collective-permute-start(bf16[192,4096]{1,0:T(8,128)(2,1)S(1)} %bitcast.131), channel_id=1, source_target_pairs={{0,16},{4,20},{8,24},{12,28},{16,0},{20,4},{24,8},{28,12},{1,17},{... | collective-permute-start | bytes 4718600 | tf_op jit(solution)/shard_map/ppermute | solution.py:192
  271.4 71.8 %collective-permute-start.48 = (bf16[192,4096]{1,0:T(8,128)(2,1)S(1)}, bf16[192,4096]{1,0:T(8,128)(2,1)S(1)}, u32[]{:S(2)}, u32[]{:S(2)}) collective-permute-start(bf16[192,4096]{1,0:T(8,128)(2,1)S(1)} %bitcast.129), channel_id=1, source_target_pairs={{0,4},{4,0},{8,12},{12,8},{16,20},{20,16},{24,28},{28,24},{1,5},{5... | collective-permute-start | bytes 4718600 | tf_op jit(solution)/shard_map/ppermute | solution.py:192
  271.7 71.6 %collective-permute-start.28 = (bf16[256,1536]{1,0:T(8,128)(2,1)S(1)}, bf16[256,1536]{1,0:T(8,128)(2,1)}, u32[]{:S(2)}, u32[]{:S(2)}) collective-permute-start(bf16[256,1536]{1,0:T(8,128)(2,1)S(1)} %pad_maximum_fusion.15.refs_0_.refs_4_), channel_id=1, source_target_pairs={{0,1},{1,2},{2,3},{4,5},{5,6},{6,7},{8,9},{9,10},{10,11},{12,13},{... | collective-permute-start | bytes 2359304 | tf_op jit(solution)/shard_map/ppermute | solution.py:348
  304.3 35.6 %collective-permute-start.47 = (bf16[192,4096]{1,0:T(8,128)(2,1)S(1)}, bf16[192,4096]{1,0:T(8,128)(2,1)}, u32[]{:S(2)}, u32[]{:S(2)}) collective-permute-start(bf16[192,4096]{1,0:T(8,128)(2,1)S(1)} %collective-permute-done.45), channel_id=1, source_target_pairs={{0,8},{4,12},{8,0},{12,4},{16,24},{20,28},{24,16},{28,20},{1,9},{5... | collective-permute-start | bytes 4718600 | tf_op jit(solution)/shard_map/ppermute | solution.py:192
  313.7 34.9 %collective-permute-start.50 = (bf16[192,4096]{1,0:T(8,128)(2,1)S(1)}, bf16[192,4096]{1,0:T(8,128)(2,1)S(1)}, u32[]{:S(2)}, u32[]{:S(2)}) collective-permute-start(bf16[192,4096]{1,0:T(8,128)(2,1)S(1)} %collective-permute-done.46), channel_id=1, source_target_pairs={{0,4},{4,0},{8,12},{12,8},{16,20},{20,16},{24,28},{28,24},{1,5},{5... | collective-permute-start | bytes 4718600 | tf_op jit(solution)/shard_map/ppermute | solution.py:192
  374.6 34.9 %collective-permute-start.51 = (bf16[192,4096]{1,0:T(8,128)(2,1)}, bf16[192,4096]{1,0:T(8,128)(2,1)}, u32[]{:S(2)}, u32[]{:S(2)}) collective-permute-start(bf16[192,4096]{1,0:T(8,128)(2,1)} %collective-permute-done.47), channel_id=1, source_target_pairs={{0,4},{4,0},{8,12},{12,8},{16,20},{20,16},{24,28},{28,24},{1,5},{5... | collective-permute-start | bytes 4718600 | tf_op jit(solution)/shard_map/ppermute | solution.py:192
  377.3 41.5 %collective-permute-start.44 = (bf16[192,4096]{1,0:T(8,128)(2,1)}, bf16[192,4096]{1,0:T(8,128)(2,1)}, u32[]{:S(2)}, u32[]{:S(2)}) collective-permute-start(bf16[192,4096]{1,0:T(8,128)(2,1)} %collective-permute-done.40), channel_id=1, source_target_pairs={{0,4},{4,0},{8,12},{12,8},{16,20},{20,16},{24,28},{28,24},{1,5},{5... | collective-permute-start | bytes 4718600 | tf_op jit(solution)/shard_map/ppermute | solution.py:192
  497.3 147.3 %collective-permute-start.150 = (bf16[2048,768]{0,1:T(8,128)(2,1)}, bf16[2048,768]{0,1:T(8,128)(2,1)}, u32[]{:S(2)}, u32[]{:S(2)}) collective-permute-start(bf16[2048,768]{0,1:T(8,128)(2,1)} %convolution_convert_fusion.2), channel_id=1, source_target_pairs={{0,4},{4,0},{8,12},{12,8},{16,20},{20,16},{24,28},{28,24},{1,5},{5... | collective-permute-start | bytes 9437192 | tf_op jit(solution)/shard_map/ppermute | solution.py:192
  497.4 151.9 %collective-permute-start.147 = (bf16[2048,768]{0,1:T(8,128)(2,1)}, bf16[2048,768]{0,1:T(8,128)(2,1)}, u32[]{:S(2)}, u32[]{:S(2)}) collective-permute-start(bf16[2048,768]{0,1:T(8,128)(2,1)} %convolution_convert_fusion.3), channel_id=1, source_target_pairs={{0,4},{4,0},{8,12},{12,8},{16,20},{20,16},{24,28},{28,24},{1,5},{5... | collective-permute-start | bytes 9437192 | tf_op jit(solution)/shard_map/ppermute | solution.py:192
  551.7 36.6 %collective-permute-start.69 = (bf16[768,1536]{1,0:T(8,128)(2,1)}, bf16[768,1536]{1,0:T(8,128)(2,1)S(1)}, u32[]{:S(2)}, u32[]{:S(2)}) collective-permute-start(bf16[768,1536]{1,0:T(8,128)(2,1)} %convolution_convert_fusion.5), channel_id=1, source_target_pairs={{0,4},{4,0},{8,12},{12,8},{16,20},{20,16},{24,28},{28,24},{1,5},{5... | collective-permute-start | bytes 7077896 | tf_op jit(solution)/shard_map/ppermute | solution.py:192
  622.4 125.5 %collective-permute-start.132 = (bf16[768,4096]{1,0:T(8,128)(2,1)S(1)}, bf16[768,4096]{1,0:T(8,128)(2,1)S(1)}, u32[]{:S(2)}, u32[]{:S(2)}) collective-permute-start(bf16[768,4096]{1,0:T(8,128)(2,1)S(1)} %bitcast.118), channel_id=1, source_target_pairs={{0,4},{4,0},{8,12},{12,8},{16,20},{20,16},{24,28},{28,24},{1,5},{5... | collective-permute-start | bytes 18874376 | tf_op jit(solution)/shard_map/ppermute | solution.py:192
  630.5 46.3 %collective-permute-start.84 = (bf16[768,1536]{1,0:T(8,128)(2,1)S(1)}, bf16[768,1536]{1,0:T(8,128)(2,1)}, u32[]{:S(2)}, u32[]{:S(2)}) collective-permute-start(bf16[768,1536]{1,0:T(8,128)(2,1)S(1)} %convolution_convert_fusion.4), channel_id=1, source_target_pairs={{0,4},{4,0},{8,12},{12,8},{16,20},{20,16},{24,28},{28,24},{1,5},{5... | collective-permute-start | bytes 7077896 | tf_op jit(solution)/shard_map/ppermute | solution.py:192
  646.7 37.7 %collective-permute-start.151 = (bf16[1024,768]{0,1:T(8,128)(2,1)S(1)}, bf16[1024,768]{0,1:T(8,128)(2,1)S(1)}, u32[]{:S(2)}, u32[]{:S(2)}) collective-permute-start(bf16[1024,768]{0,1:T(8,128)(2,1)S(1)} %add_convert_fusion.4), channel_id=1, source_target_pairs={{0,16},{4,20},{8,24},{12,28},{16,0},{20,4},{24,8},{28,12},{1,17},{... | collective-permute-start | bytes 4718600 | tf_op jit(solution)/shard_map/ppermute | solution.py:192
  676.6 82.6 %collective-permute-start.117 = (bf16[768,4096]{1,0:T(8,128)(2,1)S(1)}, bf16[768,4096]{1,0:T(8,128)(2,1)S(1)}, u32[]{:S(2)}, u32[]{:S(2)}) collective-permute-start(bf16[768,4096]{1,0:T(8,128)(2,1)S(1)} %convolution_convert_fusion.1), channel_id=1, source_target_pairs={{0,4},{4,0},{8,12},{12,8},{16,20},{20,16},{24,28},{28,24},{1,5},{5... | collective-permute-start | bytes 18874376 | tf_op jit(solution)/shard_map/ppermute | solution.py:192
  749.0 83.7 %collective-permute-start.133 = (bf16[384,4096]{1,0:T(8,128)(2,1)S(1)}, bf16[384,4096]{1,0:T(8,128)(2,1)S(1)}, u32[]{:S(2)}, u32[]{:S(2)}) collective-permute-start(bf16[384,4096]{1,0:T(8,128)(2,1)S(1)} %add_convert_fusion), channel_id=1, source_target_pairs={{0,16},{4,20},{8,24},{12,28},{16,0},{20,4},{24,8},{28,12},{1,17},{... | collective-permute-start | bytes 9437192 | tf_op jit(solution)/shard_map/ppermute | solution.py:192
  767.2 71.0 %collective-permute-start.118 = (bf16[384,4096]{1,0:T(8,128)(2,1)S(1)}, bf16[384,4096]{1,0:T(8,128)(2,1)S(1)}, u32[]{:S(2)}, u32[]{:S(2)}) collective-permute-start(bf16[384,4096]{1,0:T(8,128)(2,1)S(1)} %add_convert_fusion.2), channel_id=1, source_target_pairs={{0,8},{4,12},{8,0},{12,4},{16,24},{20,28},{24,16},{28,20},{1,9},{5... | collective-permute-start | bytes 9437192 | tf_op jit(solution)/shard_map/ppermute | solution.py:192
  (245 other events, 3282.6 us)

commit v2 on v1

--- a/solution.py
+++ b/solution.py
@@ -61,34 +61,6 @@
 
 def two_heads(ref, g):
     return jnp.concatenate([lanes(ref, GROUP * g + i) for i in range(GROUP)], axis=0)
-
-
-def attend_body(chunks, place_ref, q_ref, *refs):
-    k_refs, v_refs = refs[:chunks], refs[chunks : 2 * chunks]
-    o_ref, lse_ref = refs[2 * chunks :]
-    tokens = q_ref.shape[0]
-    place = place_ref[0]
-    mask = chunk_mask(tokens)
-    lse_ref[...] = jnp.zeros_like(lse_ref)
-    for g in range(KV_STEP):
-        q = two_heads(q_ref, g)
-        scores = head_scores(place, q, [lanes(k, g) for k in k_refs], mask)
-        top = functools.reduce(
-            jnp.maximum, [jnp.max(s, axis=1, keepdims=True) for s in scores]
-        )
-        weights = [jnp.exp(s - top) for s in scores]
-        total = sum(jnp.sum(w, axis=1, keepdims=True) for w in weights)
-        inverse = 1.0 / total
-        out = sum(
-            nn((w * inverse).astype(BF), lanes(v, g)) for w, v in zip(weights, v_refs)
-        )
-        lse = top + jnp.log(total)
-        for i in range(GROUP):
-            h = GROUP * g + i
-            o_ref[:, h * HEAD_DIM : (h + 1) * HEAD_DIM] = out[
-                i * tokens : (i + 1) * tokens
-            ].astype(BF)
-            lse_ref[0, :, h : h + 1] = lse[i * tokens : (i + 1) * tokens]
 
 
 def attend_back_body(chunks, place_ref, q_ref, do_ref, lse_ref, *refs):
@@ -134,38 +106,16 @@
     steps = KV_HEADS // KV_STEP
     q_spec = pl.BlockSpec((tokens, q_width), lambda i, s: (0, i))
     k_spec = pl.BlockSpec((tokens, k_width), lambda i, s: (0, i))
-    v_spec = pl.BlockSpec((tokens, k_width), lambda i, s: (0, i + steps))
+
+    def kv_spec(r, at):
+        return pl.BlockSpec((None, tokens, k_width), lambda i, s: (r, 0, i + at))
     lse_spec = pl.BlockSpec((1, tokens, 128), lambda i, s: (i, 0, 0))
-    return steps, q_spec, k_spec, v_spec, lse_spec
-
-
-def attend(place, q, kvs):
-    chunks, tokens = len(kvs), q.shape[0]
-    steps, q_spec, k_spec, v_spec, lse_spec = attention_specs(tokens)
-    span = chunks * tokens
-    flops = 4 * HEADS * HEAD_DIM * tokens * span
-    return pl.pallas_call(
-        functools.partial(attend_body, chunks),
-        grid_spec=pltpu.PrefetchScalarGridSpec(
-            num_scalar_prefetch=1,
-            grid=(steps,),
-            in_specs=[q_spec] + [k_spec] * chunks + [v_spec] * chunks,
-            out_specs=[q_spec, lse_spec],
-        ),
-        out_shape=[
-            jax.ShapeDtypeStruct(q.shape, BF),
-            jax.ShapeDtypeStruct((steps, tokens, 128), F32),
-        ],
-        cost_estimate=pl.CostEstimate(
-            flops=flops, bytes_accessed=8 * q.size, transcendentals=HEADS * tokens * span
-        ),
-        name="attend",
-    )(place, q, *kvs, *kvs)
+    return steps, q_spec, k_spec, kv_spec, lse_spec
 
 
 def attend_back(place, q, do, lse, kvs):
-    chunks, tokens = len(kvs), q.shape[0]
-    steps, q_spec, k_spec, v_spec, lse_spec = attention_specs(tokens)
+    chunks, tokens = kvs.shape[0], q.shape[0]
+    steps, q_spec, k_spec, kv_spec, lse_spec = attention_specs(tokens)
     span = chunks * tokens
     kvd = KV_HEADS * HEAD_DIM
     flops = 10 * HEADS * HEAD_DIM * tokens * span
@@ -174,7 +124,9 @@
         grid_spec=pltpu.PrefetchScalarGridSpec(
             num_scalar_prefetch=1,
             grid=(steps,),
-            in_specs=[q_spec, q_spec, lse_spec] + [k_spec] * chunks + [v_spec] * chunks,
+            in_specs=[q_spec, q_spec, lse_spec]
+            + [kv_spec(r, 0) for r in range(chunks)]
+            + [kv_spec(r, steps) for r in range(chunks)],
             out_specs=[q_spec] + [k_spec] * (2 * chunks),
         ),
         out_shape=[jax.ShapeDtypeStruct(q.shape, BF)]
@@ -183,24 +135,393 @@
             flops=flops, bytes_accessed=16 * q.size, transcendentals=HEADS * tokens * span
         ),
         name="attend_back",
-    )(place, q, do, lse, *kvs, *kvs)
+    )(place, q, do, lse, *[kvs] * (2 * chunks))
     return outs[0], outs[1 : chunks + 1], outs[chunks + 1 :]
+
+
+MESH = pl.DeviceIdType.MESH
+TILE = 4 * HEAD_DIM
+
+
+class Gather:
+    def __init__(self, me, place, bits, src, out, send, recv):
+        self.me, self.bits, self.src, self.out = me, bits, src, out
+        self.send, self.recv = send, recv
+        self.rows = src.shape[0]
+        self.quarter = -(-self.rows // 64) * 16
+        self.most = self.rows - self.quarter
+        units, parts = self.most // 16, len(bits)
+        self.size = [16 * (units // parts + (i < units % parts)) for i in range(parts)]
+        self.start = [sum(self.size[:i]) for i in range(parts)]
+        self.odd = place % 2
+        self.pair = place + 1 - 2 * self.odd
+        self.count = 0
+        self.waits = []
+        own = {}
+        for bit in bits:
+            own[bit] = self.copy(self.src, 0, 1, self.most, bit, self.odd * self.quarter)
+        self.own = own
+        self.own_core = self.copy(self.src, 0, 0, self.rows, 1, 0)
+        self.forwards = []
+        self.arrival = {}
+        for bit in bits:
+            for i in range(len(bits)):
+                self.arrival[(bit, i)] = own[bit]
+        for step in range(1, len(bits)):
+            for i in range(len(bits)):
+                order = bits[i:] + bits[:i]
+                bit = order[step]
+                held = [0]
+                for b in order[:step]:
+                    held = held + [m | b for m in held]
+                for m in held[1:]:
+                    start = self.odd * self.quarter + self.start[i]
+                    made = self.copy(out, m, 1, self.size[i], bit, start)
+                    self.forwards.append((m, i, made))
+                    self.arrival[(m | bit, i)] = made
+        masks = list(range(2, 2 * max(bits), 2))
+        self.masks = masks
+        self.across = [
+            self.copy(out, m, 2, self.quarter, 0, self.odd * self.most) for m in masks
+        ]
+        self.core = [self.copy(out, m, 1, self.rows, 1, 0) for m in masks]
+        self.seen = set()
+
+    def copy(self, ref, m, kind, rows, bit, start):
+        at = (self.me ^ m) * self.rows + start
+        source = ref.at[pl.ds(pl.multiple_of(start, 16), rows)] if ref is self.src else ref.at[pl.ds(pl.multiple_of(at, 16), rows)]
+        target = {"seq": self.pair} if kind == 2 else {"dp": self.me ^ bit}
+        index = self.count
+        self.count += 1
+        return pltpu.make_async_remote_copy(
+            src_ref=source,
+            dst_ref=self.out.at[pl.ds(pl.multiple_of(at, 16), rows)],
+            send_sem=self.send.at[index],
+            recv_sem=self.recv.at[index],
+            device_id=target,
+            device_id_type=MESH,
+        )
+
+    def begin(self):
+        for bit in self.bits:
+            self.own[bit].start()
+        self.own_core.start()
+
+    def arrived(self, copy):
+        if id(copy) not in self.seen:
+            self.seen.add(id(copy))
+            copy.wait_recv()
+
+    def forward(self):
+        for m, i, made in self.forwards:
+            self.arrived(self.arrival[(m, i)])
+            made.start()
+
+    def cross(self):
+        for m, made in zip(self.masks, self.across):
+            for i in range(len(self.bits)):
+                self.arrived(self.arrival[(m, i)])
+            made.start()
+
+    def share(self):
+        for across, made in zip(self.across, self.core):
+            across.wait_recv()
+            made.start()
+
+    def finish(self):
+        self.own_core.wait_recv()
+        for made in self.core:
+            made.wait_recv()
+
+    def drain(self):
+        for made in list(self.own.values()) + [self.own_core] + [f[2] for f in self.forwards] + self.across + self.core:
+            made.wait_send()
+
+
+def gather_copies(chip_bits):
+    forwards = sum(chip_bits * (2**step - 1) for step in range(1, chip_bits))
+    return chip_bits + 1 + forwards + 2 * (2**chip_bits - 1)
+
+
+def forward_body(dp, seq, x_ref, gain_ref, cos_ref, first_ref, second_ref, *refs):
+    w_in, refs = refs[:7], refs[7:]
+    w_out, refs = refs[:7], refs[7:]
+    q_ref, o_ref, lse_ref, n1_ref, gains_ref, kvs_ref = refs[:6]
+    stage, refs = refs[6:13], refs[13:]
+    wq, wk, wv, kvbuf, gbuf, qh, kh, vh, oh, send, recv, kv_send, kv_recv, g_send, g_recv, own_sem, load_sem, kv_out = refs
+    me, place = lax.axis_index("dp"), lax.axis_index("seq")
+    bits = [1 << i for i in range(1, dp.bit_length() - 1)]
+    tokens, model = x_ref.shape
+    block = model // dp
+
+    for i in range(7):
+        pltpu.make_async_copy(w_in[i], stage[i], own_sem.at[i]).start()
+    for r in range(1, seq):
+        kvbuf[r] = jnp.zeros_like(kvbuf[r])
+
+    barrier = pltpu.get_barrier_semaphore()
+    for off in range(1, dp):
+        pl.semaphore_signal(barrier, inc=1, device_id={"dp": me ^ off}, device_id_type=MESH)
+    up, down = place + 1, place - 1
+    odd = place % 2
+    pair = place + 1 - 2 * odd
+    other = place - 1 + 2 * odd
+    has_other = (other >= 0) & (other < seq)
+    pl.semaphore_signal(barrier, inc=1, device_id={"seq": pair}, device_id_type=MESH)
+
+    @pl.when(has_other)
+    def _():
+        pl.semaphore_signal(barrier, inc=1, device_id={"seq": other}, device_id_type=MESH)
+
+        pl.semaphore_wait(barrier, dp + 1)
+
+    @pl.when(jnp.logical_not(has_other))
+    def _():
+        pl.semaphore_wait(barrier, dp)
+
+    gains = [
+        pltpu.make_async_remote_copy(
+            src_ref=gain_ref,
+            dst_ref=gbuf.at[me],
+            send_sem=g_send.at[off],
+            recv_sem=g_recv.at[off],
+            device_id={"dp": me ^ off},
+            device_id_type=MESH,
+        )
+        for off in range(1, dp)
+    ]
+    for g in gains:
+        g.start()
+    turned = bits[1:] + bits[:1]
+    jobs = [
+        Gather(me, place, turned if i in (1, 2, 5) else bits, w_in[i], w_out[i], send.at[i], recv.at[i])
+        for i in range(7)
+    ]
+    first = jobs[:3]
+    job_o, job_g, job_u, job_d = jobs[3:]
+    for job in first:
+        job.begin()
+
+    def own_out(i):
+        rows = w_in[i].shape[0]
+        return pltpu.make_async_copy(stage[i], w_out[i].at[pl.ds(pl.multiple_of(me * rows, 8), rows)], own_sem.at[i])
+
+    for i in range(7):
+        pltpu.make_async_copy(w_in[i], stage[i], own_sem.at[i]).wait()
+        own_out(i).start()
+
+    gbuf[me] = gain_ref[...]
+    x = x_ref[...].astype(F32)
+    scale = lax.rsqrt(jnp.mean(x * x, axis=1, keepdims=True) + EPS)
+    for g in gains:
+        g.wait_recv()
+    for k in range(dp):
+        gains_ref[:, k * block : (k + 1) * block] = gbuf[k, :, :block]
+    n1_ref[...] = (x * scale * gains_ref[0:1, :]).astype(BF)
+
+    for job in first:
+        job.forward()
+    job_o.begin()
+    job_g.begin()
+    for job in first:
+        job.cross()
+    for job in first:
+        job.share()
+    for i in range(7):
+        own_out(i).wait()
+    for job in first:
+        job.finish()
+    loads = [
+        pltpu.make_async_copy(w_out[i], ref, load_sem.at[i]) for i, ref in enumerate((wq, wk, wv))
+    ]
+    for load in loads:
+        load.start()
+
+    def turn(value):
+        ahead = pltpu.roll(value, TILE - HEAD_DIM // 2, 1)
+        behind = pltpu.roll(value, HEAD_DIM // 2, 1)
+        return value * cos_ref[...] + behind * second_ref[...] - ahead * first_ref[...]
+
+    kvd = wk.shape[1]
+    loads[1].wait()
+
+    @pl.loop(0, kvd // TILE)
+    def _(t):
+        at = pl.multiple_of(t * TILE, 128)
+        kvbuf[0, :, pl.ds(at, TILE)] = turn(nn(n1_ref[...], wk[:, pl.ds(at, TILE)])).astype(BF)
+
+    loads[2].wait()
+
+    @pl.loop(0, kvd // TILE)
+    def _(t):
+        at = pl.multiple_of(t * TILE, 128)
+        kvbuf[0, :, pl.ds(kvd + at, TILE)] = nn(n1_ref[...], wv[:, pl.ds(at, TILE)]).astype(BF)
+
+    def kv_copy(r):
+        return pltpu.make_async_remote_copy(
+            src_ref=kvbuf.at[r],
+            dst_ref=kvbuf.at[r + 1],
+            send_sem=kv_send.at[r],
+            recv_sem=kv_recv.at[r],
+            device_id={"seq": up},
+            device_id_type=MESH,
+        )
+
+    def kv_send_on(r):
+        @pl.when((place >= r) & (place < seq - 1))
+        def _():
+            kv_copy(r).start()
+
+    def kv_wait(r):
+        @pl.when(place >= r)
+        def _():
+            pltpu.make_async_remote_copy(
+                src_ref=kvbuf.at[r - 1],
+                dst_ref=kvbuf.at[r],
+                send_sem=kv_send.at[r - 1],
+                recv_sem=kv_recv.at[r - 1],
+                device_id={"seq": down},
+                device_id_type=MESH,
+            ).wait_recv()
+
+    kv_send_on(0)
+    loads[0].wait()
+
+    @pl.loop(0, model // TILE)
+    def _(t):
+        at = pl.multiple_of(t * TILE, 128)
+        q_ref[:, pl.ds(at, TILE)] = turn(nn(n1_ref[...], wq[:, pl.ds(at, TILE)])).astype(BF)
+
+    for h in range(HEADS):
+        qh[h] = lanes(q_ref, h)
+
+    def split_heads(r):
+        for g in range(KV_HEADS):
+            kh[g, r * tokens : (r + 1) * tokens, :] = kvbuf[r, :, g * HEAD_DIM : (g + 1) * HEAD_DIM]
+            vh[g, r * tokens : (r + 1) * tokens, :] = kvbuf[r, :, kvd + g * HEAD_DIM : kvd + (g + 1) * HEAD_DIM]
+
+    job_o.forward()
+    job_u.begin()
+    split_heads(0)
+    for r in range(1, seq):
+        kv_wait(r)
+        if r < seq - 1:
+            kv_send_on(r)
+        if r == 1:
+            job_o.cross()
+            job_g.forward()
+            job_d.begin()
+            job_o.share()
+        split_heads(r)
+    job_g.cross()
+
+    row = lax.broadcasted_iota(jnp.int32, (tokens, tokens), 0)
+    col = lax.broadcasted_iota(jnp.int32, (tokens, tokens), 1)
+    lse_ref[...] = jnp.zeros_like(lse_ref)
+    lane = lax.broadcasted_iota(jnp.int32, (tokens, 128), 1)
+
+    half = HEADS // 2
+
+    def attend_heads(start, stop):
+        @pl.loop(start, stop)
+        def _(h):
+            g = h // GROUP
+            q = qh[h]
+            scores = []
+            for r in range(seq):
+                s = nt(q, kh[g, r * tokens : (r + 1) * tokens, :]) * SCALE
+                scores.append(jnp.where(col <= row if r == 0 else place >= r, s, NEG))
+            top = functools.reduce(jnp.maximum, [jnp.max(s, axis=1, keepdims=True) for s in scores])
+            weights = [jnp.exp(s - top) for s in scores]
+            total = sum(jnp.sum(w, axis=1, keepdims=True) for w in weights)
+            inverse = 1.0 / total
+            oh[h] = sum(
+                nn((w * inverse).astype(BF), vh[g, r * tokens : (r + 1) * tokens, :])
+                for r, w in enumerate(weights)
+            ).astype(BF)
+            lse_ref[h // half] += jnp.where(lane == h % half, top + jnp.log(total), 0.0)
+
+    attend_heads(0, half)
+    job_g.share()
+    job_u.forward()
+    attend_heads(half, HEADS)
+    for h in range(HEADS):
+        o_ref[:, h * HEAD_DIM : (h + 1) * HEAD_DIM] = oh[h]
+    job_u.cross()
+    job_d.forward()
+    job_u.share()
+    job_d.cross()
+    job_d.share()
+    kv_save = pltpu.make_async_copy(kvbuf, kvs_ref, kv_out)
+    kv_save.start()
+    for job in (job_o, job_g, job_u, job_d):
+        job.finish()
+    for r in range(seq - 1):
+
+        @pl.when((place >= r) & (place < seq - 1))
+        def _():
+            kv_copy(r).wait_send()
+
+    for g in gains:
+        g.wait_send()
+    for job in jobs:
+        job.drain()
+    kv_save.wait()
+
+
+def forward_call(dp, seq, x, gains, tables, weights):
+    tokens, model = x.shape
+    chip_bits = dp.bit_length() - 2
+    copies = gather_copies(chip_bits)
+    anyspec = pl.BlockSpec(memory_space=pl.ANY)
+    vmem = pl.BlockSpec(memory_space=pltpu.VMEM)
+    out_shape = [jax.ShapeDtypeStruct((dp * w.shape[0], w.shape[1]), BF) for w in weights]
+    out_shape += [
+        jax.ShapeDtypeStruct((tokens, model), BF),
+        jax.ShapeDtypeStruct((tokens, model), BF),
+        jax.ShapeDtypeStruct((2, tokens, 128), F32),
+        jax.ShapeDtypeStruct((tokens, model), BF),
+        jax.ShapeDtypeStruct((8, model), F32),
+        jax.ShapeDtypeStruct((seq, tokens, model), BF),
+    ]
+    kvd = weights[1].shape[1]
+    dma = pltpu.SemaphoreType.DMA
+    return pl.pallas_call(
+        functools.partial(forward_body, dp, seq),
+        out_shape=out_shape,
+        in_specs=[vmem] * 5 + [anyspec] * 7,
+        out_specs=[anyspec] * 7 + [vmem] * 5 + [anyspec],
+        scratch_shapes=[pltpu.VMEM(w.shape, BF) for w in weights]
+        + [
+            pltpu.VMEM((model, model), BF),
+            pltpu.VMEM((model, kvd), BF),
+            pltpu.VMEM((model, kvd), BF),
+            pltpu.VMEM((seq, tokens, model), BF),
+            pltpu.VMEM((dp, 8, 256), F32),
+            pltpu.VMEM((HEADS, tokens, HEAD_DIM), BF),
+            pltpu.VMEM((KV_HEADS, seq * tokens, HEAD_DIM), BF),
+            pltpu.VMEM((KV_HEADS, seq * tokens, HEAD_DIM), BF),
+            pltpu.VMEM((HEADS, tokens, HEAD_DIM), BF),
+            dma((7, copies)),
+            dma((7, copies)),
+            dma((seq,)),
+            dma((seq,)),
+            dma((dp,)),
+            dma((dp,)),
+            dma((7,)),
+            dma((3,)),
+            dma(()),
+        ],
+        compiler_params=pltpu.CompilerParams(
+            collective_id=0, has_side_effects=True, vmem_limit_bytes=60 * 1024 * 1024
+        ),
+        name="forward",
+    )(x, gains, *tables, *weights)
 
 
 def flip(value, axis, bit):
     size = lax.axis_size(axis)
     return lax.ppermute(value, axis, [(i, i ^ bit) for i in range(size)])
-
-
-def gather_rows(shard, bits, me, parts):
-    pieces = {0: shard}
-    for bit in list(bits) + [1]:
-        pieces.update({off ^ bit: flip(piece, "dp", bit) for off, piece in list(pieces.items())})
-    rows = shard.shape[0]
-    whole = jnp.zeros((parts * rows, shard.shape[1]), shard.dtype)
-    for off, piece in pieces.items():
-        whole = lax.dynamic_update_slice(whole, piece, ((me ^ off) * rows, 0))
-    return whole
 
 
 def xor_order(bits):
@@ -308,26 +629,7 @@
     kvd = w_key.shape[-1]
     place_arr = place.reshape(1).astype(jnp.int32)
 
-    gains = {0: jnp.concatenate([gain_attn, gain_mlp], axis=0)}
-    for bit in [1] + bits:
-        gains.update({off ^ bit: flip(g, "dp", bit) for off, g in list(gains.items())})
-    stacked = jnp.stack([gains[off] for off in range(dp)]).astype(F32)
-    owner = (jnp.arange(dp)[:, None] ^ me) == jnp.arange(dp)[None, :]
-    natural = jnp.sum(jnp.where(owner[:, :, None, None], stacked[None], 0.0), axis=1)
-    natural = natural.transpose(1, 0, 2).reshape(2, 1, model)
-    gain_one, gain_two = natural[0], natural[1]
-
-    gather = functools.partial(gather_rows, me=me, parts=dp)
-    w_q = gather(w_query[0], bits)
-    w_k = gather(w_key[0], turned)
-    w_v = gather(w_value[0], turned)
-    w_o = gather(w_out[0], bits)
-    w_g = gather(w_gate[0], bits)
-    w_u = gather(w_up[0], turned)
     half_model = model // 2
-    w_d = jnp.concatenate(
-        [gather(w_down[0][:, :half_model], bits), gather(w_down[0][:, half_model:], turned)], axis=1
-    )
 
     def xor_columns(value, way):
         width = value.shape[1] // dp
@@ -336,17 +638,15 @@
 
     tables = rope_tables(place, rows, model)
     x = tokens[0].astype(F32)
+    packed = jnp.zeros((8, 256), F32)
+    packed = packed.at[0, : gain_attn.shape[1]].set(gain_attn[0].astype(F32))
+    packed = packed.at[1, : gain_mlp.shape[1]].set(gain_mlp[0].astype(F32))
+    shards = [w[0] for w in (w_query, w_key, w_value, w_out, w_gate, w_up, w_down)]
+    outs = forward_call(dp, seq, tokens[0], packed, [t[:, :TILE] for t in tables], shards)
+    w_q, w_k, w_v, w_o, w_g, w_u, w_d = outs[:7]
+    q, mixed, lse, n1, gains, kvs = outs[7:]
+    gain_one, gain_two = gains[0:1], gains[1:2]
     scale_one = norm_scale(x)
-    n1 = (x * scale_one * gain_one).astype(BF)
-    q = rotate(nn(n1, w_q), tables, 1.0).astype(BF)
-    kv = jnp.concatenate(
-        [rotate(nn(n1, w_k), tables, 1.0).astype(BF), nn(n1, w_v).astype(BF)], axis=1
-    )
-    kvs = [kv]
-    for far in range(1, seq):
-        pairs = [(i, i + 1) for i in range(far - 1, seq - 1)]
-        kvs.append(lax.ppermute(kvs[-1], "seq", pairs))
-    mixed, lse = attend(place_arr, q, kvs)
     x2 = x + nn(mixed, w_o)
     scale_two = norm_scale(x2)
     n2 = (x2 * scale_two * gain_two).astype(BF)

time: 994 us -> 816 us (0.82)
  waiting for transfers between devices: 421 us -> 199 us
  Pallas kernels: 38.2 us -> 215 us
  local copies, waits for them, and re-layouts: 128 us -> 40.1 us
  starting transfers between devices: 245 us -> 214 us
    ppermute x92 -> x29, waiting for transfers between devices: 308 us -> 80.6 us  [flip(): return lax.ppermute(value, axis, [(i, i ^ bit) for i in range(size)])]
    pallas_call x1, Pallas kernels: 18.4 us -> 195 us  [forward_call(): pl.pallas_call(functools.partial(forward_body, dp, seq), out_shape=out_sh...]
    dynamic_update_slice x63 -> x0, local copies, waits for them, and re-layouts: 63 us -> none  [gather_rows(): whole = lax.dynamic_update_slice(whole, piece, ((me ^ off) * rows, 0))]
    ppermute x92 -> x29, starting transfers between devices: 66.2 us -> 27.6 us  [flip(): return lax.ppermute(value, axis, [(i, i ^ bit) for i in range(size)])]
    another operation x22 -> x5, local copies, waits for them, and re-layouts: 22.8 us -> 1.01 us
    ppermute x36, starting transfers between devices: 106 us -> 118 us  [line_sum(): held = lax.ppermute(mine, 'seq', pairs)]
    dot_general x38 -> x35, matrix products: 111 us -> 108 us  [dot(): return lax.dot_general(a, b, (dims, ((), ())), preferred_element_type=F32)]
  transfers between devices with their start and end apart: 170 -> 104, of which waited for: 67 -> 47; matrix products, arithmetic and copies ran while one was open for 21% -> 12% of each run, Pallas kernels for 2% -> 0%
where the time goes in v2:
time: 816 us; the launch traced here: 811 us
  Pallas kernels  215 us (26%)
  starting transfers between devices  214 us (26%)
  waiting for transfers between devices  199 us (24%)
  matrix products  108 us (13%)
  local copies, waits for them, and re-layouts  40.1 us (5%)
  other arithmetic  30.5 us (4%)
    pallas_call x1, Pallas kernels, forward_call(): pl.pallas_call(functools.partial(forward_body, dp, seq), out_shape=out_sh...  195 us
    ppermute x36, starting transfers between devices, line_sum(): held = lax.ppermute(mine, 'seq', pairs)  118 us
    dot_general x35, matrix products, dot(): return lax.dot_general(a, b, (dims, ((), ())), preferred_element_type=F32)  108 us
    ppermute x29, waiting for transfers between devices, flip(): return lax.ppermute(value, axis, [(i, i ^ bit) for i in range(size)])  80.6 us
    ppermute x36, waiting for transfers between devices, line_sum(): held = lax.ppermute(held, 'seq', pairs)  69.1 us
    ppermute x36, starting transfers between devices, line_sum(): held = lax.ppermute(held, 'seq', pairs)  64.3 us
    ppermute x36, waiting for transfers between devices, line_sum(): held = lax.ppermute(mine, 'seq', pairs)  42.1 us
    ppermute x29, starting transfers between devices, flip(): return lax.ppermute(value, axis, [(i, i ^ bit) for i in range(size)])  27.6 us
  transfers between devices with their start and end apart: 104, of which 47 were waited for; matrix products, arithmetic and copies ran while one was open for 12% of the time, Pallas kernels for 0%

profile of v2, /device:TPU:0, one launch (start us, length us, event | category | flops | bytes accessed | tf_op | source)
XLA Modules:
  0.0 810.6 jit_solution(10643982162973726593)
XLA Ops:
  11.4 195.4 %forward.1 = (bf16[1536,1536]{1,0:T(8,128)(2,1)}, bf16[1536,768]{1,0:T(8,128)(2,1)}, bf16[1536,768]{1,0:T(8,128)(2,1)}, bf16[1536,1536]{1,0:T(8,128)(2,1)}, bf16...) custom-call(bf16[256,1536]{1,0:T(8,128)(2,1)} %bitcast.86, ...), custom_call_target="tpu_custom_call" | custom-call | tf_op jit(solution)/shard_map/forward/pallas_call | solution.py:489
  212.7 10.4 %fusion.146 = f32[256,4096]{1,0:T(8,128)} fusion(bf16[256,1536]{1,0:T(8,128)(2,1)S(1)} %multiply_convert_fusion.3, bf16[1536,4096]{1,0:T(8,128)(2,1)} %get-tuple-element.61), kind=kOutput, calls=%fused_computation.404 | convolution fusion | flops 3221225472 | bytes 17563648 | tf_op jit(solution)/shard_map/dot_general | solution.py:24
  223.1 10.2 %fusion.145 = f32[256,4096]{1,0:T(8,128)} fusion(bf16[256,1536]{1,0:T(8,128)(2,1)S(1)} %multiply_convert_fusion.3, bf16[1536,4096]{1,0:T(8,128)(2,1)} %get-tuple-element.60), kind=kOutput, calls=%fused_computation.403 | convolution fusion | flops 3221225472 | bytes 17563648 | tf_op jit(solution)/shard_map/dot_general | solution.py:24
  233.3 8.5 %multiply_convert_fusion = (bf16[256,4096]{1,0:T(8,128)(2,1)S(1)}, bf16[256,4096]{1,0:T(8,128)(2,1)S(1)}, bf16[256,4096]{1,0:T(8,128)(2,1)}) fusion(f32[256,4096]{1,0:T(8,128)} %fusion.145, f32[256,4096]{1,0:T(8,128)} %fusion.146, bf16[4096,1536]{1,0:T(8,128)(2,1)S(1)} %bitcast.106, bf16[1,256,1536]{2,1,0:T(8,128)(2,1)S(1)} %copy-done.32), kind=kOutput, calls=%fused_computation.7 | convolution fusion | flops 3238002688 | bytes 28049408 | tf_op jit(solution)/shard_map/dot_general | solution.py:24
  241.8 7.2 fusion.147
  249.0 7.5 multiply_reduce_fusion
  262.6 19.8 %attend_back.1 = (bf16[256,1536]{1,0:T(8,128)(2,1)}, bf16[256,768]{1,0:T(8,128)(2,1)}, bf16[256,768]{1,0:T(8,128)(2,1)}, bf16[256,768]{1,0:T(8,128)(2,1)}, bf16[...) custom-call(s32[1]{0:T(128)} %bitcast.14.place_ref, ...), custom_call_target="tpu_custom_call" | custom-call | flops 4026531840 | bytes 6291456 | tf_op jit(solution)/shard_map/attend_back/pallas_call | solution.py:122
  303.7 8.3 %fusion = f32[1,256,1536]{2,1,0:T(8,128)} fusion(f32[256,1536]{1,0:T(8,128)S(1)} %copy-done.9, bf16[256,4096]{1,0:T(8,128)(2,1)S(1)} %copy-done.37, bf16[4096,1536]{1,0:T(8,128)(2,1)} %get-tuple-element.62), kind=kOutput, calls=%fused_computation.44 | convolution fusion | flops 3221618688 | bytes 17825792 | tf_op jit(solution)/shard_map/dot_general | solution.py:24
  313.8 5.1 fusion.148
  341.1 9.1 %collective-permute-done.37 = bf16[384,768]{1,0:T(8,128)(2,1)S(1)} collective-permute-done((bf16[384,768]{1,0:T(8,128)(2,1)S(1)}, bf16[384,768]{1,0:T(8,128)(2,1)S(1)}, u32[]{:S(2)}, u32[]{:S(2)}) %collective-permute-start.37) | collective-permute-done | bytes 589856 | tf_op jit(solution)/shard_map/ppermute | solution.py:524
  361.7 16.1 %collective-permute-start.39 = (bf16[48,1536]{1,0:T(8,128)(2,1)S(1)}, bf16[48,1536]{1,0:T(8,128)(2,1)S(1)}, u32[]{:S(2)}, u32[]{:S(2)}) collective-permute-start(bf16[48,1536]{1,0:T(8,128)(2,1)S(1)} %get-tuple-element.184), channel_id=1, source_target_pairs={{0,1},{4,5},{8,9},{12,13},{16,17},{20,21},{24,25},{28,29}} | collective-permute-start | bytes 442376 | tf_op jit(solution)/shard_map/ppermute | solution.py:566
  385.4 7.6 collective-permute-done.2
  401.7 11.8 %collective-permute-start.41 = (bf16[48,1536]{1,0:T(8,128)(2,1)S(1)}, bf16[48,1536]{1,0:T(8,128)(2,1)S(1)}, u32[]{:S(2)}, u32[]{:S(2)}) collective-permute-start(bf16[48,1536]{1,0:T(8,128)(2,1)S(1)} %get-tuple-element.180), channel_id=1, source_target_pairs={{0,1},{1,2},{2,3},{4,5},{5,6},{6,7},{8,9},{9,10},{10,11},{12,13},{... | collective-permute-start | bytes 442376 | tf_op jit(solution)/shard_map/ppermute | solution.py:566
  446.1 5.3 collective-permute-done.49
  459.7 9.1 %collective-permute-done.5 = bf16[192,1536]{1,0:T(8,128)(2,1)S(1)} collective-permute-done((bf16[192,1536]{1,0:T(8,128)(2,1)S(1)}, bf16[192,1536]{1,0:T(8,128)(2,1)S(1)}, u32[]{:S(2)}, u32[]{:S(2)}) %collective-permute-start.5) | collective-permute-done | bytes 589856 | tf_op jit(solution)/shard_map/ppermute | solution.py:524
  488.1 7.2 collective-permute-start.8
  522.8 7.4 collective-permute-done.16
  534.7 5.6 collective-permute-done.83
  541.0 5.8 collective-permute-start.87
  553.1 5.1 collective-permute-start.88
  569.0 8.3 %collective-permute-done.20 = bf16[192,1536]{1,0:T(8,128)(2,1)S(1)} collective-permute-done((bf16[192,1536]{1,0:T(8,128)(2,1)S(1)}, bf16[192,1536]{1,0:T(8,128)(2,1)S(1)}, u32[]{:S(2)}, u32[]{:S(2)}) %collective-permute-start.20) | collective-permute-done | bytes 589856 | tf_op jit(solution)/shard_map/ppermute | solution.py:524
  577.6 5.8 collective-permute-start.21
  595.3 5.0 collective-permute-start.89
  601.6 5.2 collective-permute-start.23
  633.1 14.6 %collective-permute-done.31 = bf16[48,1536]{1,0:T(8,128)(2,1)S(1)} collective-permute-done((bf16[48,1536]{1,0:T(8,128)(2,1)S(1)}, bf16[48,1536]{1,0:T(8,128)(2,1)S(1)}, u32[]{:S(2)}, u32[]{:S(2)}) %collective-permute-start.31) | collective-permute-done | bytes 147488 | tf_op jit(solution)/shard_map/ppermute | solution.py:577
  671.0 20.7 %collective-permute-done.68 = bf16[192,4096]{1,0:T(8,128)(2,1)} collective-permute-done((bf16[192,4096]{1,0:T(8,128)(2,1)}, bf16[192,4096]{1,0:T(8,128)(2,1)}, u32[]{:S(2)}, u32[]{:S(2)}) %collective-permute-start.68) | collective-permute-done | bytes 1572896 | tf_op jit(solution)/shard_map/ppermute | solution.py:524
  741.4 7.8 collective-permute-done.74
  749.7 10.3 %collective-permute-start.75 = (bf16[48,4096]{1,0:T(8,128)(2,1)S(1)}, bf16[48,4096]{1,0:T(8,128)(2,1)S(1)}, u32[]{:S(2)}, u32[]{:S(2)}) collective-permute-start(bf16[48,4096]{1,0:T(8,128)(2,1)S(1)} %get-tuple-element.110), channel_id=1, source_target_pairs={{0,1},{1,2},{2,3},{4,5},{5,6},{6,7},{8,9},{9,10},{10,11},{12,13},{... | collective-permute-start | bytes 1179656 | tf_op jit(solution)/shard_map/ppermute | solution.py:577
  761.9 6.6 collective-permute-start.60
  775.9 6.3 collective-permute-done.63
  784.3 6.3 collective-permute-done.79
  792.7 6.3 collective-permute-done.64
  (545 shorter events, 341.6 us)
Async XLA Ops:
  284.5 45.8 %collective-permute-start = (bf16[256,1536]{1,0:T(8,128)(2,1)}, bf16[256,1536]{1,0:T(8,128)(2,1)}, u32[]{:S(2)}, u32[]{:S(2)}) collective-permute-start(bf16[256,1536]{1,0:T(8,128)(2,1)} %pad_maximum_fusion.6), channel_id=1, source_target_pairs={{3,2},{7,6},{11,10},{15,14},{19,18},{23,22},{27,26},{31,30}} | collective-permute-start | bytes 2359304 | tf_op jit(solution)/shard_map/ppermute | solution.py:696
  291.4 182.0 %collective-permute-start.84 = (bf16[2048,768]{0,1:T(8,128)(2,1)}, bf16[2048,768]{0,1:T(8,128)(2,1)}, u32[]{:S(2)}, u32[]{:S(2)}) collective-permute-start(bf16[2048,768]{0,1:T(8,128)(2,1)} %convolution_convert_fusion.2), channel_id=1, source_target_pairs={{0,4},{4,0},{8,12},{12,8},{16,20},{20,16},{24,28},{28,24},{1,5},{5... | collective-permute-start | bytes 9437192 | tf_op jit(solution)/shard_map/ppermute | solution.py:524
  294.6 183.1 %collective-permute-start.81 = (bf16[2048,768]{0,1:T(8,128)(2,1)}, bf16[2048,768]{0,1:T(8,128)(2,1)}, u32[]{:S(2)}, u32[]{:S(2)}) collective-permute-start(bf16[2048,768]{0,1:T(8,128)(2,1)} %convolution_convert_fusion.3), channel_id=1, source_target_pairs={{0,4},{4,0},{8,12},{12,8},{16,20},{20,16},{24,28},{28,24},{1,5},{5... | collective-permute-start | bytes 9437192 | tf_op jit(solution)/shard_map/ppermute | solution.py:524
  299.0 33.6 %collective-permute-start.36 = (bf16[768,768]{1,0:T(8,128)(2,1)}, bf16[768,768]{1,0:T(8,128)(2,1)}, u32[]{:S(2)}, u32[]{:S(2)}) collective-permute-start(bf16[768,768]{1,0:T(8,128)(2,1)} %convolution_convert_fusion.7), channel_id=1, source_target_pairs={{0,4},{4,0},{8,12},{12,8},{16,20},{20,16},{24,28},{28,24},{1,5},{5... | collective-permute-start | bytes 3538952 | tf_op jit(solution)/shard_map/ppermute | solution.py:524
  301.2 35.0 %collective-permute-start.33 = (bf16[768,768]{1,0:T(8,128)(2,1)}, bf16[768,768]{1,0:T(8,128)(2,1)}, u32[]{:S(2)}, u32[]{:S(2)}) collective-permute-start(bf16[768,768]{1,0:T(8,128)(2,1)} %convolution_convert_fusion.8), channel_id=1, source_target_pairs={{0,4},{4,0},{8,12},{12,8},{16,20},{20,16},{24,28},{28,24},{1,5},{5... | collective-permute-start | bytes 3538952 | tf_op jit(solution)/shard_map/ppermute | solution.py:524
  331.8 22.1 %collective-permute-start.1 = (bf16[256,1536]{1,0:T(8,128)(2,1)S(1)}, bf16[256,1536]{1,0:T(8,128)(2,1)S(1)}, u32[]{:S(2)}, u32[]{:S(2)}) collective-permute-start(bf16[256,1536]{1,0:T(8,128)(2,1)S(1)} %add_convert_fusion.26), channel_id=1, source_target_pairs={{2,1},{3,2},{6,5},{7,6},{10,9},{11,10},{14,13},{15,14},{18,17},{19... | collective-permute-start | bytes 2359304 | tf_op jit(solution)/shard_map/ppermute | solution.py:696
  354.1 38.9 %collective-permute-start.2 = (bf16[256,1536]{1,0:T(8,128)(2,1)S(1)}, bf16[256,1536]{1,0:T(8,128)(2,1)S(1)}, u32[]{:S(2)}, u32[]{:S(2)}) collective-permute-start(bf16[256,1536]{1,0:T(8,128)(2,1)S(1)} %add_convert_fusion.25), channel_id=1, source_target_pairs={{1,0},{2,1},{3,2},{5,4},{6,5},{7,6},{9,8},{10,9},{11,10},{13,12},{... | collective-permute-start | bytes 2359304 | tf_op jit(solution)/shard_map/ppermute | solution.py:696
  361.7 19.2 %collective-permute-start.39 = (bf16[48,1536]{1,0:T(8,128)(2,1)S(1)}, bf16[48,1536]{1,0:T(8,128)(2,1)S(1)}, u32[]{:S(2)}, u32[]{:S(2)}) collective-permute-start(bf16[48,1536]{1,0:T(8,128)(2,1)S(1)} %get-tuple-element.184), channel_id=1, source_target_pairs={{0,1},{4,5},{8,9},{12,13},{16,17},{20,21},{24,25},{28,29}} | collective-permute-start | bytes 442376 | tf_op jit(solution)/shard_map/ppermute | solution.py:566
  380.9 37.6 %collective-permute-start.3 = (bf16[768,1536]{1,0:T(8,128)(2,1)S(1)}, bf16[768,1536]{1,0:T(8,128)(2,1)S(1)}, u32[]{:S(2)}, u32[]{:S(2)}) collective-permute-start(bf16[768,1536]{1,0:T(8,128)(2,1)S(1)} %convolution_convert_fusion.5), channel_id=1, source_target_pairs={{0,4},{4,0},{8,12},{12,8},{16,20},{20,16},{24,28},{28,24},{1,5},{5... | collective-permute-start | bytes 7077896 | tf_op jit(solution)/shard_map/ppermute | solution.py:524
  381.0 20.5 %collective-permute-start.40 = (bf16[48,1536]{1,0:T(8,128)(2,1)S(1)}, bf16[48,1536]{1,0:T(8,128)(2,1)S(1)}, u32[]{:S(2)}, u32[]{:S(2)}) collective-permute-start(bf16[48,1536]{1,0:T(8,128)(2,1)S(1)} %get-tuple-element.182), channel_id=1, source_target_pairs={{0,1},{1,2},{4,5},{5,6},{8,9},{9,10},{12,13},{13,14},{16,17},{17,1... | collective-permute-start | bytes 442376 | tf_op jit(solution)/shard_map/ppermute | solution.py:566
  401.7 31.5 %collective-permute-start.41 = (bf16[48,1536]{1,0:T(8,128)(2,1)S(1)}, bf16[48,1536]{1,0:T(8,128)(2,1)S(1)}, u32[]{:S(2)}, u32[]{:S(2)}) collective-permute-start(bf16[48,1536]{1,0:T(8,128)(2,1)S(1)} %get-tuple-element.180), channel_id=1, source_target_pairs={{0,1},{1,2},{2,3},{4,5},{5,6},{6,7},{8,9},{9,10},{10,11},{12,13},{... | collective-permute-start | bytes 442376 | tf_op jit(solution)/shard_map/ppermute | solution.py:566
  432.6 24.1 %collective-permute-start.4 = (bf16[384,1536]{1,0:T(8,128)(2,1)S(1)}, bf16[384,1536]{1,0:T(8,128)(2,1)S(1)}, u32[]{:S(2)}, u32[]{:S(2)}) collective-permute-start(bf16[384,1536]{1,0:T(8,128)(2,1)S(1)} %add_convert_fusion.16), channel_id=1, source_target_pairs={{0,8},{4,12},{8,0},{12,4},{16,24},{20,28},{24,16},{28,20},{1,9},{5... | collective-permute-start | bytes 3538952 | tf_op jit(solution)/shard_map/ppermute | solution.py:524
  451.4 113.9 %collective-permute-start.66 = (bf16[768,4096]{1,0:T(8,128)(2,1)S(1)}, bf16[768,4096]{1,0:T(8,128)(2,1)S(1)}, u32[]{:S(2)}, u32[]{:S(2)}) collective-permute-start(bf16[768,4096]{1,0:T(8,128)(2,1)S(1)} %bitcast.91), channel_id=1, source_target_pairs={{0,4},{4,0},{8,12},{12,8},{16,20},{20,16},{24,28},{28,24},{1,5},{5... | collective-permute-start | bytes 18874376 | tf_op jit(solution)/shard_map/ppermute | solution.py:524
  459.6 46.0 %collective-permute-start.18 = (bf16[768,1536]{1,0:T(8,128)(2,1)S(1)}, bf16[768,1536]{1,0:T(8,128)(2,1)S(1)}, u32[]{:S(2)}, u32[]{:S(2)}) collective-permute-start(bf16[768,1536]{1,0:T(8,128)(2,1)S(1)} %convolution_convert_fusion.4), channel_id=1, source_target_pairs={{0,4},{4,0},{8,12},{12,8},{16,20},{20,16},{24,28},{28,24},{1,5},{5... | collective-permute-start | bytes 7077896 | tf_op jit(solution)/shard_map/ppermute | solution.py:524
  475.5 35.6 %collective-permute-start.85 = (bf16[1024,768]{0,1:T(8,128)(2,1)S(1)}, bf16[1024,768]{0,1:T(8,128)(2,1)S(1)}, u32[]{:S(2)}, u32[]{:S(2)}) collective-permute-start(bf16[1024,768]{0,1:T(8,128)(2,1)S(1)} %add_convert_fusion.4), channel_id=1, source_target_pairs={{0,16},{4,20},{8,24},{12,28},{16,0},{20,4},{24,8},{28,12},{1,17},{... | collective-permute-start | bytes 4718600 | tf_op jit(solution)/shard_map/ppermute | solution.py:524
  483.2 33.0 %collective-permute-start.82 = (bf16[1024,768]{0,1:T(8,128)(2,1)S(1)}, bf16[1024,768]{0,1:T(8,128)(2,1)S(1)}, u32[]{:S(2)}, u32[]{:S(2)}) collective-permute-start(bf16[1024,768]{0,1:T(8,128)(2,1)S(1)} %add_convert_fusion.6), channel_id=1, source_target_pairs={{0,8},{4,12},{8,0},{12,4},{16,24},{20,28},{24,16},{28,20},{1,9},{5... | collective-permute-start | bytes 4718600 | tf_op jit(solution)/shard_map/ppermute | solution.py:524
  505.4 78.0 %collective-permute-start.51 = (bf16[768,4096]{1,0:T(8,128)(2,1)S(1)}, bf16[768,4096]{1,0:T(8,128)(2,1)S(1)}, u32[]{:S(2)}, u32[]{:S(2)}) collective-permute-start(bf16[768,4096]{1,0:T(8,128)(2,1)S(1)} %convolution_convert_fusion.1), channel_id=1, source_target_pairs={{0,4},{4,0},{8,12},{12,8},{16,20},{20,16},{24,28},{28,24},{1,5},{5... | collective-permute-start | bytes 18874376 | tf_op jit(solution)/shard_map/ppermute | solution.py:524
  519.9 20.5 %collective-permute-start.83 = (bf16[512,768]{0,1:T(8,128)(2,1)S(1)}, bf16[512,768]{0,1:T(8,128)(2,1)S(1)}, u32[]{:S(2)}, u32[]{:S(2)}) collective-permute-start(bf16[512,768]{0,1:T(8,128)(2,1)S(1)} %add_convert_fusion.22), channel_id=1, source_target_pairs={{0,16},{4,20},{8,24},{12,28},{16,0},{20,4},{24,8},{28,12},{1,17},{... | collective-permute-start | bytes 2359304 | tf_op jit(solution)/shard_map/ppermute | solution.py:524
  530.2 32.9 %collective-permute-start.19 = (bf16[384,1536]{1,0:T(8,128)(2,1)S(1)}, bf16[384,1536]{1,0:T(8,128)(2,1)S(1)}, u32[]{:S(2)}, u32[]{:S(2)}) collective-permute-start(bf16[384,1536]{1,0:T(8,128)(2,1)S(1)} %add_convert_fusion.14), channel_id=1, source_target_pairs={{0,16},{4,20},{8,24},{12,28},{16,0},{20,4},{24,8},{28,12},{1,17},{... | collective-permute-start | bytes 3538952 | tf_op jit(solution)/shard_map/ppermute | solution.py:524
  553.1 40.8 %collective-permute-start.88 = (bf16[128,1536]{0,1:T(8,128)(2,1)}, bf16[128,1536]{0,1:T(8,128)(2,1)}, u32[]{:S(2)}, u32[]{:S(2)}) collective-permute-start(bf16[128,1536]{0,1:T(8,128)(2,1)} %get-tuple-element.132), channel_id=1, source_target_pairs={{0,1},{1,2},{4,5},{5,6},{8,9},{9,10},{12,13},{13,14},{16,17},{17,1... | collective-permute-start | bytes 1179656 | tf_op jit(solution)/shard_map/ppermute | solution.py:566
  558.2 35.7 %collective-permute-start.91 = (bf16[128,1536]{0,1:T(8,128)(2,1)}, bf16[128,1536]{0,1:T(8,128)(2,1)}, u32[]{:S(2)}, u32[]{:S(2)}) collective-permute-start(bf16[128,1536]{0,1:T(8,128)(2,1)} %get-tuple-element.133), channel_id=1, source_target_pairs={{2,1},{3,2},{6,5},{7,6},{10,9},{11,10},{14,13},{15,14},{18,17},{19... | collective-permute-start | bytes 1179656 | tf_op jit(solution)/shard_map/ppermute | solution.py:566
  566.4 90.6 %collective-permute-start.67 = (bf16[384,4096]{1,0:T(8,128)(2,1)S(1)}, bf16[384,4096]{1,0:T(8,128)(2,1)S(1)}, u32[]{:S(2)}, u32[]{:S(2)}) collective-permute-start(bf16[384,4096]{1,0:T(8,128)(2,1)S(1)} %add_convert_fusion), channel_id=1, source_target_pairs={{0,16},{4,20},{8,24},{12,28},{16,0},{20,4},{24,8},{28,12},{1,17},{... | collective-permute-start | bytes 9437192 | tf_op jit(solution)/shard_map/ppermute | solution.py:524
  591.6 71.0 %collective-permute-start.52 = (bf16[384,4096]{1,0:T(8,128)(2,1)S(1)}, bf16[384,4096]{1,0:T(8,128)(2,1)S(1)}, u32[]{:S(2)}, u32[]{:S(2)}) collective-permute-start(bf16[384,4096]{1,0:T(8,128)(2,1)S(1)} %add_convert_fusion.2), channel_id=1, source_target_pairs={{0,8},{4,12},{8,0},{12,4},{16,24},{20,28},{24,16},{28,20},{1,9},{5... | collective-permute-start | bytes 9437192 | tf_op jit(solution)/shard_map/ppermute | solution.py:524
  625.9 22.5 %collective-permute-start.94 = (bf16[128,1536]{0,1:T(8,128)(2,1)S(1)}, bf16[128,1536]{0,1:T(8,128)(2,1)S(1)}, u32[]{:S(2)}, u32[]{:S(2)}) collective-permute-start(bf16[128,1536]{0,1:T(8,128)(2,1)S(1)} %collective-permute-done.93), channel_id=1, source_target_pairs={{1,2},{2,3},{5,6},{6,7},{9,10},{10,11},{13,14},{14,15},{17,18},{18... | collective-permute-start | bytes 1179656 | tf_op jit(solution)/shard_map/ppermute | solution.py:577
  630.5 19.7 %collective-permute-start.97 = (bf16[128,1536]{0,1:T(8,128)(2,1)S(1)}, bf16[128,1536]{0,1:T(8,128)(2,1)S(1)}, u32[]{:S(2)}, u32[]{:S(2)}) collective-permute-start(bf16[128,1536]{0,1:T(8,128)(2,1)S(1)} %collective-permute-done.96), channel_id=1, source_target_pairs={{1,0},{2,1},{5,4},{6,5},{9,8},{10,9},{13,12},{14,13},{17,16},{18,1... | collective-permute-start | bytes 1179656 | tf_op jit(solution)/shard_map/ppermute | solution.py:577
  659.2 32.5 %collective-permute-start.68 = (bf16[192,4096]{1,0:T(8,128)(2,1)}, bf16[192,4096]{1,0:T(8,128)(2,1)}, u32[]{:S(2)}, u32[]{:S(2)}) collective-permute-start(bf16[192,4096]{1,0:T(8,128)(2,1)} %add_convert_fusion.9), channel_id=1, source_target_pairs={{0,8},{4,12},{8,0},{12,4},{16,24},{20,28},{24,16},{28,20},{1,9},{5... | collective-permute-start | bytes 4718600 | tf_op jit(solution)/shard_map/ppermute | solution.py:524
  664.8 33.7 %collective-permute-start.53 = (bf16[192,4096]{1,0:T(8,128)(2,1)}, bf16[192,4096]{1,0:T(8,128)(2,1)}, u32[]{:S(2)}, u32[]{:S(2)}) collective-permute-start(bf16[192,4096]{1,0:T(8,128)(2,1)} %add_convert_fusion.12), channel_id=1, source_target_pairs={{0,16},{4,20},{8,24},{12,28},{16,0},{20,4},{24,8},{28,12},{1,17},{... | collective-permute-start | bytes 4718600 | tf_op jit(solution)/shard_map/ppermute | solution.py:524
  697.9 22.4 %collective-permute-start.72 = (bf16[48,4096]{1,0:T(8,128)(2,1)S(1)}, bf16[48,4096]{1,0:T(8,128)(2,1)S(1)}, u32[]{:S(2)}, u32[]{:S(2)}) collective-permute-start(bf16[48,4096]{1,0:T(8,128)(2,1)S(1)} %get-tuple-element.139), channel_id=1, source_target_pairs={{3,2},{7,6},{11,10},{15,14},{19,18},{23,22},{27,26},{31,30}} | collective-permute-start | bytes 1179656 | tf_op jit(solution)/shard_map/ppermute | solution.py:566
  702.2 27.9 %collective-permute-start.57 = (bf16[48,4096]{1,0:T(8,128)(2,1)S(1)}, bf16[48,4096]{1,0:T(8,128)(2,1)S(1)}, u32[]{:S(2)}, u32[]{:S(2)}) collective-permute-start(bf16[48,4096]{1,0:T(8,128)(2,1)S(1)} %get-tuple-element.143), channel_id=1, source_target_pairs={{3,2},{7,6},{11,10},{15,14},{19,18},{23,22},{27,26},{31,30}} | collective-permute-start | bytes 1179656 | tf_op jit(solution)/shard_map/ppermute | solution.py:566
  733.5 27.9 %collective-permute-start.56 = (bf16[48,4096]{1,0:T(8,128)(2,1)S(1)}, bf16[48,4096]{1,0:T(8,128)(2,1)S(1)}, u32[]{:S(2)}, u32[]{:S(2)}) collective-permute-start(bf16[48,4096]{1,0:T(8,128)(2,1)S(1)} %get-tuple-element.140), channel_id=1, source_target_pairs={{0,1},{1,2},{2,3},{4,5},{5,6},{6,7},{8,9},{9,10},{10,11},{12,13},{... | collective-permute-start | bytes 1179656 | tf_op jit(solution)/shard_map/ppermute | solution.py:566
  740.0 21.3 %collective-permute-start.59 = (bf16[48,4096]{1,0:T(8,128)(2,1)S(1)}, bf16[48,4096]{1,0:T(8,128)(2,1)S(1)}, u32[]{:S(2)}, u32[]{:S(2)}) collective-permute-start(bf16[48,4096]{1,0:T(8,128)(2,1)S(1)} %add_convert_fusion.48), channel_id=1, source_target_pairs={{1,0},{2,1},{3,2},{5,4},{6,5},{7,6},{9,8},{10,9},{11,10},{13,12},{... | collective-permute-start | bytes 1179656 | tf_op jit(solution)/shard_map/ppermute | solution.py:566
  749.7 20.1 %collective-permute-start.75 = (bf16[48,4096]{1,0:T(8,128)(2,1)S(1)}, bf16[48,4096]{1,0:T(8,128)(2,1)S(1)}, u32[]{:S(2)}, u32[]{:S(2)}) collective-permute-start(bf16[48,4096]{1,0:T(8,128)(2,1)S(1)} %get-tuple-element.110), channel_id=1, source_target_pairs={{0,1},{1,2},{2,3},{4,5},{5,6},{6,7},{8,9},{9,10},{10,11},{12,13},{... | collective-permute-start | bytes 1179656 | tf_op jit(solution)/shard_map/ppermute | solution.py:577
  (166 other events, 2170.2 us)

commit v3 on v2

--- a/solution.py
+++ b/solution.py
@@ -16,7 +16,6 @@
 BF = jnp.bfloat16
 F32 = jnp.float32
 NEG = -1e30
-KV_STEP = 4
 SCALE = HEAD_DIM ** (-0.5)
 
 
@@ -36,107 +35,8 @@
     return dot(a, b, ((0,), (0,)))
 
 
-def chunk_mask(tokens):
-    row = lax.broadcasted_iota(jnp.int32, (tokens, tokens), 0)
-    col = lax.broadcasted_iota(jnp.int32, (tokens, tokens), 1)
-    mask = col <= row
-    return jnp.concatenate([mask] * GROUP, axis=0)
-
-
-def head_scores(place, q, keys, mask):
-    scores = []
-    for r, k in enumerate(keys):
-        s = nt(q, k) * SCALE
-        if r == 0:
-            s = jnp.where(mask, s, NEG)
-        else:
-            s = jnp.where(place >= r, s, NEG)
-        scores.append(s)
-    return scores
-
-
 def lanes(ref, head, width=HEAD_DIM):
     return ref[:, head * HEAD_DIM : head * HEAD_DIM + width]
-
-
-def two_heads(ref, g):
-    return jnp.concatenate([lanes(ref, GROUP * g + i) for i in range(GROUP)], axis=0)
-
-
-def attend_back_body(chunks, place_ref, q_ref, do_ref, lse_ref, *refs):
-    k_refs, v_refs = refs[:chunks], refs[chunks : 2 * chunks]
-    dq_ref = refs[2 * chunks]
-    dk_refs = refs[2 * chunks + 1 : 3 * chunks + 1]
-    dv_refs = refs[3 * chunks + 1 :]
-    tokens = q_ref.shape[0]
-    place = place_ref[0]
-    mask = chunk_mask(tokens)
-    for g in range(KV_STEP):
-        q = two_heads(q_ref, g)
-        do = two_heads(do_ref, g)
-        lse = jnp.concatenate(
-            [lse_ref[0, :, GROUP * g + i : GROUP * g + i + 1] for i in range(GROUP)],
-            axis=0,
-        )
-        keys = [lanes(k, g) for k in k_refs]
-        scores = head_scores(place, q, keys, mask)
-        probs = [jnp.exp(s - lse) for s in scores]
-        dprobs = [nt(do, lanes(v, g)) for v in v_refs]
-        inner = sum(
-            jnp.sum(p * d, axis=1, keepdims=True) for p, d in zip(probs, dprobs)
-        )
-        dq = jnp.zeros((GROUP * tokens, HEAD_DIM), F32)
-        span = slice(g * HEAD_DIM, (g + 1) * HEAD_DIM)
-        for r in range(chunks):
-            ds = (probs[r] * (dprobs[r] - inner)).astype(BF)
-            dq += nn(ds, keys[r])
-            dk_refs[r][:, span] = (tn(ds, q) * SCALE).astype(BF)
-            dv_refs[r][:, span] = tn(probs[r].astype(BF), do).astype(BF)
-        dq = (dq * SCALE).astype(BF)
-        for i in range(GROUP):
-            h = GROUP * g + i
-            dq_ref[:, h * HEAD_DIM : (h + 1) * HEAD_DIM] = dq[
-                i * tokens : (i + 1) * tokens
-            ]
-
-
-def attention_specs(tokens):
-    q_width = KV_STEP * GROUP * HEAD_DIM
-    k_width = KV_STEP * HEAD_DIM
-    steps = KV_HEADS // KV_STEP
-    q_spec = pl.BlockSpec((tokens, q_width), lambda i, s: (0, i))
-    k_spec = pl.BlockSpec((tokens, k_width), lambda i, s: (0, i))
-
-    def kv_spec(r, at):
-        return pl.BlockSpec((None, tokens, k_width), lambda i, s: (r, 0, i + at))
-    lse_spec = pl.BlockSpec((1, tokens, 128), lambda i, s: (i, 0, 0))
-    return steps, q_spec, k_spec, kv_spec, lse_spec
-
-
-def attend_back(place, q, do, lse, kvs):
-    chunks, tokens = kvs.shape[0], q.shape[0]
-    steps, q_spec, k_spec, kv_spec, lse_spec = attention_specs(tokens)
-    span = chunks * tokens
-    kvd = KV_HEADS * HEAD_DIM
-    flops = 10 * HEADS * HEAD_DIM * tokens * span
-    outs = pl.pallas_call(
-        functools.partial(attend_back_body, chunks),
-        grid_spec=pltpu.PrefetchScalarGridSpec(
-            num_scalar_prefetch=1,
-            grid=(steps,),
-            in_specs=[q_spec, q_spec, lse_spec]
-            + [kv_spec(r, 0) for r in range(chunks)]
-            + [kv_spec(r, steps) for r in range(chunks)],
-            out_specs=[q_spec] + [k_spec] * (2 * chunks),
-        ),
-        out_shape=[jax.ShapeDtypeStruct(q.shape, BF)]
-        + [jax.ShapeDtypeStruct((tokens, kvd), BF)] * (2 * chunks),
-        cost_estimate=pl.CostEstimate(
-            flops=flops, bytes_accessed=16 * q.size, transcendentals=HEADS * tokens * span
-        ),
-        name="attend_back",
-    )(place, q, do, lse, *[kvs] * (2 * chunks))
-    return outs[0], outs[1 : chunks + 1], outs[chunks + 1 :]
 
 
 MESH = pl.DeviceIdType.MESH
@@ -246,9 +146,9 @@
 def forward_body(dp, seq, x_ref, gain_ref, cos_ref, first_ref, second_ref, *refs):
     w_in, refs = refs[:7], refs[7:]
     w_out, refs = refs[:7], refs[7:]
-    q_ref, o_ref, lse_ref, n1_ref, gains_ref, kvs_ref = refs[:6]
-    stage, refs = refs[6:13], refs[13:]
-    wq, wk, wv, kvbuf, gbuf, qh, kh, vh, oh, send, recv, kv_send, kv_recv, g_send, g_recv, own_sem, load_sem, kv_out = refs
+    qh, kh, vh, o_ref, lse_ref, n1_ref, gains_ref = refs[:7]
+    stage, refs = refs[7:14], refs[14:]
+    wq, wk, wv, kvbuf, gbuf, oh, send, recv, kv_send, kv_recv, g_send, g_recv, own_sem, load_sem = refs
     me, place = lax.axis_index("dp"), lax.axis_index("seq")
     bits = [1 << i for i in range(1, dp.bit_length() - 1)]
     tokens, model = x_ref.shape
@@ -390,10 +290,9 @@
     @pl.loop(0, model // TILE)
     def _(t):
         at = pl.multiple_of(t * TILE, 128)
-        q_ref[:, pl.ds(at, TILE)] = turn(nn(n1_ref[...], wq[:, pl.ds(at, TILE)])).astype(BF)
-
-    for h in range(HEADS):
-        qh[h] = lanes(q_ref, h)
+        q = turn(nn(n1_ref[...], wq[:, pl.ds(at, TILE)])).astype(BF)
+        for i in range(TILE // HEAD_DIM):
+            qh[t * (TILE // HEAD_DIM) + i] = q[:, i * HEAD_DIM : (i + 1) * HEAD_DIM]
 
     def split_heads(r):
         for g in range(KV_HEADS):
@@ -439,7 +338,7 @@
                 nn((w * inverse).astype(BF), vh[g, r * tokens : (r + 1) * tokens, :])
                 for r, w in enumerate(weights)
             ).astype(BF)
-            lse_ref[h // half] += jnp.where(lane == h % half, top + jnp.log(total), 0.0)
+            lse_ref[...] += jnp.where(lane == h, top + jnp.log(total), 0.0)
 
     attend_heads(0, half)
     job_g.share()
@@ -452,8 +351,6 @@
     job_u.share()
     job_d.cross()
     job_d.share()
-    kv_save = pltpu.make_async_copy(kvbuf, kvs_ref, kv_out)
-    kv_save.start()
     for job in (job_o, job_g, job_u, job_d):
         job.finish()
     for r in range(seq - 1):
@@ -466,7 +363,6 @@
         g.wait_send()
     for job in jobs:
         job.drain()
-    kv_save.wait()
 
 
 def forward_call(dp, seq, x, gains, tables, weights):
@@ -476,13 +372,16 @@
     anyspec = pl.BlockSpec(memory_space=pl.ANY)
     vmem = pl.BlockSpec(memory_space=pltpu.VMEM)
     out_shape = [jax.ShapeDtypeStruct((dp * w.shape[0], w.shape[1]), BF) for w in weights]
+    heads = jax.ShapeDtypeStruct((HEADS, tokens, HEAD_DIM), BF)
+    keys = jax.ShapeDtypeStruct((KV_HEADS, seq * tokens, HEAD_DIM), BF)
     out_shape += [
+        heads,
+        keys,
+        keys,
         jax.ShapeDtypeStruct((tokens, model), BF),
-        jax.ShapeDtypeStruct((tokens, model), BF),
-        jax.ShapeDtypeStruct((2, tokens, 128), F32),
+        jax.ShapeDtypeStruct((tokens, 128), F32),
         jax.ShapeDtypeStruct((tokens, model), BF),
         jax.ShapeDtypeStruct((8, model), F32),
-        jax.ShapeDtypeStruct((seq, tokens, model), BF),
     ]
     kvd = weights[1].shape[1]
     dma = pltpu.SemaphoreType.DMA
@@ -490,7 +389,7 @@
         functools.partial(forward_body, dp, seq),
         out_shape=out_shape,
         in_specs=[vmem] * 5 + [anyspec] * 7,
-        out_specs=[anyspec] * 7 + [vmem] * 5 + [anyspec],
+        out_specs=[anyspec] * 7 + [vmem] * 7,
         scratch_shapes=[pltpu.VMEM(w.shape, BF) for w in weights]
         + [
             pltpu.VMEM((model, model), BF),
@@ -498,9 +397,6 @@
             pltpu.VMEM((model, kvd), BF),
             pltpu.VMEM((seq, tokens, model), BF),
             pltpu.VMEM((dp, 8, 256), F32),
-            pltpu.VMEM((HEADS, tokens, HEAD_DIM), BF),
-            pltpu.VMEM((KV_HEADS, seq * tokens, HEAD_DIM), BF),
-            pltpu.VMEM((KV_HEADS, seq * tokens, HEAD_DIM), BF),
             pltpu.VMEM((HEADS, tokens, HEAD_DIM), BF),
             dma((7, copies)),
             dma((7, copies)),
@@ -510,13 +406,583 @@
             dma((dp,)),
             dma((7,)),
             dma((3,)),
-            dma(()),
         ],
         compiler_params=pltpu.CompilerParams(
             collective_id=0, has_side_effects=True, vmem_limit_bytes=60 * 1024 * 1024
         ),
         name="forward",
     )(x, gains, *tables, *weights)
+
+
+def head_column(lse, h):
+    lane = lax.broadcasted_iota(jnp.int32, lse.shape, 1)
+    return jnp.sum(jnp.where(lane == h, lse, 0.0), axis=1, keepdims=True)
+
+
+def back_group(place, chunks, g, q_ref, do_ref, lse, k, v, dq_ref, dk_ref, dv_ref, acc_k, acc_v):
+    tokens = q_ref.shape[1]
+    row = lax.broadcasted_iota(jnp.int32, (tokens, tokens), 0)
+    col = lax.broadcasted_iota(jnp.int32, (tokens, tokens), 1)
+    for i in range(GROUP):
+        h = GROUP * g + i
+        q, do = q_ref[h], do_ref[h]
+        total = head_column(lse, h)
+        probs, dprobs = [], []
+        for r in range(chunks):
+            span = slice(r * tokens, (r + 1) * tokens)
+            s = nt(q, k[span, :]) * SCALE
+            s = jnp.where(col <= row if r == 0 else place >= r, s, NEG)
+            probs.append(jnp.exp(s - total))
+            dprobs.append(nt(do, v[span, :]))
+        inner = sum(jnp.sum(p * d, axis=1, keepdims=True) for p, d in zip(probs, dprobs))
+        dq = jnp.zeros((tokens, HEAD_DIM), F32)
+        for r in range(chunks):
+            span = slice(r * tokens, (r + 1) * tokens)
+            ds = (probs[r] * (dprobs[r] - inner)).astype(BF)
+            dq += nn(ds, k[span, :])
+            dk = tn(ds, q)
+            dv = tn(probs[r].astype(BF), do)
+            if i == 0:
+                acc_k[span, :] = dk
+                acc_v[span, :] = dv
+            else:
+                dk_ref[g, span, :] = ((acc_k[span, :] + dk) * SCALE).astype(BF)
+                dv_ref[g, span, :] = (acc_v[span, :] + dv).astype(BF)
+        dq_ref[h] = (dq * SCALE).astype(BF)
+
+
+COLS = 512
+LAG_B, LAG_C, LAG_D = 1, 3, 5
+SLOTS_CORE, SLOTS, SLOTS_SUM, SLOTS_OUT = 2, 4, 10, 8
+
+
+def backward_body(seq, x_ref, gains_ref, e2_ref, cos_ref, first_ref, second_ref, hidden_ref, eb_ref, lefts_ref,
+                  qh, kh, vh, do_ref, lse_ref, gain2_ref, rights_in, wq_in, wk_in, wv_in, *refs):
+    dx_ref, gain_out, res = refs[:3]
+    (rights, doh, dqh, dkh, dvh, acc_k, acc_v, dkv, dkv_in, dn1, wt,
+     cs, cr, sums, r0, r1, zs, zr, zt, gsend, grecv, gsum, gzrecv,
+     load_sem, w_sem, core_s, core_r, s0_s, s0_r, s1_s, s1_r, z_s, z_r, a_s, a_r, t_sem, kv_s, kv_r,
+     g_s, g_r, gz_s, gz_r, core_free, s0_free, s1_free, z_free) = refs[3:]
+    me, place = lax.axis_index("dp"), lax.axis_index("seq")
+    core, chip_x, chip_y = me % 2, (me // 2) % 2, me // 4
+    tokens, model = x_ref.shape
+    rows = model // 8
+    sub = rows // seq
+    kvd = wk_in.shape[1]
+    d_rows = hidden_ref.shape[0] // 8
+    d_chunks = d_rows * 3 // rows
+    n_chunks = rights.shape[1] // COLS
+    o_panels = model // COLS
+    gu_panels = n_chunks - 3 * o_panels
+    total_chunks = d_chunks + n_chunks
+
+    def owner(x, y, c):
+        return ((chip_y + y) % 2) * 4 + ((chip_x + x) % 2) * 2 + (core + c) % 2
+
+    partner = owner(0, 0, 1)
+    near = [[owner(1, 0, 0), owner(0, 1, 0)], [owner(0, 1, 0), owner(1, 0, 0)]]
+
+    load = pltpu.make_async_copy(rights_in, rights.at[:, : rights_in.shape[1]], load_sem)
+    load.start()
+
+    barrier = pltpu.get_barrier_semaphore()
+    for off in range(1, 8):
+        pl.semaphore_signal(barrier, inc=1, device_id={"dp": me ^ off}, device_id_type=MESH)
+    for far in range(1, seq):
+        to = (place + far) % seq
+        pl.semaphore_signal(barrier, inc=1, device_id={"seq": to}, device_id_type=MESH)
+    pl.semaphore_wait(barrier, 7 + seq - 1)
+
+    for h in range(HEADS):
+        doh[h] = lanes(do_ref, h)
+    load.wait()
+
+    def remote(src, dst, send, recv, **target):
+        return pltpu.make_async_remote_copy(
+            src_ref=src, dst_ref=dst, send_sem=send, recv_sem=recv, device_id=target, device_id_type=MESH
+        )
+
+    def signal(sem, **target):
+        pl.semaphore_signal(sem, inc=1, device_id=target, device_id_type=MESH)
+
+    def core_copy(c):
+        s = c % SLOTS_CORE
+        return remote(cs.at[s], cr.at[s], core_s.at[s], core_r.at[s], dp=partner)
+
+    def first_copy(c, parity):
+        s = c % SLOTS
+        return remote(sums.at[c % SLOTS_SUM, pl.ds(2 * rows, 2 * rows)], r0.at[s], s0_s.at[s], s0_r.at[s], dp=near[parity][0])
+
+    def second_copy(c, parity):
+        s = c % SLOTS
+        return remote(sums.at[c % SLOTS_SUM, pl.ds(rows, rows)], r1.at[s], s1_s.at[s], s1_r.at[s], dp=near[parity][1])
+
+    def offsets(index, parity):
+        low, high = index % 2, index // 2
+        return (high, low) if parity == 0 else (low, high)
+
+    def stage_a(c, parity):
+        s, t = c % SLOTS_CORE, c % SLOTS_SUM
+
+        @pl.when(c >= SLOTS_CORE)
+        def _():
+            core_copy(c).wait_send()
+
+        def put(away, term):
+            @pl.loop(0, 4)
+            def _(index):
+                dx, dy = offsets(index, parity)
+                at = pl.multiple_of(index * rows, 16)
+                if away:
+                    cs[s, pl.ds(at, rows), :] = term(owner(dx, dy, 1)).astype(BF)
+                else:
+                    sums[t, pl.ds(at, rows), :] = term(owner(dx, dy, 0)).astype(BF)
+
+        def term_d(who):
+            size = rows // 3
+            at = pl.multiple_of(who * d_rows + c * size, 16)
+            left = hidden_ref[pl.ds(at, size), :]
+            return jnp.concatenate(
+                [nn(left, eb_ref[:, i * COLS : (i + 1) * COLS]) for i in range(3)], axis=0
+            )
+
+        k = c - d_chunks
+        which = (k >= gu_panels).astype(jnp.int32) + (k >= gu_panels + o_panels).astype(jnp.int32)
+
+        def term_n(who):
+            left = lefts_ref[pl.ds(pl.multiple_of(which * model + who * rows, 16), rows), :]
+            return nn(left, rights[:, pl.ds(pl.multiple_of(k * COLS, 128), COLS)])
+
+        def both(term):
+            put(True, term)
+
+            @pl.when(c >= SLOTS_CORE)
+            def _():
+                pl.semaphore_wait(core_free, 1)
+
+            core_copy(c).start()
+            put(False, term)
+
+        @pl.when(c < d_chunks)
+        def _():
+            both(term_d)
+
+        @pl.when(c >= d_chunks)
+        def _():
+            both(term_n)
+
+    def add_rows(count, target, extra):
+        @pl.loop(0, count // 64)
+        def _(i):
+            at = pl.multiple_of(i * 64, 16)
+            target[pl.ds(at, 64), :] = (target[pl.ds(at, 64), :].astype(F32) + extra[pl.ds(at, 64), :].astype(F32)).astype(BF)
+
+    def stage_b(c, parity):
+        core_copy(c).wait_recv()
+        add_rows(4 * rows, sums.at[c % SLOTS_SUM], cr.at[c % SLOTS_CORE])
+
+        @pl.when(c < total_chunks - SLOTS_CORE)
+        def _():
+            signal(core_free, dp=partner)
+
+        @pl.when(c >= SLOTS)
+        def _():
+            pl.semaphore_wait(s0_free.at[parity], 1)
+
+        first_copy(c, parity).start()
+
+    def stage_c(c, parity):
+        first_copy(c, parity).wait_recv()
+        add_rows(2 * rows, sums.at[c % SLOTS_SUM], r0.at[c % SLOTS])
+
+        @pl.when(c < total_chunks - SLOTS)
+        def _():
+            signal(s0_free.at[parity], dp=near[parity][0])
+
+        @pl.when(c >= SLOTS)
+        def _():
+            pl.semaphore_wait(s1_free.at[parity], 1)
+
+        second_copy(c, parity).start()
+        first_copy(c, parity).wait_send()
+
+    def stage_d(c, parity):
+        second_copy(c, parity).wait_recv()
+        add_rows(rows, sums.at[c % SLOTS_SUM], r1.at[c % SLOTS])
+
+        @pl.when(c < total_chunks - SLOTS)
+        def _():
+            signal(s1_free.at[parity], dp=near[parity][1])
+
+        second_copy(c, parity).wait_send()
+
+    def step_of(way):
+        return 1 - 2 * way
+
+    def inside(at):
+        return (at >= 0) & (at < seq)
+
+    def z_copy(c, way, hop):
+        s = c % SLOTS
+        slot = way * (seq - 1) + hop - 1
+        return remote(zs.at[slot, s], zr.at[slot, s], z_s.at[slot, s], z_r.at[slot, s], seq=place + step_of(way))
+
+    def z_sends(way, hop):
+        return inside(place + step_of(way) * (seq - hop))
+
+    def z_gets(way, hop):
+        return inside(place - step_of(way)) & inside(place - step_of(way) + step_of(way) * (seq - hop))
+
+    def part(c, index):
+        index = jnp.minimum(jnp.maximum(index, 0), seq - 1)
+        return sums[c % SLOTS_SUM, pl.ds(pl.multiple_of(index * sub, 16), sub), :].astype(F32)
+
+    def z_take(c, way, hop):
+        slot = way * (seq - 1) + hop - 1
+        gets = z_gets(way, hop)
+
+        @pl.when(gets)
+        def _():
+            z_copy(c, way, hop).wait_recv()
+
+        return jnp.where(gets, zr[slot, c % SLOTS].astype(F32), 0.0)
+
+    def z_release(c, way, hop):
+        slot = way * (seq - 1) + hop - 1
+
+        @pl.when(z_gets(way, hop) & (c < total_chunks - SLOTS))
+        def _():
+            signal(z_free.at[slot], seq=place - step_of(way))
+
+    def stage_z(c, hop):
+        for way in range(2):
+            slot = way * (seq - 1) + hop - 1
+            value = part(c, place + step_of(way) * (seq - hop))
+            if hop > 1:
+                value = value + z_take(c, way, hop - 1)
+            sends = z_sends(way, hop)
+
+            @pl.when(sends & (c >= SLOTS))
+            def _():
+                z_copy(c, way, hop).wait_send()
+
+            zs[slot, c % SLOTS] = value.astype(BF)
+            if hop > 1:
+                z_release(c, way, hop - 1)
+
+            @pl.when(sends & (c >= SLOTS))
+            def _():
+                pl.semaphore_wait(z_free.at[slot], 1)
+
+            @pl.when(sends)
+            def _():
+                z_copy(c, way, hop).start()
+
+    def res_at(c, source):
+        index = jnp.minimum(jnp.maximum(source, 0), seq - 1)
+        return res.at[pl.ds(pl.multiple_of(c * rows + index * sub, 16), sub)]
+
+    def own_copy(c):
+        s = c % SLOTS_OUT
+        return pltpu.make_async_copy(zt.at[s], res_at(c, place), t_sem.at[s])
+
+    def a_copy(c, way, hop):
+        s = c % SLOTS_OUT
+        slot = way * (seq - 1) + hop - 1
+        source = place - step_of(way) * (hop - 1)
+        src = zt.at[s] if hop == 1 else res_at(c, source)
+        return remote(src, res_at(c, source), a_s.at[slot, s], a_r.at[slot, s], seq=place + step_of(way))
+
+    def a_sends(way, hop):
+        return inside(place + step_of(way)) & inside(place - step_of(way) * (hop - 1))
+
+    def a_gets(way, hop):
+        return inside(place - step_of(way) * hop)
+
+    def stage_total(c):
+        value = part(c, place)
+        for way in range(2):
+            value = value + z_take(c, way, seq - 1)
+
+        @pl.when(c >= SLOTS_OUT)
+        def _():
+            own_copy(c).wait()
+
+        for way in range(2):
+            @pl.when((c >= SLOTS_OUT) & a_sends(way, 1))
+            def _():
+                a_copy(c, way, 1).wait_send()
+
+        zt[c % SLOTS_OUT] = value.astype(BF)
+        for way in range(2):
+            z_release(c, way, seq - 1)
+        own_copy(c).start()
+        stage_out(c, 1)
+
+    def stage_out(c, hop):
+        for way in range(2):
+            if hop > 1:
+                @pl.when(a_gets(way, hop - 1))
+                def _():
+                    a_copy(c, way, hop - 1).wait_recv()
+
+            if hop < seq:
+                if hop > 1:
+                    @pl.when((c >= SLOTS_OUT) & a_sends(way, hop))
+                    def _():
+                        a_copy(c, way, hop).wait_send()
+
+                @pl.when(a_sends(way, hop))
+                def _():
+                    a_copy(c, way, hop).start()
+
+    lag_total = LAG_D + seq - 1
+    stages = [(LAG_B, stage_b), (LAG_C, stage_c), (LAG_D, stage_d), (LAG_D, lambda c, parity: stage_z(c, 1))]
+    stages += [(LAG_D + hop - 1, lambda c, parity, hop=hop: stage_z(c, hop)) for hop in range(2, seq)]
+    stages += [(lag_total, lambda c, parity: stage_total(c))]
+    stages += [(lag_total + hop - 1, lambda c, parity, hop=hop: stage_out(c, hop)) for hop in range(2, seq + 1)]
+    last_lag = lag_total + seq - 1
+
+    def tick(c, parity):
+        for lag, stage in sorted(stages, key=lambda pair: -pair[0]):
+            then = c - lag
+
+            @pl.when((then >= 0) & (then < total_chunks))
+            def _():
+                stage(then, (parity + lag) % 2)
+
+        @pl.when(c < total_chunks)
+        def _():
+            stage_a(c, parity)
+
+    def kv_copy(r):
+        return remote(dkv.at[r], dkv_in.at[r - 1], kv_s.at[r], kv_r.at[r], seq=place - 1)
+
+    def kv_send(r):
+        @pl.when(place >= r)
+        def _():
+            kv_copy(r).start()
+
+    def kv_take(r):
+        gets = (place + 1 >= r) & (place + 1 < seq)
+
+        @pl.when(gets)
+        def _():
+            kv_copy(r).wait_recv()
+            add_rows(tokens, dkv.at[r - 1], dkv_in.at[r - 1])
+
+    def turn_back(value):
+        ahead = pltpu.roll(value, TILE - HEAD_DIM // 2, 1)
+        behind = pltpu.roll(value, HEAD_DIM // 2, 1)
+        return (value * cos_ref[...] - behind * second_ref[...] + ahead * first_ref[...]).astype(BF)
+
+    q_at = (gu_panels + o_panels) * COLS
+
+    def w_load(t, i):
+        at = pl.multiple_of(t * TILE, 16)
+        s = t % 2
+        src, lo, width = ((wq_in, 0, model), (wk_in, model, kvd), (wv_in, model + kvd, kvd))[i]
+        return pltpu.make_async_copy(src.at[pl.ds(at, TILE)], wt.at[s, :, pl.ds(lo, width)], w_sem.at[s, i])
+
+    def last_norm():
+        for h in range(HEADS):
+            rights[:, q_at + h * HEAD_DIM : q_at + (h + 1) * HEAD_DIM] = dqh[h]
+        for t in range(model // TILE):
+            at = q_at + t * TILE
+            rights[:, at : at + TILE] = turn_back(rights[:, at : at + TILE].astype(F32))
+        for t in range(kvd // TILE):
+            at = q_at + model + t * TILE
+            rights[:, at : at + TILE] = turn_back(dkv[0, :, t * TILE : (t + 1) * TILE].astype(F32))
+        rights[:, q_at + model + kvd :] = dkv[0, :, kvd:]
+        for i in range(3):
+            w_load(0, i).start()
+
+        @pl.loop(0, model // TILE)
+        def _(t):
+            for i in range(3):
+                w_load(t, i).wait()
+
+            @pl.when(t + 1 < model // TILE)
+            def _():
+                for i in range(3):
+                    w_load(t + 1, i).start()
+
+            dn1[:, pl.ds(pl.multiple_of(t * TILE, 128), TILE)] = nt(rights[:, q_at:], wt[t % 2])
+
+        x = x_ref[...].astype(F32)
+        scale = lax.rsqrt(jnp.mean(x * x, axis=1, keepdims=True) + EPS)
+        unit = x * scale
+        grad = dn1[...]
+        term = jnp.sum(grad * unit, axis=0, keepdims=True)
+        scaled = grad * gains_ref[0:1, :]
+        inner = jnp.mean(scaled * unit, axis=1, keepdims=True)
+        dx_ref[...] = e2_ref[...] + scale * (scaled - unit * inner)
+        for k in range(8):
+            gsend[k, 0:1, :rows] = term[:, k * rows : (k + 1) * rows]
+            gsend[k, 1:2, :rows] = gain2_ref[0:1, k * rows : (k + 1) * rows]
+
+    def gain_copies():
+        return [
+            remote(gsend.at[me ^ off], grecv.at[me], g_s.at[off], g_r.at[off], dp=me ^ off) for off in range(1, 8)
+        ]
+
+    def gain_line():
+        return [
+            remote(gsum, gzrecv.at[place], gz_s.at[far], gz_r.at[far], seq=(place + far) % seq) for far in range(1, seq)
+        ]
+
+    ticks = total_chunks + last_lag
+    d_pairs = KV_HEADS // 2
+
+    @pl.loop(0, -(-ticks // 2))
+    def _(p):
+        for parity in range(2):
+            tick(2 * p + parity, parity)
+
+        @pl.when(p < d_pairs)
+        def _():
+            for i in range(2):
+                g = 2 * p + i
+                back_group(place, seq, g, qh, doh, lse_ref[...], kh.at[g], vh.at[g], dqh, dkh, dvh, acc_k, acc_v)
+
+        @pl.when(p == d_pairs - 1)
+        def _():
+            for r in range(seq):
+                for g in range(KV_HEADS):
+                    lo = g * HEAD_DIM
+                    dkv[r, :, lo : lo + HEAD_DIM] = dkh[g, r * tokens : (r + 1) * tokens, :]
+                    dkv[r, :, kvd + lo : kvd + lo + HEAD_DIM] = dvh[g, r * tokens : (r + 1) * tokens, :]
+            kv_send(seq - 1)
+
+        for r in range(seq - 1, 0, -1):
+            @pl.when(p == d_pairs - 1 + 2 * (seq - r))
+            def _():
+                kv_take(r)
+                if r > 1:
+                    kv_send(r - 1)
+                else:
+                    last_norm()
+                    for made in gain_copies():
+                        made.start()
+                    grecv[me] = gsend[me]
+
+        @pl.when(p == d_pairs + 2 * seq - 2)
+        def _():
+            for made in gain_copies():
+                made.wait_recv()
+            gsum[...] = sum(grecv[k] for k in range(1, 8)) + grecv[0]
+            gzrecv[place] = gsum[...]
+            for made in gain_line():
+                made.start()
+
+        @pl.when(p == d_pairs + 2 * seq - 1)
+        def _():
+            for made in gain_line():
+                made.wait_recv()
+            gain_out[...] = sum(gzrecv[k] for k in range(seq))
+
+    for made in gain_copies() + gain_line():
+        made.wait_send()
+    for r in range(1, seq):
+        @pl.when(place >= r)
+        def _():
+            kv_copy(r).wait_send()
+    for c in range(total_chunks - SLOTS_CORE, total_chunks):
+        core_copy(c).wait_send()
+    for way in range(2):
+        for hop in range(1, seq):
+            for c in range(total_chunks - SLOTS, total_chunks):
+                @pl.when(z_sends(way, hop))
+                def _():
+                    z_copy(c, way, hop).wait_send()
+            for c in range(total_chunks - SLOTS_OUT, total_chunks):
+                @pl.when(a_sends(way, hop))
+                def _():
+                    a_copy(c, way, hop).wait_send()
+    for c in range(total_chunks - SLOTS_OUT, total_chunks):
+        own_copy(c).wait()
+
+
+def backward_call(seq, x, gains, e2, tables, hidden_t, eb, lefts, qh, kh, vh, do, lse, gain2, rights, w_q, w_k, w_v):
+    tokens, model = x.shape
+    rows = model // 8
+    sub = rows // seq
+    kvd = w_k.shape[1]
+    wide = rights.shape[1] + model + 2 * kvd
+    chunks = hidden_t.shape[0] // 8 * 3 // rows + wide // COLS
+    anyspec = pl.BlockSpec(memory_space=pl.ANY)
+    vmem = pl.BlockSpec(memory_space=pltpu.VMEM)
+    dma, regular = pltpu.SemaphoreType.DMA, pltpu.SemaphoreType.REGULAR
+    hops = 2 * (seq - 1)
+    heads = pltpu.VMEM((HEADS, tokens, HEAD_DIM), BF)
+    keys = pltpu.VMEM((KV_HEADS, seq * tokens, HEAD_DIM), BF)
+    return pl.pallas_call(
+        functools.partial(backward_body, seq),
+        out_shape=[
+            jax.ShapeDtypeStruct((tokens, model), F32),
+            jax.ShapeDtypeStruct((8, 256), F32),
+            jax.ShapeDtypeStruct((chunks * rows, COLS), BF),
+        ],
+        in_specs=[vmem] * 15 + [anyspec] * 4,
+        out_specs=[vmem, vmem, anyspec],
+        scratch_shapes=[
+            pltpu.VMEM((tokens, wide), BF),
+            heads, heads, keys, keys,
+            pltpu.VMEM((seq * tokens, HEAD_DIM), F32),
+            pltpu.VMEM((seq * tokens, HEAD_DIM), F32),
+            pltpu.VMEM((seq, tokens, model), BF),
+            pltpu.VMEM((seq - 1, tokens, model), BF),
+            pltpu.VMEM((tokens, model), F32),
+            pltpu.VMEM((2, TILE, model + 2 * kvd), BF),
+            pltpu.VMEM((SLOTS_CORE, 4 * rows, COLS), BF),
+            pltpu.VMEM((SLOTS_CORE, 4 * rows, COLS), BF),
+            pltpu.VMEM((SLOTS_SUM, 4 * rows, COLS), BF),
+            pltpu.VMEM((SLOTS, 2 * rows, COLS), BF),
+            pltpu.VMEM((SLOTS, rows, COLS), BF),
+            pltpu.VMEM((hops, SLOTS, sub, COLS), BF),
+            pltpu.VMEM((hops, SLOTS, sub, COLS), BF),
+            pltpu.VMEM((SLOTS_OUT, sub, COLS), BF),
+            pltpu.VMEM((8, 8, 256), F32),
+            pltpu.VMEM((8, 8, 256), F32),
+            pltpu.VMEM((8, 256), F32),
+            pltpu.VMEM((seq, 8, 256), F32),
+            dma(()), dma((2, 3)),
+            dma((SLOTS_CORE,)), dma((SLOTS_CORE,)),
+            dma((SLOTS,)), dma((SLOTS,)),
+            dma((SLOTS,)), dma((SLOTS,)),
+            dma((hops, SLOTS)), dma((hops, SLOTS)),
+            dma((hops, SLOTS_OUT)), dma((hops, SLOTS_OUT)),
+            dma((SLOTS_OUT,)),
+            dma((seq,)), dma((seq,)),
+            dma((8,)), dma((8,)),
+            dma((seq,)), dma((seq,)),
+            regular, regular((2,)), regular((2,)), regular((hops,)),
+        ],
+        compiler_params=pltpu.CompilerParams(
+            collective_id=1, has_side_effects=True, vmem_limit_bytes=62 * 1024 * 1024
+        ),
+        name="backward",
+    )(x, gains, e2, *tables, hidden_t, eb, lefts, qh, kh, vh, do, lse, gain2, rights, w_q, w_k, w_v)
+
+
+def attend_back(place, qh, kh, vh, doh, lse):
+    chunks = kh.shape[1] // qh.shape[1]
+
+    def body(place_ref, q_ref, k_ref, v_ref, do_ref, lse_ref, dq_ref, dk_ref, dv_ref, acc_k, acc_v):
+        @pl.loop(0, KV_HEADS)
+        def _(g):
+            back_group(place_ref[0], chunks, g, q_ref, do_ref, lse_ref[...], k_ref.at[g], v_ref.at[g], dq_ref, dk_ref, dv_ref, acc_k, acc_v)
+
+    vmem = pl.BlockSpec(memory_space=pltpu.VMEM)
+    acc = pltpu.VMEM(kh.shape[1:], F32)
+    return pl.pallas_call(
+        body,
+        in_specs=[pl.BlockSpec(memory_space=pltpu.SMEM)] + [vmem] * 5,
+        out_specs=[vmem] * 3,
+        out_shape=[jax.ShapeDtypeStruct(a.shape, BF) for a in (qh, kh, vh)],
+        scratch_shapes=[acc, acc],
+        name="attend_back",
+    )(place, qh, kh, vh, doh, lse)
 
 
 def flip(value, axis, bit):
@@ -644,7 +1110,7 @@
     shards = [w[0] for w in (w_query, w_key, w_value, w_out, w_gate, w_up, w_down)]
     outs = forward_call(dp, seq, tokens[0], packed, [t[:, :TILE] for t in tables], shards)
     w_q, w_k, w_v, w_o, w_g, w_u, w_d = outs[:7]
-    q, mixed, lse, n1, gains, kvs = outs[7:]
+    qh, kh, vh, mixed, lse, n1, gains = outs[7:]
     gain_one, gain_two = gains[0:1], gains[1:2]
     scale_one = norm_scale(x)
     x2 = x + nn(mixed, w_o)
@@ -658,6 +1124,46 @@
 
     e = cotangent[0].astype(F32)
     eb = cotangent[0]
+    dh = nt(eb, w_d)
+    dgate = (dh * up * sig * (1.0 + gate * (1.0 - sig))).astype(BF)
+    dup = (dh * gate * sig).astype(BF)
+    dn2 = nt(dgate, w_g) + nt(dup, w_u)
+    dx2, term_gain_two = norm_back(x2, scale_two, gain_two, dn2)
+    e2 = e + dx2
+    e2b = e2.astype(BF)
+    do = nt(e2b, w_o).astype(BF)
+    if len(bits) == 2 and (model // dp) % (16 * seq) == 0:
+        lefts = jnp.concatenate([n2.T, mixed.T, n1.T], axis=0)
+        rights = jnp.concatenate([dgate, dup, e2b], axis=1)
+        dx, grads, res = backward_call(
+            seq, tokens[0], gains, e2, [t[:, :TILE] for t in tables], hidden.T, eb, lefts,
+            qh, kh, vh, do, lse, term_gain_two[None], rights, w_q, w_k, w_v,
+        )
+        block = model // dp
+        res = res.reshape(-1, block, COLS)
+        n_down = w_down.shape[1] * 3 // block
+        n_ff, n_model = w_gate.shape[2] // COLS, model // COLS
+
+        def columns(lo, count):
+            return res[lo : lo + count].transpose(1, 0, 2).reshape(block, count * COLS).astype(F32)
+
+        down = res[:n_down].reshape(n_down, 3, block // 3, COLS).transpose(0, 2, 1, 3)
+        at = n_down + 2 * n_ff
+        attn = columns(at + n_model, 2 * n_model)
+        return (
+            result[None],
+            dx[None],
+            attn[None, :, :model],
+            attn[None, :, model : model + kvd],
+            attn[None, :, model + kvd :],
+            columns(at, n_model)[None],
+            columns(n_down, n_ff)[None],
+            columns(n_down + n_ff, n_ff)[None],
+            down.reshape(1, w_down.shape[1], model).astype(F32),
+            grads[0:1, :block],
+            grads[1:2, :block],
+        )
+
     hidden_a = xor_columns(hidden, bits)
     hidden_b = xor_columns(hidden, turned)
     sum_down = jnp.concatenate(
@@ -667,16 +1173,9 @@
         ],
         axis=1,
     )
-    dh = nt(eb, w_d)
-    dgate = (dh * up * sig * (1.0 + gate * (1.0 - sig))).astype(BF)
-    dup = (dh * gate * sig).astype(BF)
     n2_a, n2_b = xor_columns(n2, bits), xor_columns(n2, turned)
     sum_gate = scatter_term(n2_a, dgate, bits)
     sum_up = scatter_term(n2_b, dup, turned)
-    dn2 = nt(dgate, w_g) + nt(dup, w_u)
-    dx2, term_gain_two = norm_back(x2, scale_two, gain_two, dn2)
-    e2 = e + dx2
-    e2b = e2.astype(BF)
     mixed_a, mixed_b = xor_columns(mixed, bits), xor_columns(mixed, turned)
     sum_out = jnp.concatenate(
         [
@@ -685,8 +1184,10 @@
         ],
         axis=1,
     )
-    do = nt(e2b, w_o).astype(BF)
-    dq, dks, dvs = attend_back(place_arr, q, do, lse, kvs)
+    doh = do.reshape(rows, HEADS, HEAD_DIM).transpose(1, 0, 2)
+    dqh, dkh, dvh = attend_back(place_arr, qh, kh, vh, doh, lse)
+    dq = dqh.transpose(1, 0, 2).reshape(rows, model)
+    dks, dvs = (a.reshape(KV_HEADS, seq, rows, HEAD_DIM).transpose(1, 2, 0, 3).reshape(seq, rows, kvd) for a in (dkh, dvh))
     held = None
     for far in range(seq - 1, -1, -1):
         mine = jnp.concatenate([dks[far], dvs[far]], axis=1)

time: 816 us -> 648 us (0.79)
  Pallas kernels: 215 us -> 511 us
  starting transfers between devices: 214 us -> 0 us
  waiting for transfers between devices: 199 us -> 0 us
  matrix products: 108 us -> 59.2 us
  other arithmetic: 30.5 us -> 13.2 us
  local copies, waits for them, and re-layouts: 40.1 us -> 53.7 us
    pallas_call x1, Pallas kernels: 19.8 us -> 314 us  [backward_call(): pl.pallas_call(functools.partial(backward_body, seq), out_shape=[jax.Shap...]
    ppermute x104 -> x0, starting transfers between devices: 214 us -> none  [the longest x36 118 us: line_sum(): held = lax.ppermute(mine, 'seq', pairs)]
    ppermute x104 -> x0, waiting for transfers between devices: 199 us -> none  [the longest x29 80.6 us: flip(): return lax.ppermute(value, axis, [(i, i ^ bit) for i in range(size)])]
    dot_general x35 -> x8, matrix products: 108 us -> 59.2 us  [dot(): return lax.dot_general(a, b, (dims, ((), ())), preferred_element_type=F32)]
    convert_element_type x0 -> x8, local copies, waits for them, and re-layouts: none -> 21.5 us  [the longest x2 11 us: local(): down.reshape(1, w_down.shape[1], model).astype(F32)]
    dot_general x0 -> x2, local copies, waits for them, and re-layouts: none -> 11.2 us  [dot(): return lax.dot_general(a, b, (dims, ((), ())), preferred_element_type=F32)]
    convert_element_type x38 -> x3, other arithmetic: 19.2 us -> 8.23 us  [the longest x1 5.98 us: local(): hidden = (gate * sig * up).astype(BF)]
    unnamed x194 -> x29, local copies, waits for them, and re-layouts: 16.7 us -> 5.99 us
  transfers between devices with their start and end apart: 104 -> 0, of which waited for: 47 -> 0; matrix products, arithmetic and copies ran while one was open for 12% -> 0% of each run, Pallas kernels for 0% -> 0%
where the time goes in v3:
time: 648 us; the launch traced here: 638 us
  Pallas kernels  511 us (79%)
  matrix products  59.2 us (9%)
  local copies, waits for them, and re-layouts  53.7 us (8%)
  other arithmetic  13.2 us (2%)
    pallas_call x1, Pallas kernels, backward_call(): pl.pallas_call(functools.partial(backward_body, seq), out_shape=[jax.Shap...  314 us
    pallas_call x1, Pallas kernels, forward_call(): pl.pallas_call(functools.partial(forward_body, dp, seq), out_shape=out_sh...  197 us
    dot_general x8, matrix products, dot(): return lax.dot_general(a, b, (dims, ((), ())), preferred_element_type=F32)  59.2 us

profile of v3, /device:TPU:0, one launch (start us, length us, event | category | flops | bytes accessed | tf_op | source)
XLA Modules:
  0.0 638.3 jit_solution(16632865189221440166)
XLA Ops:
  5.1 196.7 %forward.1 = (bf16[1536,1536]{1,0:T(8,128)(2,1)}, bf16[1536,768]{1,0:T(8,128)(2,1)}, bf16[1536,768]{1,0:T(8,128)(2,1)}, bf16[1536,1536]{1,0:T(8,128)(2,1)}, bf16...) custom-call(bf16[256,1536]{1,0:T(8,128)(2,1)} %bitcast.98, ...), custom_call_target="tpu_custom_call" | custom-call | tf_op jit(solution)/shard_map/forward/pallas_call | solution.py:388
  201.9 4.1 multiply_reduce_fusion.2
  206.8 6.5 %fusion.12 = f32[256,4096]{1,0:T(8,128)S(1)} fusion(bf16[1536,4096]{1,0:T(8,128)(2,1)} %get-tuple-element.55, f32[256,1536]{1,0:T(8,128)S(1)} %get-tuple-element.87, f32[1536]{0:T(1024)S(1)} %slice_reduce_fusion, f32[256]{0:T(256)S(1)} %add_rsqrt_fusion), kind=kOutput, calls=%fused_computation.48 | convolution fusion | flops 3222405120 | bytes 18357248 | tf_op jit(solution)/shard_map/dot_general | solution.py:23
  213.4 8.3 %fusion.13 = f32[256,4096]{1,0:T(8,128)S(1)} fusion(bf16[1536,4096]{1,0:T(8,128)(2,1)} %get-tuple-element.56, f32[256,1536]{1,0:T(8,128)S(1)} %get-tuple-element.87, f32[1536]{0:T(1024)S(1)} %slice_reduce_fusion, f32[256]{0:T(256)S(1)} %add_rsqrt_fusion), kind=kOutput, calls=%fused_computation.49 | convolution fusion | flops 3222405120 | bytes 18357248 | tf_op jit(solution)/shard_map/dot_general | solution.py:23
  221.8 10.6 %multiply_convert_fusion = (bf16[256,4096]{1,0:T(8,128)(2,1)S(1)}, bf16[256,4096]{1,0:T(8,128)(2,1)S(1)}) fusion(f32[256,4096]{1,0:T(8,128)S(1)} %fusion.12, f32[256,4096]{1,0:T(8,128)S(1)} %fusion.13, bf16[4096,1536]{1,0:T(8,128)(2,1)} %get-tuple-element.57, bf16[1,256,1536]{2,1,0:T(8,128)(2,1)S(1)} %copy-done.5), kind=kOutput, calls=%fused_computation.10 | convolution fusion | flops 3234856960 | bytes 25952256 | tf_op jit(solution)/shard_map/dot_general | solution.py:23
  232.3 6.5 %fusion.14 = f32[256,1536]{1,0:T(8,128)S(1)} fusion(bf16[256,4096]{1,0:T(8,128)(2,1)S(1)} %get-tuple-element.74, bf16[1536,4096]{1,0:T(8,128)(2,1)} %get-tuple-element.55), kind=kOutput, calls=%fused_computation.50 | convolution fusion | flops 3221225472 | bytes 16252928 | tf_op jit(solution)/shard_map/dot_general | solution.py:23
  238.8 6.8 %multiply_reduce_fusion = (f32[1536]{0:T(1024)S(1)}, f32[256]{0:T(256)S(1)}, f32[256,1536]{1,0:T(8,128)S(1)}) fusion(f32[256,1536]{1,0:T(8,128)S(1)} %get-tuple-element.87, f32[256]{0:T(256)S(1)} %add_rsqrt_fusion, f32[1536]{0:T(1024)S(1)} %slice_reduce_fusion, f32[256,1536]{1,0:T(8,128)S(1)} %fusion.14, bf16[256,4096]{1,0:T(8,128)(2,1)S(1)} %get-tuple-element.73, ...), kind=kOutput, calls=%fused_computation.24 | convolution fusion | flops 3223976192 | bytes 19412992 | tf_op jit(solution)/shard_map/dot_general | solution.py:23
  245.7 1.6 fusion.8
  247.3 2.4 pad_maximum_fusion.rights_in
  249.8 4.6 convolution_convert_fusion.do_ref
  254.6 0.9 copy-done.7
  255.9 2.4 copy.37.lefts_ref
  258.4 5.6 copy.35
  263.9 5.6 copy.36
  269.6 6.0 fusion.hidden_ref
  276.1 314.3 %backward.1 = (f32[256,1536]{1,0:T(8,128)}, f32[8,256]{1,0:T(8,128)}, bf16[6336,512]{1,0:T(8,128)(2,1)}) custom-call(bf16[256,1536]{1,0:T(8,128)(2,1)} %bitcast.99, f32[8,1536]{1,0:T(8,128)} %get-tuple-element.54.gains_ref, f32[256,1536]{1,0:T(8,128)} %get-tuple-element.72.e2_ref, f32[256,384]{1,0:T(8,128)} %copy.44.cos_ref, f32[256,384]{1,0:T(8,128)} %copy.45.first_ref, ...), custom_call_target="tpu_custom_call" | custom-call | tf_op jit(solution)/shard_map/backward/pallas_call | solution.py:919
  590.4 4.3 fusion.9
  595.2 1.8 copy.40
  597.0 2.3 reshape.190
  599.3 1.8 convert_bitcast_fusion
  601.2 1.8 copy.41
  603.0 2.3 reshape.191
  605.3 4.9 copy.51
  610.2 6.1 reshape.192
  616.3 1.3 slice.89
  618.3 1.1 slice_bitcast_fusion.1
  619.4 1.1 slice_bitcast_fusion
  620.5 1.1 slice.93
  622.1 1.7 reshape.189
  623.8 1.3 fusion.11
  625.2 11.7 %fusion.4 = f32[1,256,1536]{2,1,0:T(8,128)} fusion(f32[256,1536]{1,0:T(8,128)S(1)} %copy-done.1, bf16[4096,1536]{1,0:T(8,128)(2,1)} %get-tuple-element.57, f32[256,4096]{1,0:T(8,128)} %copy-done.3, f32[256,4096]{1,0:T(8,128)} %copy-done.2), kind=kOutput, calls=%fused_computation.19 | convolution fusion | flops 3227910144 | bytes 24117248 | tf_op jit(solution)/shard_map/dot_general | solution.py:23
  636.9 1.1 copy.55
  (49 shorter events, 8.0 us)
Async XLA Ops:
  2.2 2.1 copy-start.10
  2.2 2.1 copy-start.11
  4.5 0.6 copy-start.9
  5.1 196.7 %copy-start.4 = (bf16[1,256,1536]{2,1,0:T(8,128)(2,1)S(1)}, bf16[1,256,1536]{2,1,0:T(8,128)(2,1)}, u32[]{:S(2)}) copy-start(bf16[1,256,1536]{2,1,0:T(8,128)(2,1)} %param.15) | copy-start | bytes 2359300
  205.9 48.5 %copy-start = (f32[256,1536]{1,0:T(8,128)}, f32[256,1536]{1,0:T(8,128)S(1)}, u32[]{:S(2)}) copy-start(f32[256,1536]{1,0:T(8,128)S(1)} %get-tuple-element.87) | copy-start | bytes 4718596
  213.4 8.3 %copy-start.2 = (f32[256,4096]{1,0:T(8,128)}, f32[256,4096]{1,0:T(8,128)S(1)}, u32[]{:S(2)}) copy-start(f32[256,4096]{1,0:T(8,128)S(1)} %fusion.12) | copy-start | bytes 12582916
  213.4 8.3 %copy-start.5 = (bf16[1,256,1536]{2,1,0:T(8,128)(2,1)S(1)}, bf16[1,256,1536]{2,1,0:T(8,128)(2,1)}, u32[]{:S(2)}) copy-start(bf16[1,256,1536]{2,1,0:T(8,128)(2,1)} %param.16) | copy-start | bytes 2359300
  221.7 10.6 %copy-start.3 = (f32[256,4096]{1,0:T(8,128)}, f32[256,4096]{1,0:T(8,128)S(1)}, u32[]{:S(2)}) copy-start(f32[256,4096]{1,0:T(8,128)S(1)} %fusion.13) | copy-start | bytes 12582916
  254.4 1.1 copy-start.7
  254.4 1.4 copy-start.8
  621.6 3.6 copy-start.1
  625.2 11.7 %copy-start.6 = (f32[256,1536]{1,0:T(8,128)S(1)}, f32[256,1536]{1,0:T(8,128)}, u32[]{:S(2)}) copy-start(f32[256,1536]{1,0:T(8,128)} %get-tuple-element.66) | copy-start | bytes 4718596

commit v4 on v3

--- a/solution.py
+++ b/solution.py
@@ -965,6 +965,81 @@
     )(x, gains, e2, *tables, hidden_t, eb, lefts, qh, kh, vh, do, lse, gain2, rights, w_q, w_k, w_v)
 
 
+def finish_call(res, dx, d_rows, ff, kvd):
+    tokens, model = dx.shape
+    block = res.shape[1]
+    steps = 4
+    per_d, per_f, per_m = d_rows * 3 // block // steps, ff // COLS // steps, model // COLS
+    at_f = per_d * steps // per_f
+    at_m = per_d * steps + 2 * per_f * steps
+    panel = block // 3
+    assert per_d and per_f and per_d * steps % per_f == 0 and per_m < steps
+
+    def body(d_in, g_in, u_in, o_in, q_in, kv_in, dx_in, down, gate, up, out, query, key, value, dx_out):
+        s = pl.program_id(0)
+        dx_out[...] = dx_in[...]
+        for i in range(per_d):
+            for j in range(3):
+                down[i * panel : (i + 1) * panel, j * COLS : (j + 1) * COLS] = d_in[i, j * panel : (j + 1) * panel, :].astype(F32)
+        for i in range(per_f):
+            gate[:, i * COLS : (i + 1) * COLS] = g_in[i].astype(F32)
+            up[:, i * COLS : (i + 1) * COLS] = u_in[i].astype(F32)
+        for i in range(per_m):
+
+            @pl.when(s == i)
+            def _():
+                out[:, i * COLS : (i + 1) * COLS] = o_in[0].astype(F32)
+                query[:, i * COLS : (i + 1) * COLS] = q_in[0].astype(F32)
+                mid = min(max(kvd - i * COLS, 0), COLS)
+                if mid:
+                    key[:, i * COLS : i * COLS + mid] = kv_in[0, :, :mid].astype(F32)
+                if mid < COLS:
+                    lo = i * COLS + mid - kvd
+                    value[:, lo : lo + COLS - mid] = kv_in[0, :, mid:].astype(F32)
+
+    def chunk(count, at):
+        return pl.BlockSpec((count, block, COLS), at)
+
+    wide = lambda base: chunk(per_f, lambda s: (base + s, 0, 0))
+    thin = lambda base: chunk(1, lambda s: (base + jnp.minimum(s, per_m - 1), 0, 0))
+    whole = lambda width: pl.BlockSpec((block, width), lambda s: (0, 0))
+    return pl.pallas_call(
+        body,
+        grid=(steps,),
+        in_specs=[
+            chunk(per_d, lambda s: (s, 0, 0)),
+            wide(at_f),
+            wide(at_f + steps),
+            thin(at_m),
+            thin(at_m + per_m),
+            thin(at_m + 2 * per_m),
+            pl.BlockSpec((tokens // steps, model), lambda s: (s, 0)),
+        ],
+        out_specs=[
+            pl.BlockSpec((d_rows // steps, model), lambda s: (s, 0)),
+            pl.BlockSpec((block, ff // steps), lambda s: (0, s)),
+            pl.BlockSpec((block, ff // steps), lambda s: (0, s)),
+            whole(model),
+            whole(model),
+            whole(kvd),
+            whole(kvd),
+            pl.BlockSpec((tokens // steps, model), lambda s: (s, 0)),
+        ],
+        out_shape=[
+            jax.ShapeDtypeStruct((d_rows, model), F32),
+            jax.ShapeDtypeStruct((block, ff), F32),
+            jax.ShapeDtypeStruct((block, ff), F32),
+            jax.ShapeDtypeStruct((block, model), F32),
+            jax.ShapeDtypeStruct((block, model), F32),
+            jax.ShapeDtypeStruct((block, kvd), F32),
+            jax.ShapeDtypeStruct((block, kvd), F32),
+            jax.ShapeDtypeStruct((tokens, model), F32),
+        ],
+        compiler_params=pltpu.CompilerParams(vmem_limit_bytes=60 * 1024 * 1024),
+        name="finish",
+    )(*[res] * 6, dx)
+
+
 def attend_back(place, qh, kh, vh, doh, lse):
     chunks = kh.shape[1] // qh.shape[1]
 
@@ -1140,26 +1215,19 @@
             qh, kh, vh, do, lse, term_gain_two[None], rights, w_q, w_k, w_v,
         )
         block = model // dp
-        res = res.reshape(-1, block, COLS)
-        n_down = w_down.shape[1] * 3 // block
-        n_ff, n_model = w_gate.shape[2] // COLS, model // COLS
-
-        def columns(lo, count):
-            return res[lo : lo + count].transpose(1, 0, 2).reshape(block, count * COLS).astype(F32)
-
-        down = res[:n_down].reshape(n_down, 3, block // 3, COLS).transpose(0, 2, 1, 3)
-        at = n_down + 2 * n_ff
-        attn = columns(at + n_model, 2 * n_model)
+        g_down, g_gate, g_up, g_out, g_query, g_key, g_value, dx = finish_call(
+            res.reshape(-1, block, COLS), dx, w_down.shape[1], w_gate.shape[2], kvd
+        )
         return (
             result[None],
             dx[None],
-            attn[None, :, :model],
-            attn[None, :, model : model + kvd],
-            attn[None, :, model + kvd :],
-            columns(at, n_model)[None],
-            columns(n_down, n_ff)[None],
-            columns(n_down + n_ff, n_ff)[None],
-            down.reshape(1, w_down.shape[1], model).astype(F32),
+            g_query[None],
+            g_key[None],
+            g_value[None],
+            g_out[None],
+            g_gate[None],
+            g_up[None],
+            g_down[None],
             grads[0:1, :block],
             grads[1:2, :block],
         )

time: 648 us -> 621 us (0.958)
  local copies, waits for them, and re-layouts: 53.7 us -> 20.6 us
  Pallas kernels: 511 us -> 520 us
    convert_element_type x8 -> x0, local copies, waits for them, and re-layouts: 21.5 us -> none  [the longest x2 11 us: local(): down.reshape(1, w_down.shape[1], model).astype(F32)]
    pallas_call x0 -> x1, Pallas kernels: none -> 9.18 us  [finish_call(): pl.pallas_call(body, grid=(steps,), in_specs=[chunk(per_d, lambda s: (s,...]
    slice x3 -> x0, local copies, waits for them, and re-layouts: 6.77 us -> none  [the longest x1 4.32 us: local(): res[:n_down].reshape(n_down, 3, block // 3, COLS).transpose(0, 2, 1, 3)]
where the time goes in v4:
time: 621 us; the launch traced here: 612 us
  Pallas kernels  520 us (84%)
  matrix products  59.3 us (10%)
  local copies, waits for them, and re-layouts  20.6 us (3%)
  other arithmetic  10.7 us (2%)
    pallas_call x1, Pallas kernels, backward_call(): pl.pallas_call(functools.partial(backward_body, seq), out_shape=[jax.Shap...  314 us
    pallas_call x1, Pallas kernels, forward_call(): pl.pallas_call(functools.partial(forward_body, dp, seq), out_shape=out_sh...  197 us
    dot_general x8, matrix products, dot(): return lax.dot_general(a, b, (dims, ((), ())), preferred_element_type=F32)  59.3 us

profile of v4, /device:TPU:0, one launch (start us, length us, event | category | flops | bytes accessed | tf_op | source)
XLA Modules:
  0.0 611.6 jit_solution(12431318177467059792)
XLA Ops:
  0.7 0.3 multiply_sine_fusion
  1.0 0.1 tile.12
  1.1 0.9 copy.34.cos_ref
  2.1 0.1 tile.14
  2.3 0.9 copy.35.first_ref
  3.2 0.1 tile.31
  3.4 0.9 copy.36.second_ref
  4.3 0.2 scatter.14.gain_ref
  4.5 0.0 copy-start.8
  4.5 0.6 copy-done.8
  5.1 196.7 %forward.1 = (bf16[1536,1536]{1,0:T(8,128)(2,1)}, bf16[1536,768]{1,0:T(8,128)(2,1)}, bf16[1536,768]{1,0:T(8,128)(2,1)}, bf16[1536,1536]{1,0:T(8,128)(2,1)}, bf16...) custom-call(bf16[256,1536]{1,0:T(8,128)(2,1)} %bitcast.73, ...), custom_call_target="tpu_custom_call" | custom-call | tf_op jit(solution)/shard_map/forward/pallas_call | solution.py:388
  201.9 4.1 multiply_reduce_fusion.2
  205.9 0.9 slice_reduce_fusion
  206.8 6.6 %fusion.11 = f32[256,4096]{1,0:T(8,128)S(1)} fusion(bf16[1536,4096]{1,0:T(8,128)(2,1)} %get-tuple-element.63, f32[256,1536]{1,0:T(8,128)S(1)} %get-tuple-element.98, f32[1536]{0:T(1024)S(1)} %slice_reduce_fusion, f32[256]{0:T(256)S(1)} %add_rsqrt_fusion), kind=kOutput, calls=%fused_computation.39 | convolution fusion | flops 3222405120 | bytes 18357248 | tf_op jit(solution)/shard_map/dot_general | solution.py:23
  213.4 8.4 %fusion.12 = f32[256,4096]{1,0:T(8,128)S(1)} fusion(bf16[1536,4096]{1,0:T(8,128)(2,1)} %get-tuple-element.64, f32[256,1536]{1,0:T(8,128)S(1)} %get-tuple-element.98, f32[1536]{0:T(1024)S(1)} %slice_reduce_fusion, f32[256]{0:T(256)S(1)} %add_rsqrt_fusion), kind=kOutput, calls=%fused_computation.40 | convolution fusion | flops 3222405120 | bytes 18357248 | tf_op jit(solution)/shard_map/dot_general | solution.py:23
  221.9 10.6 %multiply_convert_fusion = (bf16[256,4096]{1,0:T(8,128)(2,1)S(1)}, bf16[256,4096]{1,0:T(8,128)(2,1)S(1)}) fusion(f32[256,4096]{1,0:T(8,128)S(1)} %fusion.11, f32[256,4096]{1,0:T(8,128)S(1)} %fusion.12, bf16[4096,1536]{1,0:T(8,128)(2,1)} %get-tuple-element.65, bf16[1,256,1536]{2,1,0:T(8,128)(2,1)S(1)} %copy-done.5), kind=kOutput, calls=%fused_computation.9 | convolution fusion | flops 3234856960 | bytes 25952256 | tf_op jit(solution)/shard_map/dot_general | solution.py:23
  232.5 6.5 %fusion.13 = f32[256,1536]{1,0:T(8,128)S(1)} fusion(bf16[256,4096]{1,0:T(8,128)(2,1)S(1)} %get-tuple-element.90, bf16[1536,4096]{1,0:T(8,128)(2,1)} %get-tuple-element.63), kind=kOutput, calls=%fused_computation.41 | convolution fusion | flops 3221225472 | bytes 16252928 | tf_op jit(solution)/shard_map/dot_general | solution.py:23
  239.0 6.8 %multiply_reduce_fusion = (f32[1536]{0:T(1024)S(1)}, f32[256]{0:T(256)S(1)}, f32[256,1536]{1,0:T(8,128)S(1)}) fusion(f32[256,1536]{1,0:T(8,128)S(1)} %get-tuple-element.98, f32[256]{0:T(256)S(1)} %add_rsqrt_fusion, f32[1536]{0:T(1024)S(1)} %slice_reduce_fusion, f32[256,1536]{1,0:T(8,128)S(1)} %fusion.13, bf16[256,4096]{1,0:T(8,128)(2,1)S(1)} %get-tuple-element.89, ...), kind=kOutput, calls=%fused_computation.20 | convolution fusion | flops 3223976192 | bytes 19412992 | tf_op jit(solution)/shard_map/dot_general | solution.py:23
  245.8 1.6 fusion.8
  247.5 2.4 pad_maximum_fusion.rights_in
  249.9 4.7 convolution_convert_fusion.do_ref
  254.7 0.2 fusion.28
  254.9 0.2 pad_maximum_fusion.1
  255.0 2.4 copy.32.lefts_ref
  257.5 5.6 copy.30
  263.1 5.6 copy.31
  268.7 6.0 fusion.hidden_ref
  274.7 0.6 broadcast_in_dim.37.gain2_ref
  275.3 314.0 %backward.1 = (f32[256,1536]{1,0:T(8,128)}, f32[8,256]{1,0:T(8,128)}, bf16[6336,512]{1,0:T(8,128)(2,1)}) custom-call(bf16[256,1536]{1,0:T(8,128)(2,1)} %bitcast.74, f32[8,1536]{1,0:T(8,128)} %get-tuple-element.62.gains_ref, f32[256,1536]{1,0:T(8,128)} %get-tuple-element.88.e2_ref, f32[256,384]{1,0:T(8,128)} %copy.34.cos_ref, f32[256,384]{1,0:T(8,128)} %copy.35.first_ref, ...), custom_call_target="tpu_custom_call" | custom-call | tf_op jit(solution)/shard_map/backward/pallas_call | solution.py:919
  589.2 9.2 %finish.1 = (f32[512,1536]{1,0:T(8,128)}, f32[192,4096]{1,0:T(8,128)}, f32[192,4096]{1,0:T(8,128)}, f32[192,1536]{1,0:T(8,128)}, f32[192,1536]{1,0:T(8,128)}, /*...) custom-call(bf16[33,192,512]{2,1,0:T(8,128)(2,1)} %bitcast.67, bf16[33,192,512]{2,1,0:T(8,128)(2,1)} %bitcast.68, ...), custom_call_target="tpu_custom_call" | custom-call | tf_op jit(solution)/shard_map/finish/pallas_call | solution.py:1006
  598.4 1.3 fusion.10
  599.8 11.6 %fusion.4 = f32[1,256,1536]{2,1,0:T(8,128)} fusion(f32[256,1536]{1,0:T(8,128)S(1)} %copy-done.1, bf16[4096,1536]{1,0:T(8,128)(2,1)} %get-tuple-element.65, f32[256,4096]{1,0:T(8,128)} %copy-done.3, f32[256,4096]{1,0:T(8,128)} %copy-done.2), kind=kOutput, calls=%fused_computation.16 | convolution fusion | flops 3227910144 | bytes 24117248 | tf_op jit(solution)/shard_map/dot_general | solution.py:23
  (30 shorter events, 0.2 us)
Async XLA Ops:
  2.1 2.2 copy-start.9
  2.1 2.2 copy-start.10
  4.5 0.6 copy-start.8
  5.1 196.7 %copy-start.4 = (bf16[1,256,1536]{2,1,0:T(8,128)(2,1)S(1)}, bf16[1,256,1536]{2,1,0:T(8,128)(2,1)}, u32[]{:S(2)}) copy-start(bf16[1,256,1536]{2,1,0:T(8,128)(2,1)} %param.15) | copy-start | bytes 2359300
  205.9 48.7 %copy-start = (f32[256,1536]{1,0:T(8,128)}, f32[256,1536]{1,0:T(8,128)S(1)}, u32[]{:S(2)}) copy-start(f32[256,1536]{1,0:T(8,128)S(1)} %get-tuple-element.98) | copy-start | bytes 4718596
  213.4 8.5 %copy-start.2 = (f32[256,4096]{1,0:T(8,128)}, f32[256,4096]{1,0:T(8,128)S(1)}, u32[]{:S(2)}) copy-start(f32[256,4096]{1,0:T(8,128)S(1)} %fusion.11) | copy-start | bytes 12582916
  213.4 8.5 %copy-start.5 = (bf16[1,256,1536]{2,1,0:T(8,128)(2,1)S(1)}, bf16[1,256,1536]{2,1,0:T(8,128)(2,1)}, u32[]{:S(2)}) copy-start(bf16[1,256,1536]{2,1,0:T(8,128)(2,1)} %param.16) | copy-start | bytes 2359300
  221.9 10.6 %copy-start.3 = (f32[256,4096]{1,0:T(8,128)}, f32[256,4096]{1,0:T(8,128)S(1)}, u32[]{:S(2)}) copy-start(f32[256,4096]{1,0:T(8,128)S(1)} %fusion.12) | copy-start | bytes 12582916
  249.9 5.0 copy-start.6
  249.9 5.0 copy-start.7
  589.2 10.5 %copy-start.1 = (f32[256,1536]{1,0:T(8,128)S(1)}, f32[256,1536]{1,0:T(8,128)}, u32[]{:S(2)}) copy-start(f32[256,1536]{1,0:T(8,128)} %copy-done) | copy-start | bytes 4718596

commit v5 on v4

--- a/solution.py
+++ b/solution.py
@@ -41,6 +41,7 @@
 
 MESH = pl.DeviceIdType.MESH
 TILE = 4 * HEAD_DIM
+COLS = 512
 
 
 class Gather:
@@ -48,7 +49,7 @@
         self.me, self.bits, self.src, self.out = me, bits, src, out
         self.send, self.recv = send, recv
         self.rows = src.shape[0]
-        self.quarter = -(-self.rows // 64) * 16
+        self.quarter = -(-self.rows // 96) * 16
         self.most = self.rows - self.quarter
         units, parts = self.most // 16, len(bits)
         self.size = [16 * (units // parts + (i < units % parts)) for i in range(parts)]
@@ -146,9 +147,11 @@
 def forward_body(dp, seq, x_ref, gain_ref, cos_ref, first_ref, second_ref, *refs):
     w_in, refs = refs[:7], refs[7:]
     w_out, refs = refs[:7], refs[7:]
-    qh, kh, vh, o_ref, lse_ref, n1_ref, gains_ref = refs[:7]
-    stage, refs = refs[7:14], refs[14:]
-    wq, wk, wv, kvbuf, gbuf, oh, send, recv, kv_send, kv_recv, g_send, g_recv, own_sem, load_sem = refs
+    kept, lse_ref, gains_ref, refs = refs[:9], refs[9], refs[10], refs[11:]
+    made, stage, refs = refs[:9], refs[9:16], refs[16:]
+    qh, kh, vh, lefts, x2_ref, hidden, hidden_t, slope, swish = made
+    (wq, wk, wv, kvbuf, gbuf, oh, n1_ref, n2_ref, o_ref, wt, send, recv, kv_send, kv_recv, g_send, g_recv, own_sem,
+     load_sem, tile_sem, keep_sem) = refs
     me, place = lax.axis_index("dp"), lax.axis_index("seq")
     bits = [1 << i for i in range(1, dp.bit_length() - 1)]
     tokens, model = x_ref.shape
@@ -219,6 +222,15 @@
         gains_ref[:, k * block : (k + 1) * block] = gbuf[k, :, :block]
     n1_ref[...] = (x * scale * gains_ref[0:1, :]).astype(BF)
 
+    def keep(i):
+        return pltpu.make_async_copy(made[i], kept[i], keep_sem.at[i])
+
+    def put_left(which, source):
+        @pl.loop(0, model // TILE)
+        def _(t):
+            at = pl.multiple_of(t * TILE, 128)
+            lefts[pl.ds(pl.multiple_of(which * model + at, 16), TILE), :] = source[:, pl.ds(at, TILE)].T
+
     for job in first:
         job.forward()
     job_o.begin()
@@ -344,15 +356,75 @@
     job_g.share()
     job_u.forward()
     attend_heads(half, HEADS)
+    for i in range(3):
+        keep(i).start()
     for h in range(HEADS):
         o_ref[:, h * HEAD_DIM : (h + 1) * HEAD_DIM] = oh[h]
+
+    job_o.finish()
+    load_o = pltpu.make_async_copy(w_out[3], wq, load_sem.at[0])
+    load_o.start()
+    put_left(2, n1_ref)
+    put_left(1, o_ref)
+    load_o.wait()
+
+    @pl.loop(0, model // TILE)
+    def _(t):
+        at = pl.multiple_of(t * TILE, 128)
+        x2_ref[:, pl.ds(at, TILE)] = x_ref[:, pl.ds(at, TILE)].astype(F32) + nn(o_ref[...], wq[:, pl.ds(at, TILE)])
+
+    x2 = x2_ref[...]
+    n2_ref[...] = (x2 * lax.rsqrt(jnp.mean(x2 * x2, axis=1, keepdims=True) + EPS) * gains_ref[1:2, :]).astype(BF)
+    put_left(0, n2_ref)
+    for i in (3, 4):
+        keep(i).start()
+
+    def project(weight, take):
+        panels = weight.shape[1] // COLS
+
+        def panel(t):
+            at = pl.multiple_of(t * COLS, 128)
+            return pltpu.make_async_copy(weight.at[:, pl.ds(at, COLS)], wt.at[t % 2], tile_sem.at[t % 2])
+
+        panel(0).start()
+
+        @pl.loop(0, panels)
+        def _(t):
+            panel(t).wait()
+
+            @pl.when(t + 1 < panels)
+            def _():
+                panel(t + 1).start()
+
+            take(pl.multiple_of(t * COLS, 128), nn(n2_ref[...], wt[t % 2]))
+
+    def take_gate(at, gate):
+        swish[:, pl.ds(at, COLS)] = gate
+
+    def take_up(at, up):
+        gate = swish[:, pl.ds(at, COLS)]
+        sig = jax.nn.sigmoid(gate)
+        act = gate * sig
+        value = (act * up).astype(BF)
+        hidden[:, pl.ds(at, COLS)] = value
+        hidden_t[pl.ds(at, COLS), :] = value.T
+        slope[:, pl.ds(at, COLS)] = up * sig * (1.0 + gate * (1.0 - sig))
+        swish[:, pl.ds(at, COLS)] = act
+
     job_u.cross()
     job_d.forward()
+    job_g.finish()
+    project(w_out[4], take_gate)
     job_u.share()
+    job_u.finish()
+    project(w_out[5], take_up)
+    for i in range(5, 9):
+        keep(i).start()
     job_d.cross()
     job_d.share()
-    for job in (job_o, job_g, job_u, job_d):
-        job.finish()
+    job_d.finish()
+    for i in range(9):
+        keep(i).wait()
     for r in range(seq - 1):
 
         @pl.when((place >= r) & (place < seq - 1))
@@ -374,23 +446,28 @@
     out_shape = [jax.ShapeDtypeStruct((dp * w.shape[0], w.shape[1]), BF) for w in weights]
     heads = jax.ShapeDtypeStruct((HEADS, tokens, HEAD_DIM), BF)
     keys = jax.ShapeDtypeStruct((KV_HEADS, seq * tokens, HEAD_DIM), BF)
-    out_shape += [
+    kvd, ff = weights[1].shape[1], weights[4].shape[1]
+    made = [
         heads,
         keys,
         keys,
-        jax.ShapeDtypeStruct((tokens, model), BF),
-        jax.ShapeDtypeStruct((tokens, 128), F32),
-        jax.ShapeDtypeStruct((tokens, model), BF),
-        jax.ShapeDtypeStruct((8, model), F32),
+        jax.ShapeDtypeStruct((3 * model, tokens), BF),
+        jax.ShapeDtypeStruct((tokens, model), F32),
+        jax.ShapeDtypeStruct((tokens, ff), BF),
+        jax.ShapeDtypeStruct((ff, tokens), BF),
+        jax.ShapeDtypeStruct((tokens, ff), F32),
+        jax.ShapeDtypeStruct((tokens, ff), F32),
     ]
-    kvd = weights[1].shape[1]
+    out_shape += made + [jax.ShapeDtypeStruct((tokens, 128), F32), jax.ShapeDtypeStruct((8, model), F32)]
+    line = pltpu.VMEM((tokens, model), BF)
     dma = pltpu.SemaphoreType.DMA
     return pl.pallas_call(
         functools.partial(forward_body, dp, seq),
         out_shape=out_shape,
         in_specs=[vmem] * 5 + [anyspec] * 7,
-        out_specs=[anyspec] * 7 + [vmem] * 7,
-        scratch_shapes=[pltpu.VMEM(w.shape, BF) for w in weights]
+        out_specs=[anyspec] * 16 + [vmem] * 2,
+        scratch_shapes=[pltpu.VMEM(a.shape, a.dtype) for a in made]
+        + [pltpu.VMEM(w.shape, BF) for w in weights]
         + [
             pltpu.VMEM((model, model), BF),
             pltpu.VMEM((model, kvd), BF),
@@ -398,6 +475,10 @@
             pltpu.VMEM((seq, tokens, model), BF),
             pltpu.VMEM((dp, 8, 256), F32),
             pltpu.VMEM((HEADS, tokens, HEAD_DIM), BF),
+            line,
+            line,
+            line,
+            pltpu.VMEM((2, model, COLS), BF),
             dma((7, copies)),
             dma((7, copies)),
             dma((seq,)),
@@ -406,6 +487,8 @@
             dma((dp,)),
             dma((7,)),
             dma((3,)),
+            dma((2,)),
+            dma((9,)),
         ],
         compiler_params=pltpu.CompilerParams(
             collective_id=0, has_side_effects=True, vmem_limit_bytes=60 * 1024 * 1024
@@ -419,7 +502,7 @@
     return jnp.sum(jnp.where(lane == h, lse, 0.0), axis=1, keepdims=True)
 
 
-def back_group(place, chunks, g, q_ref, do_ref, lse, k, v, dq_ref, dk_ref, dv_ref, acc_k, acc_v):
+def back_group(place, chunks, g, slot, q_ref, do_ref, lse, k, v, dq_ref, dk_ref, dv_ref, acc_k, acc_v):
     tokens = q_ref.shape[1]
     row = lax.broadcasted_iota(jnp.int32, (tokens, tokens), 0)
     col = lax.broadcasted_iota(jnp.int32, (tokens, tokens), 1)
@@ -446,23 +529,22 @@
                 acc_k[span, :] = dk
                 acc_v[span, :] = dv
             else:
-                dk_ref[g, span, :] = ((acc_k[span, :] + dk) * SCALE).astype(BF)
-                dv_ref[g, span, :] = (acc_v[span, :] + dv).astype(BF)
+                dk_ref[slot, span, :] = ((acc_k[span, :] + dk) * SCALE).astype(BF)
+                dv_ref[slot, span, :] = (acc_v[span, :] + dv).astype(BF)
         dq_ref[h] = (dq * SCALE).astype(BF)
 
 
-COLS = 512
 LAG_B, LAG_C, LAG_D = 1, 3, 5
 SLOTS_CORE, SLOTS, SLOTS_SUM, SLOTS_OUT = 2, 4, 10, 8
 
 
-def backward_body(seq, x_ref, gains_ref, e2_ref, cos_ref, first_ref, second_ref, hidden_ref, eb_ref, lefts_ref,
-                  qh, kh, vh, do_ref, lse_ref, gain2_ref, rights_in, wq_in, wk_in, wv_in, *refs):
-    dx_ref, gain_out, res = refs[:3]
-    (rights, doh, dqh, dkh, dvh, acc_k, acc_v, dkv, dkv_in, dn1, wt,
+def backward_body(seq, x_ref, gains_ref, x2_ref, cos_ref, first_ref, second_ref, hidden_ref, eb_ref, lefts_ref,
+                  qh, kh, vh, lse_ref, wq_in, wk_in, wv_in, wo_in, wg_in, wu_in, wd_in, hid_in, slope_in, swish_in, *refs):
+    dx_ref, gain_out, out_ref, res = refs[:4]
+    (rights, doh, dqh, dkh, dvh, acc_k, acc_v, dkv, dkv_in, dn1, wt, hid, slope, swish, term2,
      cs, cr, sums, r0, r1, zs, zr, zt, gsend, grecv, gsum, gzrecv,
-     load_sem, w_sem, core_s, core_r, s0_s, s0_r, s1_s, s1_r, z_s, z_r, a_s, a_r, t_sem, kv_s, kv_r,
-     g_s, g_r, gz_s, gz_r, core_free, s0_free, s1_free, z_free) = refs[3:]
+     mid_sem, w_sem, core_s, core_r, s0_s, s0_r, s1_s, s1_r, z_s, z_r, a_s, a_r, t_sem, kv_s, kv_r,
+     g_s, g_r, gz_s, gz_r, core_free, s0_free, s1_free, z_free) = refs[4:]
     me, place = lax.axis_index("dp"), lax.axis_index("seq")
     core, chip_x, chip_y = me % 2, (me // 2) % 2, me // 4
     tokens, model = x_ref.shape
@@ -482,8 +564,35 @@
     partner = owner(0, 0, 1)
     near = [[owner(1, 0, 0), owner(0, 1, 0)], [owner(0, 1, 0), owner(1, 0, 0)]]
 
-    load = pltpu.make_async_copy(rights_in, rights.at[:, : rights_in.shape[1]], load_sem)
-    load.start()
+    ff = wg_in.shape[1]
+    part_d = COLS // 2
+
+    def mid_loads(k):
+        s = k % 2
+        at = pl.multiple_of(k * COLS, 128)
+        pairs = [
+            (wd_in.at[pl.ds(at, part_d)], wt.at[s, pl.ds(0, part_d), pl.ds(0, model)]),
+            (wd_in.at[pl.ds(at + part_d, part_d)], wt.at[s, pl.ds(0, part_d), pl.ds(model, model)]),
+            (hid_in.at[:, pl.ds(at, COLS)], hid.at[s]),
+            (slope_in.at[:, pl.ds(at, COLS)], slope.at[s]),
+            (swish_in.at[:, pl.ds(at, COLS)], swish.at[s]),
+        ]
+        return [pltpu.make_async_copy(a, b, mid_sem.at[s, i]) for i, (a, b) in enumerate(pairs)]
+
+    def ff_load(j, i):
+        return pltpu.make_async_copy(
+            (wg_in, wu_in)[i].at[pl.ds(pl.multiple_of(j * TILE, 16), TILE)], wt.at[i, :, pl.ds(0, ff)], w_sem.at[i, 0]
+        )
+
+    def o_load(t):
+        return pltpu.make_async_copy(
+            wo_in.at[pl.ds(t * TILE, TILE)], wt.at[t % 2, :, pl.ds(t // 2 * model, model)], w_sem.at[t % 2, t // 2]
+        )
+
+    for k in range(2):
+        for made in mid_loads(k):
+            made.start()
+    out_ref[...] = x2_ref[...]
 
     barrier = pltpu.get_barrier_semaphore()
     for off in range(1, 8):
@@ -492,10 +601,6 @@
         to = (place + far) % seq
         pl.semaphore_signal(barrier, inc=1, device_id={"seq": to}, device_id_type=MESH)
     pl.semaphore_wait(barrier, 7 + seq - 1)
-
-    for h in range(HEADS):
-        doh[h] = lanes(do_ref, h)
-    load.wait()
 
     def remote(src, dst, send, recv, **target):
         return pltpu.make_async_remote_copy(
@@ -755,21 +860,76 @@
         def _():
             stage_a(c, parity)
 
-    def kv_copy(r):
-        return remote(dkv.at[r], dkv_in.at[r - 1], kv_s.at[r], kv_r.at[r], seq=place - 1)
-
-    def kv_send(r):
+    pair_width = 2 * HEAD_DIM
+
+    def kv_copy(r, i):
+        return remote(dkv.at[r, i], dkv_in.at[r - 1, i], kv_s.at[r, i], kv_r.at[r, i], seq=place - 1)
+
+    def kv_send(r, i):
         @pl.when(place >= r)
         def _():
-            kv_copy(r).start()
-
-    def kv_take(r):
+            kv_copy(r, i).start()
+
+    def kv_take(r, i):
         gets = (place + 1 >= r) & (place + 1 < seq)
 
         @pl.when(gets)
         def _():
-            kv_copy(r).wait_recv()
-            add_rows(tokens, dkv.at[r - 1], dkv_in.at[r - 1])
+            kv_copy(r, i).wait_recv()
+            add_rows(tokens, dkv.at[r - 1, i], dkv_in.at[r - 1, i])
+
+    def mid_down(k):
+        s = k % 2
+        at = pl.multiple_of(k * COLS, 128)
+        for made in mid_loads(k):
+            made.wait()
+        for half in range(2):
+            lo = half * part_d
+            dh = nt(eb_ref[...], wt[s, :part_d, half * model : (half + 1) * model])
+            rights[:, pl.ds(at + lo, part_d)] = (dh * slope[s, :, lo : lo + part_d]).astype(BF)
+            rights[:, pl.ds(ff + at + lo, part_d)] = (dh * swish[s, :, lo : lo + part_d]).astype(BF)
+        for j in range(model // COLS):
+            span = slice(j * COLS, (j + 1) * COLS)
+            out_ref[:, span] += sum(
+                nn(
+                    hid[s, :, half * part_d : (half + 1) * part_d],
+                    wt[s, :part_d, half * model + j * COLS : half * model + (j + 1) * COLS],
+                )
+                for half in range(2)
+            )
+
+        @pl.when(k + 2 < ff // COLS)
+        def _():
+            for made in mid_loads(k + 2):
+                made.start()
+
+    def mid_ff(j):
+        at = pl.multiple_of(j * TILE, 128)
+        for i in range(2):
+            ff_load(j, i).wait()
+        dn1[:, pl.ds(at, TILE)] = nt(rights[:, :ff], wt[0, :, :ff]) + nt(rights[:, ff : 2 * ff], wt[1, :, :ff])
+
+        @pl.when(j + 1 < model // TILE)
+        def _():
+            for i in range(2):
+                ff_load(j + 1, i).start()
+
+    def mid_out():
+        x2 = x2_ref[...]
+        scale = lax.rsqrt(jnp.mean(x2 * x2, axis=1, keepdims=True) + EPS)
+        unit = x2 * scale
+        grad = dn1[...]
+        term2[0:1, :] = jnp.sum(grad * unit, axis=0, keepdims=True)
+        scaled = grad * gains_ref[1:2, :]
+        inner = jnp.mean(scaled * unit, axis=1, keepdims=True)
+        e2 = eb_ref[...].astype(F32) + scale * (scaled - unit * inner)
+        dx_ref[...] = e2
+        rights[:, 2 * ff : 2 * ff + model] = e2.astype(BF)
+        for t in range(model // TILE):
+            o_load(t).wait()
+            do = nt(rights[:, 2 * ff : 2 * ff + model], wt[t % 2, :, t // 2 * model : (t // 2 + 1) * model]).astype(BF)
+            for i in range(TILE // HEAD_DIM):
+                doh[t * (TILE // HEAD_DIM) + i] = do[:, i * HEAD_DIM : (i + 1) * HEAD_DIM]
 
     def turn_back(value):
         ahead = pltpu.roll(value, TILE - HEAD_DIM // 2, 1)
@@ -792,8 +952,11 @@
             rights[:, at : at + TILE] = turn_back(rights[:, at : at + TILE].astype(F32))
         for t in range(kvd // TILE):
             at = q_at + model + t * TILE
-            rights[:, at : at + TILE] = turn_back(dkv[0, :, t * TILE : (t + 1) * TILE].astype(F32))
-        rights[:, q_at + model + kvd :] = dkv[0, :, kvd:]
+            pieces = [dkv[0, 2 * t + i, :, :pair_width] for i in range(2)]
+            rights[:, at : at + TILE] = turn_back(jnp.concatenate(pieces, axis=1).astype(F32))
+        for i in range(KV_HEADS // 2):
+            at = q_at + model + kvd + i * pair_width
+            rights[:, at : at + pair_width] = dkv[0, i, :, pair_width:]
         for i in range(3):
             w_load(0, i).start()
 
@@ -807,7 +970,7 @@
                 for i in range(3):
                     w_load(t + 1, i).start()
 
-            dn1[:, pl.ds(pl.multiple_of(t * TILE, 128), TILE)] = nt(rights[:, q_at:], wt[t % 2])
+            dn1[:, pl.ds(pl.multiple_of(t * TILE, 128), TILE)] = nt(rights[:, q_at:], wt[t % 2, :, : model + 2 * kvd])
 
         x = x_ref[...].astype(F32)
         scale = lax.rsqrt(jnp.mean(x * x, axis=1, keepdims=True) + EPS)
@@ -816,10 +979,10 @@
         term = jnp.sum(grad * unit, axis=0, keepdims=True)
         scaled = grad * gains_ref[0:1, :]
         inner = jnp.mean(scaled * unit, axis=1, keepdims=True)
-        dx_ref[...] = e2_ref[...] + scale * (scaled - unit * inner)
+        dx_ref[...] += scale * (scaled - unit * inner)
         for k in range(8):
             gsend[k, 0:1, :rows] = term[:, k * rows : (k + 1) * rows]
-            gsend[k, 1:2, :rows] = gain2_ref[0:1, k * rows : (k + 1) * rows]
+            gsend[k, 1:2, :rows] = term2[0:1, k * rows : (k + 1) * rows]
 
     def gain_copies():
         return [
@@ -832,41 +995,75 @@
         ]
 
     ticks = total_chunks + last_lag
-    d_pairs = KV_HEADS // 2
+    pairs = KV_HEADS // 2
+    d_steps, f_steps = ff // COLS, model // TILE
+    d_ticks = d_steps // 2
+    out_at = (d_ticks + f_steps) // 2
+    first_at = out_at + 1
+    norm_at = first_at + pairs + seq - 2
+    assert d_ticks <= d_chunks and 2 * norm_at + 1 < total_chunks - 2 * o_panels
 
     @pl.loop(0, -(-ticks // 2))
     def _(p):
         for parity in range(2):
-            tick(2 * p + parity, parity)
-
-        @pl.when(p < d_pairs)
-        def _():
+            c = 2 * p + parity
+            tick(c, parity)
+
+            @pl.when(c < d_ticks)
+            def _():
+                @pl.loop(0, 2)
+                def _(i):
+                    mid_down(2 * c + i)
+
+            @pl.when(c == d_ticks - 1)
+            def _():
+                for i in range(2):
+                    ff_load(0, i).start()
+
+            @pl.when((c >= d_ticks) & (c < d_ticks + f_steps))
+            def _():
+                mid_ff(c - d_ticks)
+
+        @pl.when(p == out_at - 1)
+        def _():
+            for t in range(f_steps):
+                o_load(t).start()
+
+        @pl.when(p == out_at)
+        def _():
+            mid_out()
+
+        for r in range(seq - 1, 0, -1):
+            piece = p - first_at - (seq - r)
+
+            @pl.when((piece >= 0) & (piece < pairs))
+            def _():
+                kv_take(r, piece)
+                if r > 1:
+                    kv_send(r - 1, piece)
+
+        @pl.when((p >= first_at) & (p < first_at + pairs))
+        def _():
+            piece = p - first_at
             for i in range(2):
-                g = 2 * p + i
-                back_group(place, seq, g, qh, doh, lse_ref[...], kh.at[g], vh.at[g], dqh, dkh, dvh, acc_k, acc_v)
-
-        @pl.when(p == d_pairs - 1)
-        def _():
+                g = 2 * piece + i
+                back_group(place, seq, g, i, qh, doh, lse_ref[...], kh.at[g], vh.at[g], dqh, dkh, dvh, acc_k, acc_v)
             for r in range(seq):
-                for g in range(KV_HEADS):
-                    lo = g * HEAD_DIM
-                    dkv[r, :, lo : lo + HEAD_DIM] = dkh[g, r * tokens : (r + 1) * tokens, :]
-                    dkv[r, :, kvd + lo : kvd + lo + HEAD_DIM] = dvh[g, r * tokens : (r + 1) * tokens, :]
-            kv_send(seq - 1)
-
-        for r in range(seq - 1, 0, -1):
-            @pl.when(p == d_pairs - 1 + 2 * (seq - r))
-            def _():
-                kv_take(r)
-                if r > 1:
-                    kv_send(r - 1)
-                else:
-                    last_norm()
-                    for made in gain_copies():
-                        made.start()
-                    grecv[me] = gsend[me]
-
-        @pl.when(p == d_pairs + 2 * seq - 2)
+                for i in range(2):
+                    span = slice(r * tokens, (r + 1) * tokens)
+                    dkv[r, piece, :, i * HEAD_DIM : (i + 1) * HEAD_DIM] = dkh[i, span, :]
+                    lo = pair_width + i * HEAD_DIM
+                    dkv[r, piece, :, lo : lo + HEAD_DIM] = dvh[i, span, :]
+            kv_send(seq - 1, piece)
+
+        @pl.when(p == norm_at)
+        def _():
+            last_norm()
+            for made in gain_copies():
+                made.start()
+            grecv[me] = gsend[me]
+
+        @pl.when(p == norm_at + 1)
         def _():
             for made in gain_copies():
                 made.wait_recv()
@@ -875,7 +1072,7 @@
             for made in gain_line():
                 made.start()
 
-        @pl.when(p == d_pairs + 2 * seq - 1)
+        @pl.when(p == norm_at + 2)
         def _():
             for made in gain_line():
                 made.wait_recv()
@@ -886,7 +1083,8 @@
     for r in range(1, seq):
         @pl.when(place >= r)
         def _():
-            kv_copy(r).wait_send()
+            for i in range(pairs):
+                kv_copy(r, i).wait_send()
     for c in range(total_chunks - SLOTS_CORE, total_chunks):
         core_copy(c).wait_send()
     for way in range(2):
@@ -903,37 +1101,43 @@
         own_copy(c).wait()
 
 
-def backward_call(seq, x, gains, e2, tables, hidden_t, eb, lefts, qh, kh, vh, do, lse, gain2, rights, w_q, w_k, w_v):
+def backward_call(seq, x, gains, x2, tables, hidden_t, eb, lefts, qh, kh, vh, lse, weights, hidden, slope, swish):
     tokens, model = x.shape
     rows = model // 8
     sub = rows // seq
-    kvd = w_k.shape[1]
-    wide = rights.shape[1] + model + 2 * kvd
+    kvd, ff = weights[1].shape[1], hidden.shape[1]
+    wide = 2 * ff + 2 * model + 2 * kvd
     chunks = hidden_t.shape[0] // 8 * 3 // rows + wide // COLS
     anyspec = pl.BlockSpec(memory_space=pl.ANY)
     vmem = pl.BlockSpec(memory_space=pltpu.VMEM)
     dma, regular = pltpu.SemaphoreType.DMA, pltpu.SemaphoreType.REGULAR
     hops = 2 * (seq - 1)
     heads = pltpu.VMEM((HEADS, tokens, HEAD_DIM), BF)
-    keys = pltpu.VMEM((KV_HEADS, seq * tokens, HEAD_DIM), BF)
+    keys = pltpu.VMEM((2, seq * tokens, HEAD_DIM), BF)
+    panel = pltpu.VMEM((2, tokens, COLS), F32)
+    pieces = KV_HEADS // 2
     return pl.pallas_call(
         functools.partial(backward_body, seq),
         out_shape=[
             jax.ShapeDtypeStruct((tokens, model), F32),
             jax.ShapeDtypeStruct((8, 256), F32),
+            jax.ShapeDtypeStruct((tokens, model), F32),
             jax.ShapeDtypeStruct((chunks * rows, COLS), BF),
         ],
-        in_specs=[vmem] * 15 + [anyspec] * 4,
-        out_specs=[vmem, vmem, anyspec],
+        in_specs=[vmem] * 13 + [anyspec] * 10,
+        out_specs=[vmem, vmem, vmem, anyspec],
         scratch_shapes=[
             pltpu.VMEM((tokens, wide), BF),
             heads, heads, keys, keys,
             pltpu.VMEM((seq * tokens, HEAD_DIM), F32),
             pltpu.VMEM((seq * tokens, HEAD_DIM), F32),
-            pltpu.VMEM((seq, tokens, model), BF),
-            pltpu.VMEM((seq - 1, tokens, model), BF),
+            pltpu.VMEM((seq, pieces, tokens, 4 * HEAD_DIM), BF),
+            pltpu.VMEM((seq - 1, pieces, tokens, 4 * HEAD_DIM), BF),
             pltpu.VMEM((tokens, model), F32),
-            pltpu.VMEM((2, TILE, model + 2 * kvd), BF),
+            pltpu.VMEM((2, TILE, max(ff, 2 * model)), BF),
+            pltpu.VMEM((2, tokens, COLS), BF),
+            panel, panel,
+            pltpu.VMEM((8, model), F32),
             pltpu.VMEM((SLOTS_CORE, 4 * rows, COLS), BF),
             pltpu.VMEM((SLOTS_CORE, 4 * rows, COLS), BF),
             pltpu.VMEM((SLOTS_SUM, 4 * rows, COLS), BF),
@@ -946,14 +1150,14 @@
             pltpu.VMEM((8, 8, 256), F32),
             pltpu.VMEM((8, 256), F32),
             pltpu.VMEM((seq, 8, 256), F32),
-            dma(()), dma((2, 3)),
+            dma((2, 5)), dma((2, 3)),
             dma((SLOTS_CORE,)), dma((SLOTS_CORE,)),
             dma((SLOTS,)), dma((SLOTS,)),
             dma((SLOTS,)), dma((SLOTS,)),
             dma((hops, SLOTS)), dma((hops, SLOTS)),
             dma((hops, SLOTS_OUT)), dma((hops, SLOTS_OUT)),
             dma((SLOTS_OUT,)),
-            dma((seq,)), dma((seq,)),
+            dma((seq, pieces)), dma((seq, pieces)),
             dma((8,)), dma((8,)),
             dma((seq,)), dma((seq,)),
             regular, regular((2,)), regular((2,)), regular((hops,)),
@@ -962,10 +1166,10 @@
             collective_id=1, has_side_effects=True, vmem_limit_bytes=62 * 1024 * 1024
         ),
         name="backward",
-    )(x, gains, e2, *tables, hidden_t, eb, lefts, qh, kh, vh, do, lse, gain2, rights, w_q, w_k, w_v)
-
-
-def finish_call(res, dx, d_rows, ff, kvd):
+    )(x, gains, x2, *tables, hidden_t, eb, lefts, qh, kh, vh, lse, *weights, hidden, slope, swish)
+
+
+def finish_call(res, dx, result, d_rows, ff, kvd):
     tokens, model = dx.shape
     block = res.shape[1]
     steps = 4
@@ -975,9 +1179,10 @@
     panel = block // 3
     assert per_d and per_f and per_d * steps % per_f == 0 and per_m < steps
 
-    def body(d_in, g_in, u_in, o_in, q_in, kv_in, dx_in, down, gate, up, out, query, key, value, dx_out):
+    def body(d_in, g_in, u_in, o_in, q_in, kv_in, dx_in, y_in, down, gate, up, out, query, key, value, dx_out, y_out):
         s = pl.program_id(0)
         dx_out[...] = dx_in[...]
+        y_out[...] = y_in[...]
         for i in range(per_d):
             for j in range(3):
                 down[i * panel : (i + 1) * panel, j * COLS : (j + 1) * COLS] = d_in[i, j * panel : (j + 1) * panel, :].astype(F32)
@@ -1002,6 +1207,7 @@
 
     wide = lambda base: chunk(per_f, lambda s: (base + s, 0, 0))
     thin = lambda base: chunk(1, lambda s: (base + jnp.minimum(s, per_m - 1), 0, 0))
+    line = pl.BlockSpec((tokens // steps, model), lambda s: (s, 0))
     whole = lambda width: pl.BlockSpec((block, width), lambda s: (0, 0))
     return pl.pallas_call(
         body,
@@ -1013,7 +1219,8 @@
             thin(at_m),
             thin(at_m + per_m),
             thin(at_m + 2 * per_m),
-            pl.BlockSpec((tokens // steps, model), lambda s: (s, 0)),
+            line,
+            line,
         ],
         out_specs=[
             pl.BlockSpec((d_rows // steps, model), lambda s: (s, 0)),
@@ -1023,7 +1230,8 @@
             whole(model),
             whole(kvd),
             whole(kvd),
-            pl.BlockSpec((tokens // steps, model), lambda s: (s, 0)),
+            line,
+            line,
         ],
         out_shape=[
             jax.ShapeDtypeStruct((d_rows, model), F32),
@@ -1034,10 +1242,11 @@
             jax.ShapeDtypeStruct((block, kvd), F32),
             jax.ShapeDtypeStruct((block, kvd), F32),
             jax.ShapeDtypeStruct((tokens, model), F32),
+            jax.ShapeDtypeStruct((tokens, model), F32),
         ],
         compiler_params=pltpu.CompilerParams(vmem_limit_bytes=60 * 1024 * 1024),
         name="finish",
-    )(*[res] * 6, dx)
+    )(*[res] * 6, dx, result)
 
 
 def attend_back(place, qh, kh, vh, doh, lse):
@@ -1046,7 +1255,7 @@
     def body(place_ref, q_ref, k_ref, v_ref, do_ref, lse_ref, dq_ref, dk_ref, dv_ref, acc_k, acc_v):
         @pl.loop(0, KV_HEADS)
         def _(g):
-            back_group(place_ref[0], chunks, g, q_ref, do_ref, lse_ref[...], k_ref.at[g], v_ref.at[g], dq_ref, dk_ref, dv_ref, acc_k, acc_v)
+            back_group(place_ref[0], chunks, g, g, q_ref, do_ref, lse_ref[...], k_ref.at[g], v_ref.at[g], dq_ref, dk_ref, dv_ref, acc_k, acc_v)
 
     vmem = pl.BlockSpec(memory_space=pltpu.VMEM)
     acc = pltpu.VMEM(kh.shape[1:], F32)
@@ -1185,38 +1394,17 @@
     shards = [w[0] for w in (w_query, w_key, w_value, w_out, w_gate, w_up, w_down)]
     outs = forward_call(dp, seq, tokens[0], packed, [t[:, :TILE] for t in tables], shards)
     w_q, w_k, w_v, w_o, w_g, w_u, w_d = outs[:7]
-    qh, kh, vh, mixed, lse, n1, gains = outs[7:]
+    qh, kh, vh, lefts, x2, hidden, hidden_t, slope, swish, lse, gains = outs[7:]
     gain_one, gain_two = gains[0:1], gains[1:2]
-    scale_one = norm_scale(x)
-    x2 = x + nn(mixed, w_o)
-    scale_two = norm_scale(x2)
-    n2 = (x2 * scale_two * gain_two).astype(BF)
-    gate = nn(n2, w_g)
-    up = nn(n2, w_u)
-    sig = jax.nn.sigmoid(gate)
-    hidden = (gate * sig * up).astype(BF)
-    result = x2 + nn(hidden, w_d)
-
-    e = cotangent[0].astype(F32)
     eb = cotangent[0]
-    dh = nt(eb, w_d)
-    dgate = (dh * up * sig * (1.0 + gate * (1.0 - sig))).astype(BF)
-    dup = (dh * gate * sig).astype(BF)
-    dn2 = nt(dgate, w_g) + nt(dup, w_u)
-    dx2, term_gain_two = norm_back(x2, scale_two, gain_two, dn2)
-    e2 = e + dx2
-    e2b = e2.astype(BF)
-    do = nt(e2b, w_o).astype(BF)
     if len(bits) == 2 and (model // dp) % (16 * seq) == 0:
-        lefts = jnp.concatenate([n2.T, mixed.T, n1.T], axis=0)
-        rights = jnp.concatenate([dgate, dup, e2b], axis=1)
-        dx, grads, res = backward_call(
-            seq, tokens[0], gains, e2, [t[:, :TILE] for t in tables], hidden.T, eb, lefts,
-            qh, kh, vh, do, lse, term_gain_two[None], rights, w_q, w_k, w_v,
+        dx, grads, result, res = backward_call(
+            seq, tokens[0], gains, x2, [t[:, :TILE] for t in tables], hidden_t, eb, lefts,
+            qh, kh, vh, lse, outs[:7], hidden, slope, swish,
         )
         block = model // dp
-        g_down, g_gate, g_up, g_out, g_query, g_key, g_value, dx = finish_call(
-            res.reshape(-1, block, COLS), dx, w_down.shape[1], w_gate.shape[2], kvd
+        g_down, g_gate, g_up, g_out, g_query, g_key, g_value, dx, result = finish_call(
+            res.reshape(-1, block, COLS), dx, result, w_down.shape[1], w_gate.shape[2], kvd
         )
         return (
             result[None],
@@ -1232,6 +1420,19 @@
             grads[1:2, :block],
         )
 
+    scale_one = norm_scale(x)
+    scale_two = norm_scale(x2)
+    result = x2 + nn(hidden, w_d)
+    e = eb.astype(F32)
+    dh = nt(eb, w_d)
+    dgate = (dh * slope).astype(BF)
+    dup = (dh * swish).astype(BF)
+    dn2 = nt(dgate, w_g) + nt(dup, w_u)
+    dx2, term_gain_two = norm_back(x2, scale_two, gain_two, dn2)
+    e2 = e + dx2
+    e2b = e2.astype(BF)
+    do = nt(e2b, w_o).astype(BF)
+    n2, mixed, n1 = (lefts[i * model : (i + 1) * model].T for i in range(3))
     hidden_a = xor_columns(hidden, bits)
     hidden_b = xor_columns(hidden, turned)
     sum_down = jnp.concatenate(

time: 621 us -> 534 us (0.86); the launches traced: 612 us -> 533 us
  matrix products: 59.3 us -> 0 us
  local copies, waits for them, and re-layouts: 20.6 us -> 4.71 us
  other arithmetic: 10.7 us -> 1.65 us
    dot_general x8 -> x0, matrix products: 59.3 us -> none  [dot(): return lax.dot_general(a, b, (dims, ((), ())), preferred_element_type=F32)]
    pallas_call x1, Pallas kernels: 197 us -> 226 us  [forward_call(): pl.pallas_call(functools.partial(forward_body, dp, seq), out_shape=out_sh...]
    pallas_call x1, Pallas kernels: 314 us -> 290 us  [backward_call(): pl.pallas_call(functools.partial(backward_body, seq), out_shape=[jax.Shap...]
    dot_general x2 -> x0, local copies, waits for them, and re-layouts: 11.2 us -> none  [dot(): return lax.dot_general(a, b, (dims, ((), ())), preferred_element_type=F32)]
    convert_element_type x2 -> x0, other arithmetic: 7.63 us -> none  [the longest x1 5.98 us: local(): hidden = (gate * sig * up).astype(BF)]
where the time goes in v5:
time: 534 us; the launch traced here: 533 us
  Pallas kernels  526 us (99%)
    pallas_call x1, Pallas kernels, backward_call(): pl.pallas_call(functools.partial(backward_body, seq), out_shape=[jax.Shap...  290 us
    pallas_call x1, Pallas kernels, forward_call(): pl.pallas_call(functools.partial(forward_body, dp, seq), out_shape=out_sh...  226 us

profile of v5, /device:TPU:0, one launch (start us, length us, event | category | flops | bytes accessed | tf_op | source)
XLA Modules:
  0.0 533.4 jit_solution(6518138300116032332)
XLA Ops:
  0.7 0.7 convert_element_type.20
  1.4 0.7 pad_convert_fusion
  2.0 0.1 scatter.14.gain_ref
  2.1 0.0 copy-start
  2.2 0.3 multiply_sine_fusion
  2.4 0.1 tile.31
  2.6 0.9 copy.27.second_ref
  3.6 0.1 tile.14
  3.7 0.0 copy-done
  3.7 0.9 copy.26.first_ref
  4.7 0.1 tile.12
  4.8 0.9 copy.25.cos_ref
  5.8 226.1 %forward.1 = (bf16[1536,1536]{1,0:T(8,128)(2,1)}, bf16[1536,768]{1,0:T(8,128)(2,1)}, bf16[1536,768]{1,0:T(8,128)(2,1)}, bf16[1536,1536]{1,0:T(8,128)(2,1)}, bf16...) custom-call(bf16[256,1536]{1,0:T(8,128)(2,1)} %bitcast.28, ...), custom_call_target="tpu_custom_call" | custom-call | tf_op jit(solution)/shard_map/forward/pallas_call | solution.py:464
  231.9 290.3 %backward.1 = (f32[256,1536]{1,0:T(8,128)}, f32[8,256]{1,0:T(8,128)}, f32[256,1536]{1,0:T(8,128)}, bf16[6336,512]{1,0:T(8,128)(2,1)}) custom-call(bf16[256,1536]{1,0:T(8,128)(2,1)} %bitcast.29, f32[8,1536]{1,0:T(8,128)} %get-tuple-element.66.gains_ref, f32[256,1536]{1,0:T(8,128)} %get-tuple-element.67.x2_ref, f32[256,384]{1,0:T(8,128)} %copy.25.cos_ref, ...), custom_call_target="tpu_custom_call" | custom-call | tf_op jit(solution)/shard_map/backward/pallas_call | solution.py:1119
  522.2 1.3 fusion.1
  523.5 9.7 %finish.1 = (f32[512,1536]{1,0:T(8,128)}, f32[192,4096]{1,0:T(8,128)}, f32[192,4096]{1,0:T(8,128)}, f32[192,1536]{1,0:T(8,128)}, f32[192,1536]{1,0:T(8,128)}, /*...) custom-call(bf16[33,192,512]{2,1,0:T(8,128)(2,1)} %bitcast.22, ...), custom_call_target="tpu_custom_call" | custom-call | tf_op jit(solution)/shard_map/finish/pallas_call | solution.py:1212
  (6 shorter events, 0.1 us)
Async XLA Ops:
  2.1 1.6 copy-start

commit v6 on v5

--- a/solution.py
+++ b/solution.py
@@ -118,16 +118,19 @@
             self.arrived(self.arrival[(m, i)])
             made.start()
 
-    def cross(self):
-        for m, made in zip(self.masks, self.across):
+    def chosen(self, near):
+        return [i for i, m in enumerate(self.masks) if near is None or (m in self.bits) == near]
+
+    def cross(self, near=None):
+        for at in self.chosen(near):
             for i in range(len(self.bits)):
-                self.arrived(self.arrival[(m, i)])
-            made.start()
-
-    def share(self):
-        for across, made in zip(self.across, self.core):
-            across.wait_recv()
-            made.start()
+                self.arrived(self.arrival[(self.masks[at], i)])
+            self.across[at].start()
+
+    def share(self, near=None):
+        for at in self.chosen(near):
+            self.across[at].wait_recv()
+            self.core[at].start()
 
     def finish(self):
         self.own_core.wait_recv()
@@ -318,13 +321,13 @@
         kv_wait(r)
         if r < seq - 1:
             kv_send_on(r)
-        if r == 1:
+        if r == min(2, seq - 1):
             job_o.cross()
             job_g.forward()
             job_d.begin()
-            job_o.share()
         split_heads(r)
-    job_g.cross()
+    job_o.share()
+    job_g.cross(True)
 
     row = lax.broadcasted_iota(jnp.int32, (tokens, tokens), 0)
     col = lax.broadcasted_iota(jnp.int32, (tokens, tokens), 1)
@@ -353,9 +356,11 @@
             lse_ref[...] += jnp.where(lane == h, top + jnp.log(total), 0.0)
 
     attend_heads(0, half)
-    job_g.share()
     job_u.forward()
+    job_g.share(True)
     attend_heads(half, HEADS)
+    job_g.cross(False)
+    job_u.cross(True)
     for i in range(3):
         keep(i).start()
     for h in range(HEADS):
@@ -379,16 +384,16 @@
     for i in (3, 4):
         keep(i).start()
 
-    def project(weight, take):
-        panels = weight.shape[1] // COLS
+    def project(weight, take, first=0, last=None):
+        panels = weight.shape[1] // COLS if last is None else last
 
         def panel(t):
             at = pl.multiple_of(t * COLS, 128)
             return pltpu.make_async_copy(weight.at[:, pl.ds(at, COLS)], wt.at[t % 2], tile_sem.at[t % 2])
 
-        panel(0).start()
-
-        @pl.loop(0, panels)
+        panel(first).start()
+
+        @pl.loop(first, panels)
         def _(t):
             panel(t).wait()
 
@@ -411,17 +416,23 @@
         slope[:, pl.ds(at, COLS)] = up * sig * (1.0 + gate * (1.0 - sig))
         swish[:, pl.ds(at, COLS)] = act
 
-    job_u.cross()
+    job_g.share(False)
     job_d.forward()
     job_g.finish()
     project(w_out[4], take_gate)
-    job_u.share()
+    job_u.cross(False)
+    job_u.share(True)
+    job_d.cross(True)
+    job_u.share(False)
     job_u.finish()
-    project(w_out[5], take_up)
+    middle = w_out[5].shape[1] // COLS // 2
+    project(w_out[5], take_up, 0, middle)
+    job_d.cross(False)
+    job_d.share(True)
+    project(w_out[5], take_up, middle)
     for i in range(5, 9):
         keep(i).start()
-    job_d.cross()
-    job_d.share()
+    job_d.share(False)
     job_d.finish()
     for i in range(9):
         keep(i).wait()
@@ -534,8 +545,8 @@
         dq_ref[h] = (dq * SCALE).astype(BF)
 
 
-LAG_B, LAG_C, LAG_D = 1, 3, 5
-SLOTS_CORE, SLOTS, SLOTS_SUM, SLOTS_OUT = 2, 4, 10, 8
+LAG_B, LAG_C, LAG_D = 1, 4, 6
+SLOTS_CORE, SLOTS, SLOTS_SUM, SLOTS_OUT = 2, 4, 11, 8
 
 
 def backward_body(seq, x_ref, gains_ref, x2_ref, cos_ref, first_ref, second_ref, hidden_ref, eb_ref, lefts_ref,

time: 534 us -> 506 us (0.948)
  Pallas kernels: 526 us -> 498 us
    pallas_call x1, Pallas kernels: 226 us -> 201 us  [forward_call(): pl.pallas_call(functools.partial(forward_body, dp, seq), out_shape=out_sh...]
where the time goes in v6:
time: 506 us; the launch traced here: 505 us
  Pallas kernels  498 us (98%)
    pallas_call x1, Pallas kernels, backward_call(): pl.pallas_call(functools.partial(backward_body, seq), out_shape=[jax.Shap...  287 us
    pallas_call x1, Pallas kernels, forward_call(): pl.pallas_call(functools.partial(forward_body, dp, seq), out_shape=out_sh...  201 us

profile of v6, /device:TPU:0, one launch (start us, length us, event | category | flops | bytes accessed | tf_op | source)
XLA Modules:
  0.0 505.1 jit_solution(16468966882000486654)
XLA Ops:
  0.7 0.7 convert_element_type.20
  1.4 0.7 pad_convert_fusion
  2.0 0.1 scatter.14.gain_ref
  2.1 0.0 copy-start
  2.2 0.3 multiply_sine_fusion
  2.4 0.1 tile.31
  2.6 0.9 copy.27.second_ref
  3.6 0.1 tile.14
  3.7 0.0 copy-done
  3.7 0.9 copy.26.first_ref
  4.7 0.1 tile.12
  4.8 0.9 copy.25.cos_ref
  5.8 200.9 %forward.1 = (bf16[1536,1536]{1,0:T(8,128)(2,1)}, bf16[1536,768]{1,0:T(8,128)(2,1)}, bf16[1536,768]{1,0:T(8,128)(2,1)}, bf16[1536,1536]{1,0:T(8,128)(2,1)}, bf16...) custom-call(bf16[256,1536]{1,0:T(8,128)(2,1)} %bitcast.28, ...), custom_call_target="tpu_custom_call" | custom-call | tf_op jit(solution)/shard_map/forward/pallas_call | solution.py:475
  206.7 287.2 %backward.1 = (f32[256,1536]{1,0:T(8,128)}, f32[8,256]{1,0:T(8,128)}, f32[256,1536]{1,0:T(8,128)}, bf16[6336,512]{1,0:T(8,128)(2,1)}) custom-call(bf16[256,1536]{1,0:T(8,128)(2,1)} %bitcast.29, f32[8,1536]{1,0:T(8,128)} %get-tuple-element.66.gains_ref, f32[256,1536]{1,0:T(8,128)} %get-tuple-element.67.x2_ref, f32[256,384]{1,0:T(8,128)} %copy.25.cos_ref, ...), custom_call_target="tpu_custom_call" | custom-call | tf_op jit(solution)/shard_map/backward/pallas_call | solution.py:1130
  493.9 1.3 fusion.1
  495.2 9.7 %finish.1 = (f32[512,1536]{1,0:T(8,128)}, f32[192,4096]{1,0:T(8,128)}, f32[192,4096]{1,0:T(8,128)}, f32[192,1536]{1,0:T(8,128)}, f32[192,1536]{1,0:T(8,128)}, /*...) custom-call(bf16[33,192,512]{2,1,0:T(8,128)(2,1)} %bitcast.22, ...), custom_call_target="tpu_custom_call" | custom-call | tf_op jit(solution)/shard_map/finish/pallas_call | solution.py:1223
  (6 shorter events, 0.1 us)
Async XLA Ops:
  2.1 1.6 copy-start

commit v7 on v6

--- a/solution.py
+++ b/solution.py
@@ -1011,7 +1011,7 @@
     d_ticks = d_steps // 2
     out_at = (d_ticks + f_steps) // 2
     first_at = out_at + 1
-    norm_at = first_at + pairs + seq - 2
+    norm_at = first_at + pairs + seq - 1
     assert d_ticks <= d_chunks and 2 * norm_at + 1 < total_chunks - 2 * o_panels
 
     @pl.loop(0, -(-ticks // 2))
@@ -1045,7 +1045,7 @@
             mid_out()
 
         for r in range(seq - 1, 0, -1):
-            piece = p - first_at - (seq - r)
+            piece = p - first_at - (seq - r) - (r < seq - 1)
 
             @pl.when((piece >= 0) & (piece < pairs))
             def _():
@@ -1348,14 +1348,13 @@
 
 def rope_tables(place, tokens, width):
     half = HEAD_DIM // 2
-    positions = (place * tokens + jnp.arange(tokens, dtype=jnp.int32)).astype(F32)
+    lane = lax.broadcasted_iota(jnp.int32, (tokens, width), 1)
+    positions = (place * tokens + lax.broadcasted_iota(jnp.int32, (tokens, width), 0)).astype(F32)
     frequency = ROPE_BASE ** (-jnp.arange(half).astype(F32) / half)
-    angles = positions[:, None] * frequency[None, :]
+    angles = positions * jnp.tile(frequency, width // half)[None, :]
     cos, sin = jnp.cos(angles), jnp.sin(angles)
-    zero = jnp.zeros_like(sin)
-    heads = width // HEAD_DIM
-    tile = lambda a, b: jnp.tile(jnp.concatenate([a, b], axis=1), (1, heads))
-    return tile(cos, cos), tile(sin, zero), tile(zero, sin)
+    low = lane % HEAD_DIM < half
+    return cos, jnp.where(low, sin, 0.0), jnp.where(low, 0.0, sin)
 
 
 def rotate(field, tables, sign):
@@ -1397,20 +1396,20 @@
         cut = lambda off: lax.dynamic_slice_in_dim(value, (me ^ off) * width, width, 1)
         return jnp.concatenate([cut(off) for off in xor_order(way)], axis=1)
 
-    tables = rope_tables(place, rows, model)
+    tables = rope_tables(place, rows, TILE)
     x = tokens[0].astype(F32)
     packed = jnp.zeros((8, 256), F32)
     packed = packed.at[0, : gain_attn.shape[1]].set(gain_attn[0].astype(F32))
     packed = packed.at[1, : gain_mlp.shape[1]].set(gain_mlp[0].astype(F32))
     shards = [w[0] for w in (w_query, w_key, w_value, w_out, w_gate, w_up, w_down)]
-    outs = forward_call(dp, seq, tokens[0], packed, [t[:, :TILE] for t in tables], shards)
+    outs = forward_call(dp, seq, tokens[0], packed, tables, shards)
     w_q, w_k, w_v, w_o, w_g, w_u, w_d = outs[:7]
     qh, kh, vh, lefts, x2, hidden, hidden_t, slope, swish, lse, gains = outs[7:]
     gain_one, gain_two = gains[0:1], gains[1:2]
     eb = cotangent[0]
     if len(bits) == 2 and (model // dp) % (16 * seq) == 0:
         dx, grads, result, res = backward_call(
-            seq, tokens[0], gains, x2, [t[:, :TILE] for t in tables], hidden_t, eb, lefts,
+            seq, tokens[0], gains, x2, tables, hidden_t, eb, lefts,
             qh, kh, vh, lse, outs[:7], hidden, slope, swish,
         )
         block = model // dp
@@ -1431,6 +1430,7 @@
             grads[1:2, :block],
         )
 
+    tables = [jnp.tile(t, (1, model // TILE)) for t in tables]
     scale_one = norm_scale(x)
     scale_two = norm_scale(x2)
     result = x2 + nn(hidden, w_d)

time: 506 us -> 501 us (level)
  no operation moved by 1% of the time
where the time goes in v7:
time: 501 us; the launch traced here: 500 us
  Pallas kernels  494 us (99%)
    pallas_call x1, Pallas kernels, backward_call(): pl.pallas_call(functools.partial(backward_body, seq), out_shape=[jax.Shap...  283 us
    pallas_call x1, Pallas kernels, forward_call(): pl.pallas_call(functools.partial(forward_body, dp, seq), out_shape=out_sh...  201 us

profile of v7, /device:TPU:0, one launch (start us, length us, event | category | flops | bytes accessed | tf_op | source)
XLA Modules:
  0.0 499.9 jit_solution(7468318712002153492)
XLA Ops:
  0.7 0.7 convert_element_type.17
  1.4 0.1 mul.14
  1.5 0.7 pad_convert_fusion
  2.1 0.1 scatter.14.gain_ref
  2.3 0.0 copy-start
  2.3 2.4 fusion
  4.6 0.0 copy-done
  4.7 200.9 %forward.1 = (bf16[1536,1536]{1,0:T(8,128)(2,1)}, bf16[1536,768]{1,0:T(8,128)(2,1)}, bf16[1536,768]{1,0:T(8,128)(2,1)}, bf16[1536,1536]{1,0:T(8,128)(2,1)}, bf16...) custom-call(bf16[256,1536]{1,0:T(8,128)(2,1)} %bitcast.25, ...), custom_call_target="tpu_custom_call" | custom-call | tf_op jit(solution)/shard_map/forward/pallas_call | solution.py:475
  205.6 283.1 %backward.1 = (f32[256,1536]{1,0:T(8,128)}, f32[8,256]{1,0:T(8,128)}, f32[256,1536]{1,0:T(8,128)}, bf16[6336,512]{1,0:T(8,128)(2,1)}) custom-call(bf16[256,1536]{1,0:T(8,128)(2,1)} %bitcast.26, f32[8,1536]{1,0:T(8,128)} %get-tuple-element.66.gains_ref, f32[256,1536]{1,0:T(8,128)} %get-tuple-element.67.x2_ref, f32[256,384]{1,0:T(8,128)} %get-tuple-element.101.cos_ref, ...), custom_call_target="tpu_custom_call" | custom-call | tf_op jit(solution)/shard_map/backward/pallas_call | solution.py:1130
  488.7 1.3 fusion.6
  490.0 9.7 %finish.1 = (f32[512,1536]{1,0:T(8,128)}, f32[192,4096]{1,0:T(8,128)}, f32[192,4096]{1,0:T(8,128)}, f32[192,1536]{1,0:T(8,128)}, f32[192,1536]{1,0:T(8,128)}, /*...) custom-call(bf16[33,192,512]{2,1,0:T(8,128)(2,1)} %bitcast.19, ...), custom_call_target="tpu_custom_call" | custom-call | tf_op jit(solution)/shard_map/finish/pallas_call | solution.py:1223
  (5 shorter events, 0.0 us)
Async XLA Ops:
  2.3 2.4 copy-start
